TPU v7x, 512 devices: a whole 4x4x16 slice. The times are simulated.
512 devices in a mesh: gx: 16 (over z_hi, y), gy: 8 (over z_lo, core), gz: 4 (over x).
Axes of the slice: x: 4, y: 4, z: 16 (z_hi: 4, z_lo: 4; z = z_hi * 4 + z_lo), core: 2. Of those that a mesh axis runs over, the one named last changes fastest.
Arguments:
- traces: bfloat16 [8192, 32], P('gx'), may hold values from -6 to 6
- receiver_cell: int32 [8192], P('gx'), may hold values from 0 to 32767
- weight_class: int32 [8192], P('gx'), may hold values from 0 to 15
- weight_table: float32 [16], replicated, may hold values from 0.5 to 2
- obstacle_top: int32 [32, 256], P('gx', 'gy'), may hold values from 128 to 255
- obstacle_thick: int32 [32, 256], P('gx', 'gy'), may hold values from 0 to 128
- courant: float32 [64, 512, 512], P('gx', 'gy', 'gz'), may hold values from 0.06 to 0.25
- p_now: float32 [64, 512, 512], P('gx', 'gy', 'gz'), may hold values from -6 to 6
- p_prev: float32 [64, 512, 512], P('gx', 'gy', 'gz'), may hold values from -6 to 6
Outputs:
- wavefield: float32 [64, 512, 512], P('gx', 'gy', 'gz')
All inputs are finite; a program needn't handle non-finite values.
Results may differ from a plain program's by a relative error of at most 0.0003.
Values may be sent and summed in bfloat16 or wider, within the bound.
No kernel may reach another device: no remote copies, remote signals or barrier semaphores. Data moves between devices by JAX's collectives and lax.ppermute only.
A program may use at most 64 MiB of HBM per device.

v0:
```python
import jax
import jax.numpy as jnp
from jax import lax
from jax.sharding import PartitionSpec as P


def in_blocks(array, dim, count):
    dims = array.shape
    parts = array.reshape(*dims[:dim], count, dims[dim] // count, *dims[dim + 1 :])
    return jnp.moveaxis(parts, dim, 0)


def summed_on_arrival(array, axis, dim):
    count = lax.axis_size(axis)
    parts = lax.all_to_all(in_blocks(array, dim, count), axis, 0, 0, tiled=True)
    return jnp.sum(parts, axis=0)


def with_halo(cells, sides, width):
    for axis, dim in sides:
        count = lax.axis_size(axis)
        ends = count - 1
        head = lax.slice_in_dim(cells, 0, width, axis=dim)
        tail = lax.slice_in_dim(cells, cells.shape[dim] - width, cells.shape[dim], axis=dim)
        cells = jnp.concatenate(
            [
                lax.ppermute(tail, axis, [(i, (i + 1) % count) for i in range(ends)]),
                cells,
                lax.ppermute(head, axis, [((i + 1) % count, i) for i in range(ends)]),
            ],
            axis=dim,
        )
    return cells


def receiver_terms(trace_rows, class_rows, weight_table):
    one_hot = (
        class_rows[:, None] == jnp.arange(weight_table.shape[0], dtype=jnp.int32)[None, :]
    ).astype(jnp.float32)
    weights = jnp.sum(one_hot * weight_table[None, :], axis=1)
    return weights[:, None] * trace_rows.astype(jnp.float32)


def advance(wavefield, before, speeds, living, source_plane, depth_select):
    centre = wavefield[1:-1, 1:-1, 1:-1]
    beside_all = wavefield[2:, 1:-1, 1:-1] + wavefield[:-2, 1:-1, 1:-1]
    beside_all = beside_all + wavefield[1:-1, 2:, 1:-1] + wavefield[1:-1, :-2, 1:-1]
    beside_all = beside_all + wavefield[1:-1, 1:-1, 2:] + wavefield[1:-1, 1:-1, :-2]
    laplace = beside_all - 6.0 * centre
    updated = 2.0 * centre - before + speeds * laplace + source_plane[:, :, None] * depth_select
    return living * updated


def local(
    traces,
    receiver_cell,
    weight_class,
    weight_table,
    obstacle_top,
    obstacle_thick,
    courant,
    p_now,
    p_prev,
):
    tile_x, tile_y, tile_z = courant.shape
    step_count = traces.shape[1]
    grid_y = tile_y * lax.axis_size("gy")
    anchor_y = lax.axis_index("gy") * tile_y
    anchor_z = lax.axis_index("gz") * tile_z
    roof = jnp.repeat(jnp.repeat(obstacle_top, 2, axis=0), 2, axis=1)[:, :, None]
    thickness = jnp.repeat(jnp.repeat(obstacle_thick, 2, axis=0), 2, axis=1)[:, :, None]
    depth_cells = anchor_z + jnp.arange(tile_z, dtype=jnp.int32)[None, None, :]
    solid = (depth_cells >= roof) & (depth_cells < roof + thickness)
    living = jnp.where(solid, 0.0, 1.0).astype(jnp.float32)
    contrib = receiver_terms(traces, weight_class, weight_table)
    cell_x = receiver_cell // grid_y
    cell_y = receiver_cell % grid_y
    first_row = jnp.int32(0)
    row_count = tile_x * lax.axis_size("gx")
    inside = (
        (cell_x >= first_row)
        & (cell_x < first_row + row_count)
        & (cell_y >= anchor_y)
        & (cell_y < anchor_y + tile_y)
    )
    segment = jnp.where(inside, cell_x * tile_y + cell_y - anchor_y, row_count * tile_y)
    summed = jax.ops.segment_sum(contrib, segment, num_segments=row_count * tile_y + 1)
    flat_sources = summed_on_arrival(summed[:-1].reshape(row_count, tile_y * step_count), "gx", 0)
    sources = flat_sources.reshape(tile_x, tile_y, step_count)
    surface_flag = (anchor_z == 0).astype(jnp.float32)
    sources = sources * surface_flag
    depth_first = (jnp.arange(tile_z, dtype=jnp.int32) == 0).astype(jnp.float32)
    statics = with_halo(jnp.stack([courant, living]), (("gx", 1), ("gy", 2), ("gz", 3)), 2)
    source_ext = with_halo(sources, (("gx", 0), ("gy", 1)), 2)
    speeds_mid = statics[0, 1:-1, 1:-1, 1:-1]
    living_mid = statics[1, 1:-1, 1:-1, 1:-1]
    depth_second = (jnp.arange(tile_z + 2, dtype=jnp.int32) == 1).astype(jnp.float32)

    def double_step(counter, carried):
        current, previous = carried
        stacked = with_halo(jnp.stack([current, previous]), (("gx", 1), ("gy", 2), ("gz", 3)), 2)
        present = stacked[0]
        earlier = stacked[1]
        first_step = 2 * counter
        plane_one = lax.dynamic_index_in_dim(
            source_ext, step_count - 1 - first_step, 2, keepdims=False
        )[1:-1, 1:-1]
        halfway = advance(
            present, earlier[1:-1, 1:-1, 1:-1], speeds_mid, living_mid, plane_one, depth_second
        )
        plane_two = lax.dynamic_index_in_dim(
            source_ext, step_count - 2 - first_step, 2, keepdims=False
        )[2:-2, 2:-2]
        updated = advance(
            halfway, present[2:-2, 2:-2, 2:-2], courant, living, plane_two, depth_first
        )
        return (updated, halfway[1:-1, 1:-1, 1:-1])

    current, previous = lax.fori_loop(0, step_count // 2, double_step, (p_now, p_prev))
    return current


def solution(mesh):
    placed = (
        P("gx", None),
        P("gx"),
        P("gx"),
        P(),
        P("gx", "gy"),
        P("gx", "gy"),
        P("gx", "gy", "gz"),
        P("gx", "gy", "gz"),
        P("gx", "gy", "gz"),
    )
    return jax.shard_map(
        local, mesh=mesh, in_specs=placed, out_specs=P("gx", "gy", "gz"), check_vma=False
    )
```

profile of v0, /device:TPU:486, one launch (start us, length us, event | category | flops | bytes accessed | tf_op | source)
XLA Modules:
  0.0 743.6 jit_solution(11914912746914599342)
XLA Ops:
  2.4 4.3 scatter_custom_fusion
  11.3 12.9 %all-to-all-start = ((f32[16,4,2048]{2,1,0:T(4,128)}), f32[16,4,2048]{2,1,0:T(4,128)S(1)}, u32[]{:S(2)}, u32[]{:S(2)}) async-start(f32[16,4,2048]{2,1,0:T(4,128)} %reshape_reshape.3), calls=%async_computation | async-start | bytes 1048576 | tf_op jit(solution)/shard_map/all_to_all | solution.py:15
  28.2 8.5 %collective-permute-start.7 = (f32[2,2,64,128]{3,1,2,0:T(2,128)S(1)}, f32[2,2,64,128]{3,1,2,0:T(2,128)S(1)}, u32[]{:S(2)}, u32[]{:S(2)}) collective-permute-start(f32[2,2,64,128]{3,1,2,0:T(2,128)S(1)} %get-tuple-element.357), channel_id=1, source_target_pairs={{32,0},{64,32},{96,64},{128,96},{160,128},{192,160},{224,192},{256... | collective-permute-start | bytes 393224 | tf_op jit(solution)/shard_map/ppermute | solution.py:29
  36.7 28.8 %collective-permute-done.6 = f32[2,2,64,128]{3,1,2,0:T(2,128)S(1)} collective-permute-done((f32[2,2,64,128]{3,1,2,0:T(2,128)S(1)}, f32[2,2,64,128]{3,1,2,0:T(2,128)S(1)}, u32[]{:S(2)}, u32[]{:S(2)}) %collective-permute-start.6) | collective-permute-done | bytes 131104 | tf_op jit(solution)/shard_map/ppermute | solution.py:27
  74.8 4.5 collective-permute-start.11
  84.5 9.9 %collective-permute-start.13 = (f32[2,64,32]{2,1,0:T(8,128)S(1)}, f32[2,64,32]{2,1,0:T(8,128)S(1)}, u32[]{:S(2)}, u32[]{:S(2)}) collective-permute-start(f32[2,64,32]{2,1,0:T(8,128)S(1)} %slice.317), channel_id=1, source_target_pairs={{32,0},{64,32},{96,64},{128,96},{160,128},{192,160},{224,192},{256... | collective-permute-start | bytes 49160 | tf_op jit(solution)/shard_map/ppermute | solution.py:29
  105.1 637.9 %while.18 = (s32[]{:T(128)}, f32[4,64,128]{2,0,1:T(4,128)S(1)}, f32[4,64,128]{2,0,1:T(4,128)S(1)}, f32[6,66,130]{2,0,1:T(8,128)S(1)}, f32[8,68,32]{0,1,2:T(8,128...) while((s32[]{:T(128)}, f32[4,64,128]{2,0,1:T(4,128)S(1)}, ...), condition=%wide.region_4.5_spmd.clone, body=%wide.region_3.4_spmd.clone.sunk | while | flops 3102815 | bytes 9575613 | solution.py:119
  105.2 10.3 %collective-permute-start = (f32[2,2,64,128]{3,1,2,0:T(2,128)S(1)}, f32[2,2,64,128]{3,1,2,0:T(2,128)S(1)}, u32[]{:S(2)}, u32[]{:S(2)}) collective-permute-start(f32[2,2,64,128]{3,1,2,0:T(2,128)S(1)} %get-tuple-element.435), channel_id=1, source_target_pairs={{32,0},{64,32},{96,64},{128,96},{160,128},{192,160},{224,192},{256... | collective-permute-start | bytes 393224 | tf_op jit(solution)/shard_map/while/body/eval_jaxpr/ppermute | solution.py:29
  118.2 17.0 %collective-permute-done.1 = f32[2,2,64,128]{3,1,2,0:T(2,128)S(1)} collective-permute-done((f32[2,2,64,128]{3,1,2,0:T(2,128)S(1)}, f32[2,2,64,128]{3,1,2,0:T(2,128)S(1)}, u32[]{:S(2)}, u32[]{:S(2)}) %collective-permute-start.1) | collective-permute-done | bytes 131104 | tf_op jit(solution)/shard_map/while/body/eval_jaxpr/ppermute | solution.py:27
  142.8 4.2 collective-permute-start.4
  149.1 3.8 collective-permute-done.5
  158.3 3.9 collective-permute-start.1
  163.3 11.6 %collective-permute-done.1 = f32[2,2,64,128]{3,1,2,0:T(2,128)S(1)} collective-permute-done((f32[2,2,64,128]{3,1,2,0:T(2,128)S(1)}, f32[2,2,64,128]{3,1,2,0:T(2,128)S(1)}, u32[]{:S(2)}, u32[]{:S(2)}) %collective-permute-start.1) | collective-permute-done | bytes 131104 | tf_op jit(solution)/shard_map/while/body/eval_jaxpr/ppermute | solution.py:27
  187.4 3.8 collective-permute-done.5
  196.6 3.9 collective-permute-start.1
  201.5 9.8 %collective-permute-done.1 = f32[2,2,64,128]{3,1,2,0:T(2,128)S(1)} collective-permute-done((f32[2,2,64,128]{3,1,2,0:T(2,128)S(1)}, f32[2,2,64,128]{3,1,2,0:T(2,128)S(1)}, u32[]{:S(2)}, u32[]{:S(2)}) %collective-permute-start.1) | collective-permute-done | bytes 131104 | tf_op jit(solution)/shard_map/while/body/eval_jaxpr/ppermute | solution.py:27
  223.5 3.8 collective-permute-done.5
  232.8 3.9 collective-permute-start.1
  237.7 7.9 %collective-permute-done.1 = f32[2,2,64,128]{3,1,2,0:T(2,128)S(1)} collective-permute-done((f32[2,2,64,128]{3,1,2,0:T(2,128)S(1)}, f32[2,2,64,128]{3,1,2,0:T(2,128)S(1)}, u32[]{:S(2)}, u32[]{:S(2)}) %collective-permute-start.1) | collective-permute-done | bytes 131104 | tf_op jit(solution)/shard_map/while/body/eval_jaxpr/ppermute | solution.py:27
  250.0 11.9 %collective-permute-done.3 = f32[2,8,2,128]{3,1,2,0:T(8,128)S(1)} collective-permute-done((f32[2,8,2,128]{3,1,2,0:T(8,128)S(1)}, f32[2,8,2,128]{3,1,2,0:T(8,128)S(1)}, u32[]{:S(2)}, u32[]{:S(2)}) %collective-permute-start.3) | collective-permute-done | bytes 16416 | tf_op jit(solution)/shard_map/while/body/eval_jaxpr/ppermute | solution.py:27
  266.8 3.8 collective-permute-done.5
  276.0 3.9 collective-permute-start.1
  281.0 13.4 %collective-permute-done.1 = f32[2,2,64,128]{3,1,2,0:T(2,128)S(1)} collective-permute-done((f32[2,2,64,128]{3,1,2,0:T(2,128)S(1)}, f32[2,2,64,128]{3,1,2,0:T(2,128)S(1)}, u32[]{:S(2)}, u32[]{:S(2)}) %collective-permute-start.1) | collective-permute-done | bytes 131104 | tf_op jit(solution)/shard_map/while/body/eval_jaxpr/ppermute | solution.py:27
  306.4 3.8 collective-permute-done.5
  315.7 3.9 collective-permute-start.1
  320.6 12.3 %collective-permute-done.1 = f32[2,2,64,128]{3,1,2,0:T(2,128)S(1)} collective-permute-done((f32[2,2,64,128]{3,1,2,0:T(2,128)S(1)}, f32[2,2,64,128]{3,1,2,0:T(2,128)S(1)}, u32[]{:S(2)}, u32[]{:S(2)}) %collective-permute-start.1) | collective-permute-done | bytes 131104 | tf_op jit(solution)/shard_map/while/body/eval_jaxpr/ppermute | solution.py:27
  354.0 3.9 collective-permute-start.1
  358.9 10.5 %collective-permute-done.1 = f32[2,2,64,128]{3,1,2,0:T(2,128)S(1)} collective-permute-done((f32[2,2,64,128]{3,1,2,0:T(2,128)S(1)}, f32[2,2,64,128]{3,1,2,0:T(2,128)S(1)}, u32[]{:S(2)}, u32[]{:S(2)}) %collective-permute-start.1) | collective-permute-done | bytes 131104 | tf_op jit(solution)/shard_map/while/body/eval_jaxpr/ppermute | solution.py:27
  390.6 3.9 collective-permute-start.1
  395.5 11.2 %collective-permute-done.1 = f32[2,2,64,128]{3,1,2,0:T(2,128)S(1)} collective-permute-done((f32[2,2,64,128]{3,1,2,0:T(2,128)S(1)}, f32[2,2,64,128]{3,1,2,0:T(2,128)S(1)}, u32[]{:S(2)}, u32[]{:S(2)}) %collective-permute-start.1) | collective-permute-done | bytes 131104 | tf_op jit(solution)/shard_map/while/body/eval_jaxpr/ppermute | solution.py:27
  428.2 3.9 collective-permute-start.1
  433.1 8.0 %collective-permute-done.1 = f32[2,2,64,128]{3,1,2,0:T(2,128)S(1)} collective-permute-done((f32[2,2,64,128]{3,1,2,0:T(2,128)S(1)}, f32[2,2,64,128]{3,1,2,0:T(2,128)S(1)}, u32[]{:S(2)}, u32[]{:S(2)}) %collective-permute-start.1) | collective-permute-done | bytes 131104 | tf_op jit(solution)/shard_map/while/body/eval_jaxpr/ppermute | solution.py:27
  445.5 7.8 %collective-permute-done.3 = f32[2,8,2,128]{3,1,2,0:T(8,128)S(1)} collective-permute-done((f32[2,8,2,128]{3,1,2,0:T(8,128)S(1)}, f32[2,8,2,128]{3,1,2,0:T(8,128)S(1)}, u32[]{:S(2)}, u32[]{:S(2)}) %collective-permute-start.3) | collective-permute-done | bytes 16416 | tf_op jit(solution)/shard_map/while/body/eval_jaxpr/ppermute | solution.py:27
  453.9 3.9 collective-permute-start.4
  469.2 3.9 collective-permute-start.1
  474.1 15.1 %collective-permute-done.1 = f32[2,2,64,128]{3,1,2,0:T(2,128)S(1)} collective-permute-done((f32[2,2,64,128]{3,1,2,0:T(2,128)S(1)}, f32[2,2,64,128]{3,1,2,0:T(2,128)S(1)}, u32[]{:S(2)}, u32[]{:S(2)}) %collective-permute-start.1) | collective-permute-done | bytes 131104 | tf_op jit(solution)/shard_map/while/body/eval_jaxpr/ppermute | solution.py:27
  510.4 3.9 collective-permute-start.1
  515.3 13.7 %collective-permute-done.1 = f32[2,2,64,128]{3,1,2,0:T(2,128)S(1)} collective-permute-done((f32[2,2,64,128]{3,1,2,0:T(2,128)S(1)}, f32[2,2,64,128]{3,1,2,0:T(2,128)S(1)}, u32[]{:S(2)}, u32[]{:S(2)}) %collective-permute-start.1) | collective-permute-done | bytes 131104 | tf_op jit(solution)/shard_map/while/body/eval_jaxpr/ppermute | solution.py:27
  550.2 3.9 collective-permute-start.1
  555.2 12.9 %collective-permute-done.1 = f32[2,2,64,128]{3,1,2,0:T(2,128)S(1)} collective-permute-done((f32[2,2,64,128]{3,1,2,0:T(2,128)S(1)}, f32[2,2,64,128]{3,1,2,0:T(2,128)S(1)}, u32[]{:S(2)}, u32[]{:S(2)}) %collective-permute-start.1) | collective-permute-done | bytes 131104 | tf_op jit(solution)/shard_map/while/body/eval_jaxpr/ppermute | solution.py:27
  589.2 3.9 collective-permute-start.1
  594.1 11.9 %collective-permute-done.1 = f32[2,2,64,128]{3,1,2,0:T(2,128)S(1)} collective-permute-done((f32[2,2,64,128]{3,1,2,0:T(2,128)S(1)}, f32[2,2,64,128]{3,1,2,0:T(2,128)S(1)}, u32[]{:S(2)}, u32[]{:S(2)}) %collective-permute-start.1) | collective-permute-done | bytes 131104 | tf_op jit(solution)/shard_map/while/body/eval_jaxpr/ppermute | solution.py:27
  627.3 3.9 collective-permute-start.1
  632.2 13.7 %collective-permute-done.1 = f32[2,2,64,128]{3,1,2,0:T(2,128)S(1)} collective-permute-done((f32[2,2,64,128]{3,1,2,0:T(2,128)S(1)}, f32[2,2,64,128]{3,1,2,0:T(2,128)S(1)}, u32[]{:S(2)}, u32[]{:S(2)}) %collective-permute-start.1) | collective-permute-done | bytes 131104 | tf_op jit(solution)/shard_map/while/body/eval_jaxpr/ppermute | solution.py:27
  667.0 3.9 collective-permute-start.1
  671.9 13.7 %collective-permute-done.1 = f32[2,2,64,128]{3,1,2,0:T(2,128)S(1)} collective-permute-done((f32[2,2,64,128]{3,1,2,0:T(2,128)S(1)}, f32[2,2,64,128]{3,1,2,0:T(2,128)S(1)}, u32[]{:S(2)}, u32[]{:S(2)}) %collective-permute-start.1) | collective-permute-done | bytes 131104 | tf_op jit(solution)/shard_map/while/body/eval_jaxpr/ppermute | solution.py:27
  706.8 3.9 collective-permute-start.1
  711.7 12.6 %collective-permute-done.1 = f32[2,2,64,128]{3,1,2,0:T(2,128)S(1)} collective-permute-done((f32[2,2,64,128]{3,1,2,0:T(2,128)S(1)}, f32[2,2,64,128]{3,1,2,0:T(2,128)S(1)}, u32[]{:S(2)}, u32[]{:S(2)}) %collective-permute-start.1) | collective-permute-done | bytes 131104 | tf_op jit(solution)/shard_map/while/body/eval_jaxpr/ppermute | solution.py:27
  (494 shorter events, 360.5 us)
Async XLA Ops:
  11.3 69.8 %all-to-all-start = ((f32[16,4,2048]{2,1,0:T(4,128)}), f32[16,4,2048]{2,1,0:T(4,128)S(1)}, u32[]{:S(2)}, u32[]{:S(2)}) async-start(f32[16,4,2048]{2,1,0:T(4,128)} %reshape_reshape.3), calls=%async_computation | async-start | bytes 1048576 | tf_op jit(solution)/shard_map/all_to_all | solution.py:15
  24.9 40.7 %collective-permute-start.6 = (f32[2,2,64,128]{3,1,2,0:T(2,128)S(1)}, f32[2,2,64,128]{3,1,2,0:T(2,128)S(1)}, u32[]{:S(2)}, u32[]{:S(2)}) collective-permute-start(f32[2,2,64,128]{3,1,2,0:T(2,128)S(1)} %get-tuple-element.356), channel_id=1, source_target_pairs={{0,32},{32,64},{64,96},{96,128},{128,160},{160,192},{192,224},{224... | collective-permute-start | bytes 393224 | tf_op jit(solution)/shard_map/ppermute | solution.py:27
  28.2 37.3 %collective-permute-start.7 = (f32[2,2,64,128]{3,1,2,0:T(2,128)S(1)}, f32[2,2,64,128]{3,1,2,0:T(2,128)S(1)}, u32[]{:S(2)}, u32[]{:S(2)}) collective-permute-start(f32[2,2,64,128]{3,1,2,0:T(2,128)S(1)} %get-tuple-element.357), channel_id=1, source_target_pairs={{32,0},{64,32},{96,64},{128,96},{160,128},{192,160},{224,192},{256... | collective-permute-start | bytes 393224 | tf_op jit(solution)/shard_map/ppermute | solution.py:29
  73.3 6.3 collective-permute-start.10
  74.8 6.0 collective-permute-start.11
  81.4 13.1 %collective-permute-start.12 = (f32[2,64,32]{2,1,0:T(8,128)S(1)}, f32[2,64,32]{2,1,0:T(8,128)S(1)}, u32[]{:S(2)}, u32[]{:S(2)}) collective-permute-start(f32[2,64,32]{2,1,0:T(8,128)S(1)} %slice.315), channel_id=1, source_target_pairs={{0,32},{32,64},{64,96},{96,128},{128,160},{160,192},{192,224},{224... | collective-permute-start | bytes 49160 | tf_op jit(solution)/shard_map/ppermute | solution.py:27
  84.5 11.8 %collective-permute-start.13 = (f32[2,64,32]{2,1,0:T(8,128)S(1)}, f32[2,64,32]{2,1,0:T(8,128)S(1)}, u32[]{:S(2)}, u32[]{:S(2)}) collective-permute-start(f32[2,64,32]{2,1,0:T(8,128)S(1)} %slice.317), channel_id=1, source_target_pairs={{32,0},{64,32},{96,64},{128,96},{160,128},{192,160},{224,192},{256... | collective-permute-start | bytes 49160 | tf_op jit(solution)/shard_map/ppermute | solution.py:29
  96.4 6.2 collective-permute-start.14
  105.2 13.0 %collective-permute-start = (f32[2,2,64,128]{3,1,2,0:T(2,128)S(1)}, f32[2,2,64,128]{3,1,2,0:T(2,128)S(1)}, u32[]{:S(2)}, u32[]{:S(2)}) collective-permute-start(f32[2,2,64,128]{3,1,2,0:T(2,128)S(1)} %get-tuple-element.435), channel_id=1, source_target_pairs={{32,0},{64,32},{96,64},{128,96},{160,128},{192,160},{224,192},{256... | collective-permute-start | bytes 393224 | tf_op jit(solution)/shard_map/while/body/eval_jaxpr/ppermute | solution.py:29
  115.5 19.7 %collective-permute-start.1 = (f32[2,2,64,128]{3,1,2,0:T(2,128)S(1)}, f32[2,2,64,128]{3,1,2,0:T(2,128)S(1)}, u32[]{:S(2)}, u32[]{:S(2)}) collective-permute-start(f32[2,2,64,128]{3,1,2,0:T(2,128)S(1)} %get-tuple-element.436), channel_id=1, source_target_pairs={{0,32},{32,64},{64,96},{96,128},{128,160},{160,192},{192,224},{224... | collective-permute-start | bytes 393224 | tf_op jit(solution)/shard_map/while/body/eval_jaxpr/ppermute | solution.py:27
  142.8 5.9 collective-permute-start.4
  147.3 5.6 collective-permute-start.5
  156.4 6.9 collective-permute-start
  158.3 16.6 %collective-permute-start.1 = (f32[2,2,64,128]{3,1,2,0:T(2,128)S(1)}, f32[2,2,64,128]{3,1,2,0:T(2,128)S(1)}, u32[]{:S(2)}, u32[]{:S(2)}) collective-permute-start(f32[2,2,64,128]{3,1,2,0:T(2,128)S(1)} %get-tuple-element.436), channel_id=1, source_target_pairs={{0,32},{32,64},{64,96},{96,128},{128,160},{160,192},{192,224},{224... | collective-permute-start | bytes 393224 | tf_op jit(solution)/shard_map/while/body/eval_jaxpr/ppermute | solution.py:27
  185.6 5.6 collective-permute-start.5
  194.7 6.9 collective-permute-start
  196.6 14.8 %collective-permute-start.1 = (f32[2,2,64,128]{3,1,2,0:T(2,128)S(1)}, f32[2,2,64,128]{3,1,2,0:T(2,128)S(1)}, u32[]{:S(2)}, u32[]{:S(2)}) collective-permute-start(f32[2,2,64,128]{3,1,2,0:T(2,128)S(1)} %get-tuple-element.436), channel_id=1, source_target_pairs={{0,32},{32,64},{64,96},{96,128},{128,160},{160,192},{192,224},{224... | collective-permute-start | bytes 393224 | tf_op jit(solution)/shard_map/while/body/eval_jaxpr/ppermute | solution.py:27
  221.8 5.6 collective-permute-start.5
  230.8 6.9 collective-permute-start
  232.8 12.9 %collective-permute-start.1 = (f32[2,2,64,128]{3,1,2,0:T(2,128)S(1)}, f32[2,2,64,128]{3,1,2,0:T(2,128)S(1)}, u32[]{:S(2)}, u32[]{:S(2)}) collective-permute-start(f32[2,2,64,128]{3,1,2,0:T(2,128)S(1)} %get-tuple-element.436), channel_id=1, source_target_pairs={{0,32},{32,64},{64,96},{96,128},{128,160},{160,192},{192,224},{224... | collective-permute-start | bytes 393224 | tf_op jit(solution)/shard_map/while/body/eval_jaxpr/ppermute | solution.py:27
  247.6 14.3 %collective-permute-start.3 = (f32[2,8,2,128]{3,1,2,0:T(8,128)S(1)}, f32[2,8,2,128]{3,1,2,0:T(8,128)S(1)}, u32[]{:S(2)}, u32[]{:S(2)}) collective-permute-start(f32[2,8,2,128]{3,1,2,0:T(8,128)S(1)} %get-tuple-element.438), channel_id=1, source_target_pairs={{0,4},{4,8},{8,12},{12,16},{16,20},{20,24},{24,28},{1,5},{5,9},{9,... | collective-permute-start | bytes 49160 | tf_op jit(solution)/shard_map/while/body/eval_jaxpr/ppermute | solution.py:27
  274.1 6.9 collective-permute-start
  276.0 18.3 %collective-permute-start.1 = (f32[2,2,64,128]{3,1,2,0:T(2,128)S(1)}, f32[2,2,64,128]{3,1,2,0:T(2,128)S(1)}, u32[]{:S(2)}, u32[]{:S(2)}) collective-permute-start(f32[2,2,64,128]{3,1,2,0:T(2,128)S(1)} %get-tuple-element.436), channel_id=1, source_target_pairs={{0,32},{32,64},{64,96},{96,128},{128,160},{160,192},{192,224},{224... | collective-permute-start | bytes 393224 | tf_op jit(solution)/shard_map/while/body/eval_jaxpr/ppermute | solution.py:27
  304.7 5.6 collective-permute-start.5
  313.7 6.9 collective-permute-start
  315.7 17.2 %collective-permute-start.1 = (f32[2,2,64,128]{3,1,2,0:T(2,128)S(1)}, f32[2,2,64,128]{3,1,2,0:T(2,128)S(1)}, u32[]{:S(2)}, u32[]{:S(2)}) collective-permute-start(f32[2,2,64,128]{3,1,2,0:T(2,128)S(1)} %get-tuple-element.436), channel_id=1, source_target_pairs={{0,32},{32,64},{64,96},{96,128},{128,160},{160,192},{192,224},{224... | collective-permute-start | bytes 393224 | tf_op jit(solution)/shard_map/while/body/eval_jaxpr/ppermute | solution.py:27
  352.0 6.9 collective-permute-start
  354.0 15.4 %collective-permute-start.1 = (f32[2,2,64,128]{3,1,2,0:T(2,128)S(1)}, f32[2,2,64,128]{3,1,2,0:T(2,128)S(1)}, u32[]{:S(2)}, u32[]{:S(2)}) collective-permute-start(f32[2,2,64,128]{3,1,2,0:T(2,128)S(1)} %get-tuple-element.436), channel_id=1, source_target_pairs={{0,32},{32,64},{64,96},{96,128},{128,160},{160,192},{192,224},{224... | collective-permute-start | bytes 393224 | tf_op jit(solution)/shard_map/while/body/eval_jaxpr/ppermute | solution.py:27
  388.7 6.9 collective-permute-start
  390.6 16.1 %collective-permute-start.1 = (f32[2,2,64,128]{3,1,2,0:T(2,128)S(1)}, f32[2,2,64,128]{3,1,2,0:T(2,128)S(1)}, u32[]{:S(2)}, u32[]{:S(2)}) collective-permute-start(f32[2,2,64,128]{3,1,2,0:T(2,128)S(1)} %get-tuple-element.436), channel_id=1, source_target_pairs={{0,32},{32,64},{64,96},{96,128},{128,160},{160,192},{192,224},{224... | collective-permute-start | bytes 393224 | tf_op jit(solution)/shard_map/while/body/eval_jaxpr/ppermute | solution.py:27
  426.3 6.9 collective-permute-start
  428.2 12.9 %collective-permute-start.1 = (f32[2,2,64,128]{3,1,2,0:T(2,128)S(1)}, f32[2,2,64,128]{3,1,2,0:T(2,128)S(1)}, u32[]{:S(2)}, u32[]{:S(2)}) collective-permute-start(f32[2,2,64,128]{3,1,2,0:T(2,128)S(1)} %get-tuple-element.436), channel_id=1, source_target_pairs={{0,32},{32,64},{64,96},{96,128},{128,160},{160,192},{192,224},{224... | collective-permute-start | bytes 393224 | tf_op jit(solution)/shard_map/while/body/eval_jaxpr/ppermute | solution.py:27
  443.1 10.2 %collective-permute-start.3 = (f32[2,8,2,128]{3,1,2,0:T(8,128)S(1)}, f32[2,8,2,128]{3,1,2,0:T(8,128)S(1)}, u32[]{:S(2)}, u32[]{:S(2)}) collective-permute-start(f32[2,8,2,128]{3,1,2,0:T(8,128)S(1)} %get-tuple-element.438), channel_id=1, source_target_pairs={{0,4},{4,8},{8,12},{12,16},{16,20},{20,24},{24,28},{1,5},{5,9},{9,... | collective-permute-start | bytes 49160 | tf_op jit(solution)/shard_map/while/body/eval_jaxpr/ppermute | solution.py:27
  453.9 5.7 collective-permute-start.4
  467.2 6.9 collective-permute-start
  469.2 20.1 %collective-permute-start.1 = (f32[2,2,64,128]{3,1,2,0:T(2,128)S(1)}, f32[2,2,64,128]{3,1,2,0:T(2,128)S(1)}, u32[]{:S(2)}, u32[]{:S(2)}) collective-permute-start(f32[2,2,64,128]{3,1,2,0:T(2,128)S(1)} %get-tuple-element.436), channel_id=1, source_target_pairs={{0,32},{32,64},{64,96},{96,128},{128,160},{160,192},{192,224},{224... | collective-permute-start | bytes 393224 | tf_op jit(solution)/shard_map/while/body/eval_jaxpr/ppermute | solution.py:27
  508.5 6.9 collective-permute-start
  510.4 18.7 %collective-permute-start.1 = (f32[2,2,64,128]{3,1,2,0:T(2,128)S(1)}, f32[2,2,64,128]{3,1,2,0:T(2,128)S(1)}, u32[]{:S(2)}, u32[]{:S(2)}) collective-permute-start(f32[2,2,64,128]{3,1,2,0:T(2,128)S(1)} %get-tuple-element.436), channel_id=1, source_target_pairs={{0,32},{32,64},{64,96},{96,128},{128,160},{160,192},{192,224},{224... | collective-permute-start | bytes 393224 | tf_op jit(solution)/shard_map/while/body/eval_jaxpr/ppermute | solution.py:27
  548.3 6.9 collective-permute-start
  550.2 17.8 %collective-permute-start.1 = (f32[2,2,64,128]{3,1,2,0:T(2,128)S(1)}, f32[2,2,64,128]{3,1,2,0:T(2,128)S(1)}, u32[]{:S(2)}, u32[]{:S(2)}) collective-permute-start(f32[2,2,64,128]{3,1,2,0:T(2,128)S(1)} %get-tuple-element.436), channel_id=1, source_target_pairs={{0,32},{32,64},{64,96},{96,128},{128,160},{160,192},{192,224},{224... | collective-permute-start | bytes 393224 | tf_op jit(solution)/shard_map/while/body/eval_jaxpr/ppermute | solution.py:27
  587.3 6.9 collective-permute-start
  589.2 16.8 %collective-permute-start.1 = (f32[2,2,64,128]{3,1,2,0:T(2,128)S(1)}, f32[2,2,64,128]{3,1,2,0:T(2,128)S(1)}, u32[]{:S(2)}, u32[]{:S(2)}) collective-permute-start(f32[2,2,64,128]{3,1,2,0:T(2,128)S(1)} %get-tuple-element.436), channel_id=1, source_target_pairs={{0,32},{32,64},{64,96},{96,128},{128,160},{160,192},{192,224},{224... | collective-permute-start | bytes 393224 | tf_op jit(solution)/shard_map/while/body/eval_jaxpr/ppermute | solution.py:27
  625.3 6.9 collective-permute-start
  627.3 18.6 %collective-permute-start.1 = (f32[2,2,64,128]{3,1,2,0:T(2,128)S(1)}, f32[2,2,64,128]{3,1,2,0:T(2,128)S(1)}, u32[]{:S(2)}, u32[]{:S(2)}) collective-permute-start(f32[2,2,64,128]{3,1,2,0:T(2,128)S(1)} %get-tuple-element.436), channel_id=1, source_target_pairs={{0,32},{32,64},{64,96},{96,128},{128,160},{160,192},{192,224},{224... | collective-permute-start | bytes 393224 | tf_op jit(solution)/shard_map/while/body/eval_jaxpr/ppermute | solution.py:27
  665.1 6.9 collective-permute-start
  667.0 18.6 %collective-permute-start.1 = (f32[2,2,64,128]{3,1,2,0:T(2,128)S(1)}, f32[2,2,64,128]{3,1,2,0:T(2,128)S(1)}, u32[]{:S(2)}, u32[]{:S(2)}) collective-permute-start(f32[2,2,64,128]{3,1,2,0:T(2,128)S(1)} %get-tuple-element.436), channel_id=1, source_target_pairs={{0,32},{32,64},{64,96},{96,128},{128,160},{160,192},{192,224},{224... | collective-permute-start | bytes 393224 | tf_op jit(solution)/shard_map/while/body/eval_jaxpr/ppermute | solution.py:27
  704.9 6.9 collective-permute-start
  706.8 17.5 %collective-permute-start.1 = (f32[2,2,64,128]{3,1,2,0:T(2,128)S(1)}, f32[2,2,64,128]{3,1,2,0:T(2,128)S(1)}, u32[]{:S(2)}, u32[]{:S(2)}) collective-permute-start(f32[2,2,64,128]{3,1,2,0:T(2,128)S(1)} %get-tuple-element.436), channel_id=1, source_target_pairs={{0,32},{32,64},{64,96},{96,128},{128,160},{160,192},{192,224},{224... | collective-permute-start | bytes 393224 | tf_op jit(solution)/shard_map/while/body/eval_jaxpr/ppermute | solution.py:27
  (64 other events, 338.1 us)
where the time goes:
time: 748 us; the launch traced here: 744 us
  waiting for transfers between devices  350 us (47%)
  starting transfers between devices  283 us (38%)
  other arithmetic  59.8 us (8%)
  local copies, waits for them, and re-layouts  47.9 us (6%)
    ppermute x53, waiting for transfers between devices, with_halo(): lax.ppermute(tail, axis, [(i, (i + 1) % count) for i in range(ends)])  342 us
    ppermute x53, starting transfers between devices, with_halo(): lax.ppermute(head, axis, [((i + 1) % count, i) for i in range(ends)])  140 us
    ppermute x53, starting transfers between devices, with_halo(): lax.ppermute(tail, axis, [(i, (i + 1) % count) for i in range(ends)])  130 us
    mul x32, other arithmetic, advance(): return living * updated  30 us
    concatenate x35, other arithmetic, with_halo(): jnp.concatenate([lax.ppermute(tail, axis, [(i, (i + 1) % count) for i in...  20.8 us
  transfers between devices with their start and end apart: 107, of which 68 were waited for; matrix products, arithmetic and copies ran while one was open for 4% of the time, Pallas kernels for 0%

commit v1 on v0

v1 whole, which is shorter than its diff:
```python
import jax
import jax.numpy as jnp
from jax import lax
from jax.experimental import pallas as pl
from jax.experimental.pallas import tpu as pltpu
from jax.sharding import Mesh, PartitionSpec as P


AXES = ("zh", "yc", "zl", "core", "gz")
SIZES = (4, 4, 4, 2, 4)
F32 = jnp.float32
VM = pl.BlockSpec(memory_space=pltpu.VMEM)
SM = pl.BlockSpec(memory_space=pltpu.SMEM)

TY, TZ, KS = 16, 32, 8
PAIRS, WZ, Z0 = 16, 96, 24
UNROLL = 2
FIELD_ROWS, MSG_ROWS = 48, 88


def linear(zh, yc, zl, core, gz):
    return (((zh * 4 + yc) * 4 + zl) * 2 + core) * 4 + gz


def tile_devices():
    table = {}
    for zh in range(4):
        for yc in range(4):
            for zl in range(4):
                for core in range(2):
                    for gz in range(4):
                        gy = zl * 2 + core
                        ty = gy * 4 + ((yc - zl) % 4 if core == 0 else (zl - yc) % 4)
                        tz = gz * 4 + (zh if (gz + core) % 2 == 0 else 3 - zh)
                        table[ty, tz] = linear(zh, yc, zl, core, gz)
    return table


def pairs_along(dy, dz):
    table = tile_devices()
    return [
        (table[ty + dy, tz + dz], table[ty, tz])
        for (ty, tz) in sorted(table)
        if (ty + dy, tz + dz) in table
    ]


def source_of(flags, ys, zs):
    zh = zs + flags[2] * (3 - 2 * zs)
    yc = (flags[0] + ys - 2 * flags[1] * ys) & 3
    return zh * 4 + yc


def lane_group(rows):
    return lax.broadcasted_iota(jnp.int32, (rows, 128), 1) // 32


def low_lanes(rows):
    return lax.broadcasted_iota(jnp.int32, (rows, 128), 1) < 64


def pack_kernel(flags, now, prev, speed, receivers, out):
    group = lane_group(16)
    for field, ref in enumerate((now, prev, speed)):
        for x in range(4):
            parts = [ref[x, pl.ds(q, 16, stride=4), :] for q in range(4)]
            for zs in range(4):
                piece = None
                for q in range(4):
                    turn = (32 * (q - zs)) % 128
                    moved = parts[q] if turn == 0 else pltpu.roll(parts[q], turn, 1)
                    piece = moved if piece is None else jnp.where(group == q, moved, piece)
                for ys in range(4):
                    target = source_of(flags, ys, zs)
                    first = field * 16 + x * 4
                    out[target, first : first + 4, :] = piece[4 * ys : 4 * ys + 4]
    rows = receivers[...]
    for target in range(16):
        out[target, FIELD_ROWS:MSG_ROWS, :] = rows


def unpack_kernel(got, tile):
    low = low_lanes(128)
    solids = []
    for j in range(4):
        stack = []
        for field in range(2):
            stack += [got[src, pl.ds(field * 16 + j, 4, stride=4), :] for src in range(16)]
        tile[128 * j : 128 * j + 128, :] = jnp.concatenate(stack, axis=0).T
        speeds = [got[src, pl.ds(32 + j, 4, stride=4), :] for src in range(16)]
        speeds = jnp.concatenate(speeds, axis=0)
        solids.append(jnp.concatenate([speeds, jnp.zeros_like(speeds)], axis=0).T)
    for j in range(2):
        tile[512 + 128 * j : 640 + 128 * j, :] = jnp.where(
            low, solids[j], pltpu.roll(solids[j + 2], 64, 1)
        )


def source_kernel(flags, got, out):
    out[...] = jnp.zeros_like(out)

    @pl.when(flags[0] == 1)
    def _():
        def shard(src, total):
            terms = jnp.concatenate(
                [got[src, FIELD_ROWS + 8 * j : FIELD_ROWS + 8 * j + 8, :] for j in range(4)], axis=1
            )
            cell = jnp.concatenate([got[src, 80 + j : 81 + j, :] for j in range(4)], axis=1)
            cell = cell.astype(jnp.int32)
            cell_x = cell >> 9
            cell_y = (cell & 511) - flags[1]
            upper = terms.astype(jnp.bfloat16).astype(F32)
            lower = terms - upper
            at_x = (lax.broadcasted_iota(jnp.int32, (64, 512), 0) == cell_x).astype(F32)
            at_x = at_x.astype(jnp.bfloat16)
            here = [jnp.broadcast_to(cell_y, (8, 512)) == y for y in range(2 * PAIRS)]
            for part in (upper, lower):
                rows = jnp.concatenate([jnp.where(h, part, 0.0) for h in here], axis=0)
                total = total + lax.dot_general(
                    rows.astype(jnp.bfloat16),
                    at_x,
                    (((1,), (1,)), ((), ())),
                    preferred_element_type=F32,
                )
            return total

        total = lax.fori_loop(0, 16, shard, jnp.zeros((PAIRS * 16, 64), F32))
        total = jnp.concatenate([total[: PAIRS * 8], total[PAIRS * 8 :]], axis=1)
        out[0] = total.reshape(PAIRS, 8, 128)


def swap(rows):
    return pltpu.roll(rows, 64, 1)


def mix(lower, upper):
    return jnp.where(low_lanes(lower.shape[0]), lower, upper)


def load_pair(a, b, i, z, lower, upper):
    at = z + Z0
    a[i + 1, at : at + lower.shape[0], :] = mix(lower, swap(upper))
    b[i + 1, at : at + lower.shape[0], :] = mix(swap(lower), upper)


def lower_of(a, b, i, z, count):
    at = z + Z0
    return mix(a[i + 1, at : at + count, :], swap(b[i + 1, at : at + count, :]))


def upper_of(a, b, i, z, count):
    at = z + Z0
    return mix(swap(a[i + 1, at : at + count, :]), b[i + 1, at : at + count, :])


def left_speeds(i, top, right):
    if i >= 8:
        return right(i - 8)
    rows = top(i % 4)
    return mix(rows if i < 4 else swap(rows), swap(right(8 + i)))


def advance(a, b, k, m, planes, chunk, z_first, z_last, opening=False):
    top = (lax.broadcasted_iota(jnp.int32, (8, 128), 0) == 0).astype(F32)
    lane = lax.broadcasted_iota(jnp.int32, (8, 128), 1) % 64
    first, last = lane == 0, lane == 63
    starts = range(z_first + Z0, z_last + Z0, 8)
    low = low_lanes(8)

    def weigh(i, nothing):
        for at in starts:
            speed = k[i, at : at + 8, :]
            m[i, at : at + 8, :] = jnp.where(speed > 0.0, 2.0 - 6.0 * speed, 0.0)
        return nothing

    lax.fori_loop(0, PAIRS, weigh, 0)

    def drain(field):
        def row(i, nothing):
            for at in starts:
                kept = field[i + 1, at : at + 8, :]
                field[i + 1, at : at + 8, :] = jnp.where(k[i, at : at + 8, :] > 0.0, kept, 0.0)
            return nothing

        lax.fori_loop(0, PAIRS, row, 0)

    def beside(c):
        return jnp.where(first, 0.0, pltpu.roll(c, 1, 1)) + jnp.where(
            last, 0.0, pltpu.roll(c, 127, 1)
        )

    def one(now, old, step):
        for at in starts:
            now[0, at : at + 8, :] = jnp.where(low, 0.0, swap(now[PAIRS, at : at + 8, :]))
            now[PAIRS + 1, at : at + 8, :] = jnp.where(low, swap(now[1, at : at + 8, :]), 0.0)

        def row(i, carried):
            behind, centre, sides = carried
            ahead = tuple(now[i + 2, at : at + 8, :] for at in starts)
            later = tuple(beside(c) for c in ahead)
            for t, at in enumerate(starts):
                c = centre[t]
                around = sides[t] + (ahead[t] + behind[t])
                around = around + (now[i + 1, at - 1 : at + 7, :] + now[i + 1, at + 1 : at + 9, :])
                new = m[i, at : at + 8, :] * c - old[i + 1, at : at + 8, :]
                new = new + k[i, at : at + 8, :] * around
                if at == Z0:
                    new = new + planes[chunk, i, pl.ds(step, 1), :] * top
                old[i + 1, at : at + 8, :] = new
            return centre, ahead, later

        behind = tuple(now[0, at : at + 8, :] for at in starts)
        centre = tuple(now[1, at : at + 8, :] for at in starts)
        lax.fori_loop(0, PAIRS, row, (behind, centre, tuple(beside(c) for c in centre)), unroll=UNROLL)

    def two(pair, nothing):
        one(a, b, 2 * pair)
        if opening:
            pl.when(pair == 0)(lambda: drain(a))
        one(b, a, 2 * pair + 1)
        return nothing

    if opening:
        drain(b)
    lax.fori_loop(0, KS // 2, two, 0)


def clear(a, b, z_first, z_last):
    zero = jnp.zeros((8, 128), F32)
    for ref in (a, b):
        for i in range(PAIRS + 2):
            ref[i, z_first + Z0 - 8 : z_first + Z0, :] = zero
            ref[i, z_last + Z0 : z_last + Z0 + 8, :] = zero


def round_one(tile, from_z, from_y, from_c, planes, state, msg, speeds, sides, a, b, k, m):
    clear(a, b, 0, 64)
    for lower, upper, z in ((tile, from_y, 0), (from_z, from_c, TZ)):
        for y in range(TY):
            rows = slice(y * TZ, y * TZ + TZ)
            load_pair(a, b, y, z, lower[rows, :], upper[rows, :])
        for y in range(8):
            rows = slice(512 + y * TZ, 512 + y * TZ + TZ)
            k[y, z + Z0 : z + Z0 + TZ, :] = mix(lower[rows, :], swap(upper[rows, :]))
            k[y + 8, z + Z0 : z + Z0 + TZ, :] = mix(swap(lower[rows, :]), upper[rows, :])
    advance(a, b, k, m, planes, 0, 0, 64, opening=True)
    for i in range(PAIRS):
        rows = lower_of(a, b, i, 0, 56)
        state[i * 56 : i * 56 + 56, :] = rows
        if i >= 8:
            msg[(i - 8) * 56 : (i - 8) * 56 + 56, :] = rows
    for i in range(8):
        rows = upper_of(a, b, i, 0, 56)
        state[(i + 16) * 56 : (i + 16) * 56 + 56, :] = rows
        msg[(i + 8) * 56 : (i + 8) * 56 + 56, :] = rows
    for y in range(4):
        msg[896 + y * 56 : 952 + y * 56, :] = mix(
            k[8 + y, Z0 : Z0 + 56, :], swap(k[12 + y, Z0 : Z0 + 56, :])
        )
    for i in range(PAIRS):
        speeds[i] = k[i, Z0 : Z0 + 64, :]
        sides[i] = k[i, Z0 + 16 : Z0 + 32, :]


def load_left(flags, state, from_y, a, b, z, count):
    for i in range(PAIRS):
        rows = from_y[i * count : i * count + count, :]
        if i >= 8:
            rows = jnp.where(flags[0] == 1, state[(i - 8) * count : (i - 7) * count, :], rows)
        load_pair(a, b, i, z, rows, state[(i + 8) * count : (i + 9) * count, :])


def round_two(flags, state, from_y, planes, speeds, tile, msg, a, b, k, m):
    clear(a, b, 0, 56)
    load_left(flags, state, from_y, a, b, 0, 56)
    for i in range(PAIRS):
        k[i, Z0 : Z0 + 56, :] = left_speeds(
            i, lambda y: from_y[896 + y * 56 : 952 + y * 56, :], lambda j: speeds[j, 0:56, :]
        )
    advance(a, b, k, m, planes, 1, 0, 56)
    for y in range(TY):
        rows = lower_of(a, b, y + 8, 0, 48) if y < 8 else upper_of(a, b, y - 8, 0, 48)
        tile[y * 48 : y * 48 + 48, :] = rows
        msg[y * 32 : y * 32 + 32, :] = rows[16:48]


def round_three(flags, tile, from_z, from_y, from_c, planes, speeds, sides, state, msg, a, b, k, m):
    clear(a, b, -16, 48)
    for y in range(TY):
        near = []
        for main, side in ((tile, from_z), (from_y, from_c)):
            near.append(
                jnp.where(
                    flags[0] == 1,
                    main[y * 48 : y * 48 + 16, :],
                    side[y * 32 + 16 : y * 32 + 32, :],
                )
            )
        load_pair(
            a, b, y, -16, from_z[y * 32 : y * 32 + 16, :], from_c[y * 32 : y * 32 + 16, :]
        )
        load_pair(a, b, y, 0, *near)
        load_pair(
            a, b, y, 16, tile[y * 48 + 16 : y * 48 + 48, :], from_y[y * 48 + 16 : y * 48 + 48, :]
        )
        k[y, Z0 - 16 : Z0, :] = sides[y]
        k[y, Z0 : Z0 + 48, :] = speeds[y, 0:48, :]
    advance(a, b, k, m, planes, 2, -16, 48)
    for i in range(PAIRS):
        rows = lower_of(a, b, i, -8, 48)
        state[i * 48 : i * 48 + 48, :] = rows
        if i >= 8:
            msg[(i - 8) * 48 : (i - 8) * 48 + 48, :] = rows
    for i in range(8):
        rows = upper_of(a, b, i, -8, 48)
        state[(i + 16) * 48 : (i + 16) * 48 + 48, :] = rows
        msg[(i + 8) * 48 : (i + 8) * 48 + 48, :] = rows
    for y in range(4):
        msg[768 + y * 8 : 776 + y * 8, :] = mix(
            k[8 + y, Z0 - 8 : Z0, :], swap(k[12 + y, Z0 - 8 : Z0, :])
        )


def round_four(flags, state, from_y, planes, speeds, sides, above, out, a, b, k, m):
    clear(a, b, -8, 40)
    load_left(flags, state, from_y, a, b, -8, 48)
    for i in range(PAIRS):
        k[i, Z0 - 8 : Z0, :] = left_speeds(
            i, lambda y: from_y[768 + y * 8 : 776 + y * 8, :], lambda j: sides[j, 8:16, :]
        )
        k[i, Z0 : Z0 + 40, :] = left_speeds(
            i, lambda y: above[896 + y * 56 : 936 + y * 56, :], lambda j: speeds[j, 0:40, :]
        )
    advance(a, b, k, m, planes, 3, -8, 40)
    for j in range(4):
        first = 4 * j + 9 if j < 2 else 4 * j - 7
        turned = jnp.concatenate([a[first + q, Z0 : Z0 + TZ, :] for q in range(4)], axis=0).T
        half = 0 if j < 2 else 64
        for target in range(16):
            at = half + 4 * target
            out[target, 4 * j : 4 * j + 4, :] = turned[at : at + 4]


def deliver_kernel(flags, got, out):
    group = lane_group(16)
    for x in range(4):
        parts = []
        for zs in range(4):
            rows = [
                got[source_of(flags, ys, zs), pl.ds(x, 4, stride=4), :] for ys in range(4)
            ]
            parts.append(jnp.concatenate(rows, axis=0))
        for q in range(4):
            piece = None
            for zs in range(4):
                turn = (32 * (zs - q)) % 128
                moved = parts[zs] if turn == 0 else pltpu.roll(parts[zs], turn, 1)
                piece = moved if piece is None else jnp.where(group == zs, moved, piece)
            out[x, pl.ds(q, 16, stride=4), :] = piece


def call(kernel, outs, *args, flags=None, scratch=False, cost=2_000_000):
    shapes = [jax.ShapeDtypeStruct(s, F32) for s in outs]
    specs = [VM] * len(args)
    if flags is not None:
        args = (flags,) + args
        specs = [SM] + specs
    return pl.pallas_call(
        kernel,
        out_shape=shapes,
        in_specs=specs,
        out_specs=[VM] * len(outs),
        scratch_shapes=(
            [pltpu.VMEM((PAIRS + 2, WZ, 128), F32)] * 2 + [pltpu.VMEM((PAIRS, WZ, 128), F32)] * 2
            if scratch
            else []
        ),
        compiler_params=pltpu.CompilerParams(vmem_limit_bytes=48 * 1024 * 1024),
        cost_estimate=pl.CostEstimate(flops=cost, bytes_accessed=1_000_000, transcendentals=0),
    )(*args)


def local(
    traces,
    receiver_cell,
    weight_class,
    weight_table,
    obstacle_top,
    obstacle_thick,
    courant,
    p_now,
    p_prev,
):
    zh, yc, zl, core, gz = (lax.axis_index(a) for a in AXES)
    gy = zl * 2 + core
    flip_z = (gz + core) % 2
    ty = gy * 4 + jnp.where(core == 0, yc - zl, zl - yc) % 4
    tz = gz * 4 + zh + flip_z * (3 - 2 * zh)
    place = jnp.stack([zl, core, flip_z]).astype(jnp.int32)

    roof = jnp.repeat(jnp.repeat(obstacle_top, 2, axis=0), 2, axis=1)[:, :, None]
    thickness = jnp.repeat(jnp.repeat(obstacle_thick, 2, axis=0), 2, axis=1)[:, :, None]
    depth = gz * 128 + jnp.arange(128, dtype=jnp.int32)[None, None, :]
    solid = (depth >= roof) & (depth < roof + thickness)
    speed = jnp.where(solid, 0.0, courant)

    classes = weight_class[:, None] == jnp.arange(16, dtype=jnp.int32)[None, :]
    weights = jnp.sum(jnp.where(classes, weight_table[None, :], 0.0), axis=1)
    own = lax.dynamic_slice_in_dim(traces, 24 - 8 * gz, 8, axis=1)[:, ::-1]
    terms = weights[:, None] * own.astype(F32)
    terms = terms.reshape(4, 128, 8).transpose(0, 2, 1).reshape(32, 128)
    cells = receiver_cell.astype(F32).reshape(4, 128)
    receivers = jnp.concatenate([terms, cells, jnp.zeros((4, 128), F32)], axis=0)

    (packed,) = call(
        pack_kernel, [(16, MSG_ROWS, 128)], p_now, p_prev, speed, receivers, flags=place
    )
    got = lax.all_to_all(packed, ("zh", "yc"), 0, 0, tiled=True)

    def moved(array, dy, dz):
        return lax.ppermute(array, AXES, pairs_along(dy, dz))


    (tile,) = call(unpack_kernel, [(768, 128)], got)
    from_y = moved(tile, 1, 0)
    from_z = moved(tile, 0, 1)
    works = jnp.stack([(zh == 3 * core), ty * 16 - 8 * (gz % 2)]).astype(jnp.int32)
    (planes,) = call(source_kernel, [(4, PAIRS, 8, 128)], got, flags=works, cost=20_000_000)
    planes = lax.all_to_all(planes, "gz", 0, 0, tiled=True)
    from_c = moved(from_z, 1, 0)
    first_y = (ty == 0).astype(jnp.int32)[None]
    first_z = (tz == 0).astype(jnp.int32)[None]

    state, msg, speeds, sides = call(
        round_one, [(1344, 128), (1120, 128), (PAIRS, 64, 128), (PAIRS, 16, 128)],
        tile, from_z, from_y, from_c, planes, scratch=True,
    )
    above = moved(msg, -1, 0)
    sides = moved(sides, 0, -1)
    tile, msg = call(
        round_two, [(768, 128), (512, 128)],
        state, above, planes, speeds, flags=first_y, scratch=True,
    )
    from_y = moved(tile, 1, 0)
    from_z = moved(msg, 0, -1)
    from_c = moved(from_z, 1, 0)
    state, msg = call(
        round_three, [(1152, 128), (800, 128)],
        tile, from_z, from_y, from_c, planes, speeds, sides, flags=first_z, scratch=True,
    )
    (out,) = call(
        round_four, [(16, 16, 128)],
        state, moved(msg, -1, 0), planes, speeds, sides, above, flags=first_y, scratch=True,
    )
    out = lax.all_to_all(out, ("zh", "yc"), 0, 0, tiled=True)
    (wavefield,) = call(deliver_kernel, [(4, 64, 128)], out, flags=place)
    return wavefield


def solution(mesh):
    fine = Mesh(mesh.devices.reshape(SIZES), AXES)
    gx, gy, gz = ("zh", "yc"), ("zl", "core"), "gz"
    placed = (
        P(gx, None),
        P(gx),
        P(gx),
        P(),
        P(gx, gy),
        P(gx, gy),
        P(gx, gy, gz),
        P(gx, gy, gz),
        P(gx, gy, gz),
    )

    return jax.shard_map(
        local, mesh=fine, in_specs=placed, out_specs=P(gx, gy, gz), check_vma=False
    )
```

time: 748 us -> 251 us (0.34)
  the two profiles are of different devices: /device:TPU:486 before, /device:TPU:71 now
where the time goes in v1:
time: 251 us; the launch traced here: 250 us
  blocking collectives  115 us (46%)
  starting transfers between devices  54.6 us (22%)
  waiting for transfers between devices  41.3 us (16%)
  Pallas kernels  35.3 us (14%)
  local copies, waits for them, and re-layouts  3.9 us (2%)
    all_to_all x1, blocking collectives, local(): got = lax.all_to_all(packed, ('zh', 'yc'), 0, 0, tiled=True)  56.8 us
    ppermute x9, starting transfers between devices, moved(): return lax.ppermute(array, AXES, pairs_along(dy, dz))  54.6 us
    all_to_all x1, blocking collectives, local(): out = lax.all_to_all(out, ('zh', 'yc'), 0, 0, tiled=True)  50.4 us
    ppermute x9, waiting for transfers between devices, moved(): return lax.ppermute(array, AXES, pairs_along(dy, dz))  41.3 us
    pallas_call x8, Pallas kernels, call(): pl.pallas_call(kernel, out_shape=shapes, in_specs=specs, out_specs=[VM] *...  35.3 us
    all_to_all x1, blocking collectives, local(): planes = lax.all_to_all(planes, 'gz', 0, 0, tiled=True)  7.49 us
  transfers between devices with their start and end apart: 9, of which 5 were waited for; matrix products, arithmetic and copies ran while one was open for 0% of the time, Pallas kernels for 0%

profile of v1, /device:TPU:71, one launch (start us, length us, event | category | flops | bytes accessed | tf_op | source)
XLA Modules:
  0.0 250.4 jit_solution(10121281853068346011)
XLA Ops:
  0.0 0.7 copy-done.4
  0.7 0.1 copy-done
  0.8 0.1 rev.3
  0.9 0.6 copy-done.6
  1.5 0.1 copy.16
  1.6 0.6 copy-done.7
  2.1 0.1 copy.14
  2.2 0.1 copy.15
  2.4 0.1 copy.17
  2.4 0.1 pad.4.clone
  2.5 0.6 copy-done.5
  3.1 0.0 copy-done.8
  3.1 0.1 select_reduce_fusion
  3.2 0.1 pad_add_fusion.flags
  3.3 0.1 maximum_maximum_fusion.receivers
  3.4 0.1 and_select_fusion.speed
  3.5 0.8 copy-done.1
  4.3 0.1 copy-done.2
  4.3 0.9 shard_map.91
  5.3 56.8 %all_to_all.15.got = f32[16,88,128]{2,1,0:T(8,128)S(1)} all-to-all(f32[16,88,128]{2,1,0:T(8,128)S(1)} %shard_map.91), channel_id=1, replica_groups=mesh['zh'=4,'yc'=4,'zl'=4,'core'=2,'gz'=4] {'zh','yc'}, dimensions={0} | all-to-all | bytes 1441792 | tf_op jit(solution)/shard_map/all_to_all | solution.py:418
  62.0 0.3 shard_map.92.tile
  62.3 2.5 collective-permute-start
  64.8 1.9 collective-permute-start.1
  66.7 21.5 %collective-permute-done.from_z = f32[768,128]{1,0:T(8,128)S(1)} collective-permute-done((f32[768,128]{1,0:T(8,128)S(1)}, f32[768,128]{1,0:T(8,128)S(1)}, u32[]{:S(2)}, u32[]{:S(2)}) %collective-permute-start) | collective-permute-done | bytes 393248 | tf_op jit(solution)/shard_map/ppermute | solution.py:421
  88.2 1.9 collective-permute-start.2
  90.2 0.1 pad_add_fusion.1.flags
  90.2 0.6 shard_map.93
  90.8 7.5 %all_to_all.16.planes = f32[4,16,8,128]{3,2,1,0:T(8,128)S(1)} all-to-all(f32[4,16,8,128]{3,2,1,0:T(8,128)S(1)} %shard_map.93), channel_id=1, replica_groups=mesh['zh'=4,'yc'=4,'zl'=4,'core'=2,'gz'=4] {'gz'}, dimensions={0} | all-to-all | bytes 524288 | tf_op jit(solution)/shard_map/all_to_all | solution.py:429
  98.3 0.0 collective-permute-done.1.from_y
  98.3 0.0 collective-permute-done.2.from_c
  98.3 9.3 %shard_map.94 = (f32[1344,128]{1,0:T(8,128)S(1)}, f32[1120,128]{1,0:T(8,128)}, f32[16,64,128]{2,1,0:T(8,128)S(1)}, f32[16,16,128]{2,1,0:T(8,128)S(1)}) custom-call(f32[768,128]{1,0:T(8,128)S(1)} %shard_map.92.tile, f32[768,128]{1,0:T(8,128)S(1)} %collective-permute-done.from_z, f32[768,128]{1,0:T(8,128)S(1)} %collective-permute-done.1.from_y, ...), custom_call_target="tpu_custom_call" | custom-call | flops 2000000 | bytes 1000000 | tf_op jit(solution)/shard_map/pallas_call | solution.py:368
  107.6 4.6 %collective-permute-start.3 = (f32[1120,128]{1,0:T(8,128)}, f32[1120,128]{1,0:T(8,128)S(1)}, u32[]{:S(2)}, u32[]{:S(2)}) collective-permute-start(f32[1120,128]{1,0:T(8,128)} %get-tuple-element.14), channel_id=1, source_target_pairs={{0,32},{128,160},{256,288},{384,416},{385,417},{257,289},{129,161}... | collective-permute-start | bytes 1720328 | tf_op jit(solution)/shard_map/ppermute | solution.py:421
  112.1 6.9 %collective-permute-done.3.from_y.above = f32[1120,128]{1,0:T(8,128)S(1)} collective-permute-done((f32[1120,128]{1,0:T(8,128)}, f32[1120,128]{1,0:T(8,128)S(1)}, u32[]{:S(2)}, u32[]{:S(2)}) %collective-permute-start.3) | collective-permute-done | bytes 573472 | tf_op jit(solution)/shard_map/ppermute | solution.py:421
  119.1 7.6 %shard_map.95 = (f32[768,128]{1,0:T(8,128)S(1)}, f32[512,128]{1,0:T(8,128)S(1)}) custom-call(s32[1]{0:T(128)} %bitcast.3.flags, f32[1344,128]{1,0:T(8,128)S(1)} %get-tuple-element.13.state, f32[1120,128]{1,0:T(8,128)S(1)} %collective-permute-done.3.from_y.above, f32[4,16,8,128]{3,2,1,0:T(8,128)S(1)} %all_to_all.16.planes, ...), custom_call_target="tpu_custom_call" | custom-call | flops 2000000 | bytes 1000000 | tf_op jit(solution)/shard_map/pallas_call | solution.py:368
  126.7 9.7 %collective-permute-start.4 = (f32[512,128]{1,0:T(8,128)S(1)}, f32[512,128]{1,0:T(8,128)S(1)}, u32[]{:S(2)}, u32[]{:S(2)}) collective-permute-start(f32[512,128]{1,0:T(8,128)S(1)} %get-tuple-element.17), channel_id=1, source_target_pairs={{0,128},{128,256},{256,384},{384,385},{385,257},{257,129},{129,1},... | collective-permute-start | bytes 786440 | tf_op jit(solution)/shard_map/ppermute | solution.py:421
  136.5 1.9 collective-permute-start.5
  138.4 4.2 %collective-permute-done.4.from_z = f32[512,128]{1,0:T(8,128)S(1)} collective-permute-done((f32[512,128]{1,0:T(8,128)S(1)}, f32[512,128]{1,0:T(8,128)S(1)}, u32[]{:S(2)}, u32[]{:S(2)}) %collective-permute-start.4) | collective-permute-done | bytes 262176 | tf_op jit(solution)/shard_map/ppermute | solution.py:421
  142.6 1.9 collective-permute-start.6
  144.5 28.3 %collective-permute-start.7 = (f32[16,16,128]{2,1,0:T(8,128)S(1)}, f32[16,16,128]{2,1,0:T(8,128)S(1)}, u32[]{:S(2)}, u32[]{:S(2)}) collective-permute-start(f32[16,16,128]{2,1,0:T(8,128)S(1)} %get-tuple-element.18), channel_id=1, source_target_pairs={{0,128},{128,256},{256,384},{384,385},{385,257},{257,129},{129,1},... | collective-permute-start | bytes 393224 | tf_op jit(solution)/shard_map/ppermute | solution.py:421
  172.8 1.9 collective-permute-done.7.sides
  174.7 0.0 collective-permute-done.5.from_y
  174.7 0.0 collective-permute-done.6.from_c
  174.7 8.0 %shard_map.96 = (f32[1152,128]{1,0:T(8,128)S(1)}, f32[800,128]{1,0:T(8,128)S(1)}) custom-call(s32[1]{0:T(128)} %bitcast.4.flags, f32[768,128]{1,0:T(8,128)S(1)} %get-tuple-element.16.tile, f32[512,128]{1,0:T(8,128)S(1)} %collective-permute-done.4.from_z, f32[768,128]{1,0:T(8,128)S(1)} %collective-permute-done.5.from_y, ...), custom_call_target="tpu_custom_call" | custom-call | flops 2000000 | bytes 1000000 | tf_op jit(solution)/shard_map/pallas_call | solution.py:368
  182.7 1.9 collective-permute-start.8
  184.6 6.8 %collective-permute-done.8.from_y = f32[800,128]{1,0:T(8,128)S(1)} collective-permute-done((f32[800,128]{1,0:T(8,128)S(1)}, f32[800,128]{1,0:T(8,128)S(1)}, u32[]{:S(2)}, u32[]{:S(2)}) %collective-permute-start.8) | collective-permute-done | bytes 409632 | tf_op jit(solution)/shard_map/ppermute | solution.py:421
  191.4 7.2 %shard_map.97 = f32[16,16,128]{2,1,0:T(8,128)S(1)} custom-call(s32[1]{0:T(128)} %bitcast.3.flags, f32[1152,128]{1,0:T(8,128)S(1)} %get-tuple-element.19.state, f32[800,128]{1,0:T(8,128)S(1)} %collective-permute-done.8.from_y, f32[4,16,8,128]{3,2,1,0:T(8,128)S(1)} %all_to_all.16.planes, f32[16,64,128]{2,1,0:T(8,128)S(1)} %get-tuple-element.15.speeds, ...), custom_call_target="tpu_custom_call" | custom-call | flops 2000000 | bytes 1000000 | tf_op jit(solution)/shard_map/pallas_call | solution.py:368
  198.7 50.4 %all_to_all.17.got = f32[16,16,128]{2,1,0:T(8,128)S(1)} all-to-all(f32[16,16,128]{2,1,0:T(8,128)S(1)} %shard_map.97), channel_id=1, replica_groups=mesh['zh'=4,'yc'=4,'zl'=4,'core'=2,'gz'=4] {'zh','yc'}, dimensions={0} | all-to-all | bytes 262144 | tf_op jit(solution)/shard_map/all_to_all | solution.py:455
  249.1 1.4 shard_map.98
  (20 shorter events, 0.1 us)
Async XLA Ops:
  0.0 0.8 copy-start
  0.0 0.7 copy-start.4
  0.8 0.7 copy-start.6
  1.5 0.7 copy-start.7
  2.3 1.1 copy-start.3
  2.4 0.7 copy-start.5
  2.4 0.7 copy-start.8
  3.4 0.9 copy-start.1
  3.4 1.0 copy-start.2
  62.3 25.9 %collective-permute-start = (f32[768,128]{1,0:T(8,128)S(1)}, f32[768,128]{1,0:T(8,128)S(1)}, u32[]{:S(2)}, u32[]{:S(2)}) collective-permute-start(f32[768,128]{1,0:T(8,128)S(1)} %shard_map.92.tile), channel_id=1, source_target_pairs={{128,0},{256,128},{384,256},{385,384},{257,385},{129,257},{1,129},... | collective-permute-start | bytes 1179656 | tf_op jit(solution)/shard_map/ppermute | solution.py:421
  64.8 33.5 %collective-permute-start.1 = (f32[768,128]{1,0:T(8,128)S(1)}, f32[768,128]{1,0:T(8,128)S(1)}, u32[]{:S(2)}, u32[]{:S(2)}) collective-permute-start(f32[768,128]{1,0:T(8,128)S(1)} %shard_map.92.tile), channel_id=1, source_target_pairs={{32,0},{160,128},{288,256},{416,384},{417,385},{289,257},{161,129}... | collective-permute-start | bytes 1179656 | tf_op jit(solution)/shard_map/ppermute | solution.py:421
  88.2 10.1 %collective-permute-start.2 = (f32[768,128]{1,0:T(8,128)S(1)}, f32[768,128]{1,0:T(8,128)S(1)}, u32[]{:S(2)}, u32[]{:S(2)}) collective-permute-start(f32[768,128]{1,0:T(8,128)S(1)} %collective-permute-done.from_z), channel_id=1, source_target_pairs={{32,0},{160,128},{288,256},{416,384},{417,385},{289,257},{161,129}... | collective-permute-start | bytes 1179656 | tf_op jit(solution)/shard_map/ppermute | solution.py:421
  107.6 11.5 %collective-permute-start.3 = (f32[1120,128]{1,0:T(8,128)}, f32[1120,128]{1,0:T(8,128)S(1)}, u32[]{:S(2)}, u32[]{:S(2)}) collective-permute-start(f32[1120,128]{1,0:T(8,128)} %get-tuple-element.14), channel_id=1, source_target_pairs={{0,32},{128,160},{256,288},{384,416},{385,417},{257,289},{129,161}... | collective-permute-start | bytes 1720328 | tf_op jit(solution)/shard_map/ppermute | solution.py:421
  126.7 15.9 %collective-permute-start.4 = (f32[512,128]{1,0:T(8,128)S(1)}, f32[512,128]{1,0:T(8,128)S(1)}, u32[]{:S(2)}, u32[]{:S(2)}) collective-permute-start(f32[512,128]{1,0:T(8,128)S(1)} %get-tuple-element.17), channel_id=1, source_target_pairs={{0,128},{128,256},{256,384},{384,385},{385,257},{257,129},{129,1},... | collective-permute-start | bytes 786440 | tf_op jit(solution)/shard_map/ppermute | solution.py:421
  136.5 38.3 %collective-permute-start.5 = (f32[768,128]{1,0:T(8,128)S(1)}, f32[768,128]{1,0:T(8,128)S(1)}, u32[]{:S(2)}, u32[]{:S(2)}) collective-permute-start(f32[768,128]{1,0:T(8,128)S(1)} %get-tuple-element.16.tile), channel_id=1, source_target_pairs={{32,0},{160,128},{288,256},{416,384},{417,385},{289,257},{161,129}... | collective-permute-start | bytes 1179656 | tf_op jit(solution)/shard_map/ppermute | solution.py:421
  142.6 32.2 %collective-permute-start.6 = (f32[512,128]{1,0:T(8,128)S(1)}, f32[512,128]{1,0:T(8,128)S(1)}, u32[]{:S(2)}, u32[]{:S(2)}) collective-permute-start(f32[512,128]{1,0:T(8,128)S(1)} %collective-permute-done.4.from_z), channel_id=1, source_target_pairs={{32,0},{160,128},{288,256},{416,384},{417,385},{289,257},{161,129}... | collective-permute-start | bytes 786440 | tf_op jit(solution)/shard_map/ppermute | solution.py:421
  144.5 30.2 %collective-permute-start.7 = (f32[16,16,128]{2,1,0:T(8,128)S(1)}, f32[16,16,128]{2,1,0:T(8,128)S(1)}, u32[]{:S(2)}, u32[]{:S(2)}) collective-permute-start(f32[16,16,128]{2,1,0:T(8,128)S(1)} %get-tuple-element.18), channel_id=1, source_target_pairs={{0,128},{128,256},{256,384},{384,385},{385,257},{257,129},{129,1},... | collective-permute-start | bytes 393224 | tf_op jit(solution)/shard_map/ppermute | solution.py:421
  182.7 8.7 %collective-permute-start.8 = (f32[800,128]{1,0:T(8,128)S(1)}, f32[800,128]{1,0:T(8,128)S(1)}, u32[]{:S(2)}, u32[]{:S(2)}) collective-permute-start(f32[800,128]{1,0:T(8,128)S(1)} %get-tuple-element.20), channel_id=1, source_target_pairs={{0,32},{128,160},{256,288},{384,416},{385,417},{257,289},{129,161}... | collective-permute-start | bytes 1228808 | tf_op jit(solution)/shard_map/ppermute | solution.py:421

commit v2 on v1

--- a/solution.py
+++ b/solution.py
@@ -15,7 +15,7 @@
 TY, TZ, KS = 16, 32, 8
 PAIRS, WZ, Z0 = 16, 96, 24
 UNROLL = 2
-FIELD_ROWS, MSG_ROWS = 48, 88
+FIELD_ROWS, MSG_ROWS = 48, 72
 
 
 def linear(zh, yc, zl, core, gz):
@@ -31,7 +31,7 @@
                     for gz in range(4):
                         gy = zl * 2 + core
                         ty = gy * 4 + ((yc - zl) % 4 if core == 0 else (zl - yc) % 4)
-                        tz = gz * 4 + (zh if (gz + core) % 2 == 0 else 3 - zh)
+                        tz = gz * 4 + (zh if gz % 2 == 0 else 3 - zh)
                         table[ty, tz] = linear(zh, yc, zl, core, gz)
     return table
 
@@ -79,7 +79,7 @@
         out[target, FIELD_ROWS:MSG_ROWS, :] = rows
 
 
-def unpack_kernel(got, tile):
+def unpack_kernel(got, tile, near, far):
     low = low_lanes(128)
     solids = []
     for j in range(4):
@@ -94,6 +94,9 @@
         tile[512 + 128 * j : 640 + 128 * j, :] = jnp.where(
             low, solids[j], pltpu.roll(solids[j + 2], 64, 1)
         )
+    for y in range(24):
+        near[y * 16 : y * 16 + 16, :] = tile[y * 32 : y * 32 + 16, :]
+        far[y * 16 : y * 16 + 16, :] = tile[y * 32 + 16 : y * 32 + 32, :]
 
 
 def source_kernel(flags, got, out):
@@ -101,32 +104,41 @@
 
     @pl.when(flags[0] == 1)
     def _():
-        def shard(src, total):
+        offset = lax.broadcasted_iota(jnp.int32, (8, 512), 0) // 4
+
+        def shard(src, totals):
             terms = jnp.concatenate(
-                [got[src, FIELD_ROWS + 8 * j : FIELD_ROWS + 8 * j + 8, :] for j in range(4)], axis=1
+                [got[src, FIELD_ROWS + 4 * j : FIELD_ROWS + 4 * j + 4, :] for j in range(4)], axis=1
             )
-            cell = jnp.concatenate([got[src, 80 + j : 81 + j, :] for j in range(4)], axis=1)
+            terms = jnp.concatenate([terms, terms], axis=0)
+            cell = jnp.concatenate([got[src, 64 + j : 65 + j, :] for j in range(4)], axis=1)
             cell = cell.astype(jnp.int32)
             cell_x = cell >> 9
-            cell_y = (cell & 511) - flags[1]
             upper = terms.astype(jnp.bfloat16).astype(F32)
             lower = terms - upper
             at_x = (lax.broadcasted_iota(jnp.int32, (64, 512), 0) == cell_x).astype(F32)
             at_x = at_x.astype(jnp.bfloat16)
-            here = [jnp.broadcast_to(cell_y, (8, 512)) == y for y in range(2 * PAIRS)]
-            for part in (upper, lower):
-                rows = jnp.concatenate([jnp.where(h, part, 0.0) for h in here], axis=0)
-                total = total + lax.dot_general(
-                    rows.astype(jnp.bfloat16),
-                    at_x,
-                    (((1,), (1,)), ((), ())),
-                    preferred_element_type=F32,
-                )
-            return total
-
-        total = lax.fori_loop(0, 16, shard, jnp.zeros((PAIRS * 16, 64), F32))
-        total = jnp.concatenate([total[: PAIRS * 8], total[PAIRS * 8 :]], axis=1)
-        out[0] = total.reshape(PAIRS, 8, 128)
+            results = []
+            for window in range(2):
+                cell_y = jnp.broadcast_to((cell & 511) - flags[1 + window], (8, 512)) - offset
+                here = [cell_y == 2 * j for j in range(PAIRS)]
+                total = totals[window]
+                for part in (upper, lower):
+                    rows = jnp.concatenate([jnp.where(h, part, 0.0) for h in here], axis=0)
+                    total = total + lax.dot_general(
+                        rows.astype(jnp.bfloat16),
+                        at_x,
+                        (((1,), (1,)), ((), ())),
+                        preferred_element_type=F32,
+                    )
+                results.append(total)
+            return tuple(results)
+
+        zero = jnp.zeros((PAIRS * 8, 64), F32)
+        totals = lax.fori_loop(0, 16, shard, (zero, zero))
+        for window in range(2):
+            total = totals[window]
+            out[4 * window] = jnp.concatenate([total[: PAIRS * 4], total[PAIRS * 4 :]], axis=1)
 
 
 def swap(rows):
@@ -205,7 +217,7 @@
                 new = m[i, at : at + 8, :] * c - old[i + 1, at : at + 8, :]
                 new = new + k[i, at : at + 8, :] * around
                 if at == Z0:
-                    new = new + planes[chunk, i, pl.ds(step, 1), :] * top
+                    new = new + planes[(step >> 2) * 4 + chunk, pl.ds(i * 4 + (step & 3), 1), :] * top
                 old[i + 1, at : at + 8, :] = new
             return centre, ahead, later
 
@@ -233,79 +245,7 @@
             ref[i, z_last + Z0 : z_last + Z0 + 8, :] = zero
 
 
-def round_one(tile, from_z, from_y, from_c, planes, state, msg, speeds, sides, a, b, k, m):
-    clear(a, b, 0, 64)
-    for lower, upper, z in ((tile, from_y, 0), (from_z, from_c, TZ)):
-        for y in range(TY):
-            rows = slice(y * TZ, y * TZ + TZ)
-            load_pair(a, b, y, z, lower[rows, :], upper[rows, :])
-        for y in range(8):
-            rows = slice(512 + y * TZ, 512 + y * TZ + TZ)
-            k[y, z + Z0 : z + Z0 + TZ, :] = mix(lower[rows, :], swap(upper[rows, :]))
-            k[y + 8, z + Z0 : z + Z0 + TZ, :] = mix(swap(lower[rows, :]), upper[rows, :])
-    advance(a, b, k, m, planes, 0, 0, 64, opening=True)
-    for i in range(PAIRS):
-        rows = lower_of(a, b, i, 0, 56)
-        state[i * 56 : i * 56 + 56, :] = rows
-        if i >= 8:
-            msg[(i - 8) * 56 : (i - 8) * 56 + 56, :] = rows
-    for i in range(8):
-        rows = upper_of(a, b, i, 0, 56)
-        state[(i + 16) * 56 : (i + 16) * 56 + 56, :] = rows
-        msg[(i + 8) * 56 : (i + 8) * 56 + 56, :] = rows
-    for y in range(4):
-        msg[896 + y * 56 : 952 + y * 56, :] = mix(
-            k[8 + y, Z0 : Z0 + 56, :], swap(k[12 + y, Z0 : Z0 + 56, :])
-        )
-    for i in range(PAIRS):
-        speeds[i] = k[i, Z0 : Z0 + 64, :]
-        sides[i] = k[i, Z0 + 16 : Z0 + 32, :]
-
-
-def load_left(flags, state, from_y, a, b, z, count):
-    for i in range(PAIRS):
-        rows = from_y[i * count : i * count + count, :]
-        if i >= 8:
-            rows = jnp.where(flags[0] == 1, state[(i - 8) * count : (i - 7) * count, :], rows)
-        load_pair(a, b, i, z, rows, state[(i + 8) * count : (i + 9) * count, :])
-
-
-def round_two(flags, state, from_y, planes, speeds, tile, msg, a, b, k, m):
-    clear(a, b, 0, 56)
-    load_left(flags, state, from_y, a, b, 0, 56)
-    for i in range(PAIRS):
-        k[i, Z0 : Z0 + 56, :] = left_speeds(
-            i, lambda y: from_y[896 + y * 56 : 952 + y * 56, :], lambda j: speeds[j, 0:56, :]
-        )
-    advance(a, b, k, m, planes, 1, 0, 56)
-    for y in range(TY):
-        rows = lower_of(a, b, y + 8, 0, 48) if y < 8 else upper_of(a, b, y - 8, 0, 48)
-        tile[y * 48 : y * 48 + 48, :] = rows
-        msg[y * 32 : y * 32 + 32, :] = rows[16:48]
-
-
-def round_three(flags, tile, from_z, from_y, from_c, planes, speeds, sides, state, msg, a, b, k, m):
-    clear(a, b, -16, 48)
-    for y in range(TY):
-        near = []
-        for main, side in ((tile, from_z), (from_y, from_c)):
-            near.append(
-                jnp.where(
-                    flags[0] == 1,
-                    main[y * 48 : y * 48 + 16, :],
-                    side[y * 32 + 16 : y * 32 + 32, :],
-                )
-            )
-        load_pair(
-            a, b, y, -16, from_z[y * 32 : y * 32 + 16, :], from_c[y * 32 : y * 32 + 16, :]
-        )
-        load_pair(a, b, y, 0, *near)
-        load_pair(
-            a, b, y, 16, tile[y * 48 + 16 : y * 48 + 48, :], from_y[y * 48 + 16 : y * 48 + 48, :]
-        )
-        k[y, Z0 - 16 : Z0, :] = sides[y]
-        k[y, Z0 : Z0 + 48, :] = speeds[y, 0:48, :]
-    advance(a, b, k, m, planes, 2, -16, 48)
+def put_out(a, b, state, msg):
     for i in range(PAIRS):
         rows = lower_of(a, b, i, -8, 48)
         state[i * 48 : i * 48 + 48, :] = rows
@@ -315,22 +255,77 @@
         rows = upper_of(a, b, i, -8, 48)
         state[(i + 16) * 48 : (i + 16) * 48 + 48, :] = rows
         msg[(i + 8) * 48 : (i + 8) * 48 + 48, :] = rows
+
+
+def load_right(a, b, tile, from_y, edges, from_c):
+    for y in range(TY):
+        rows = slice(y * TZ, y * TZ + TZ)
+        load_pair(a, b, y, 0, tile[rows, :], from_y[rows, :])
+        for z, first in ((TZ, 0), (-16, edges.shape[0] // 2)):
+            rows = slice(first + y * 16, first + y * 16 + 16)
+            load_pair(a, b, y, z, edges[rows, :], from_c[rows, :])
+
+
+def load_left(flags, state, from_y, a, b):
+    for i in range(PAIRS):
+        rows = from_y[i * 48 : i * 48 + 48, :]
+        if i >= 8:
+            rows = jnp.where(flags[0] == 1, state[(i - 8) * 48 : (i - 7) * 48, :], rows)
+        load_pair(a, b, i, -8, rows, state[(i + 8) * 48 : (i + 9) * 48, :])
+
+
+def load_left_speeds(k, speeds, above):
+    for i in range(PAIRS):
+        k[i, Z0 - 8 : Z0 + 40, :] = left_speeds(
+            i, lambda y: above[768 + y * 48 : 816 + y * 48, :], lambda j: speeds[j, 8:56, :]
+        )
+
+
+def round_one(tile, from_y, edges, from_c, planes, state, msg, speeds, a, b, k, m):
+    clear(a, b, -16, 48)
+    load_right(a, b, tile, from_y, edges, from_c)
+    for lower, upper, first, z, count in (
+        (tile, from_y, 512, 0, TZ), (edges, from_c, 256, TZ, 16), (edges, from_c, 640, -16, 16)
+    ):
+        for y in range(8):
+            rows = slice(first + y * count, first + y * count + count)
+            at = slice(z + Z0, z + Z0 + count)
+            k[y, at, :] = mix(lower[rows, :], swap(upper[rows, :]))
+            k[y + 8, at, :] = mix(swap(lower[rows, :]), upper[rows, :])
+    advance(a, b, k, m, planes, 0, -16, 48, opening=True)
+    put_out(a, b, state, msg)
     for y in range(4):
-        msg[768 + y * 8 : 776 + y * 8, :] = mix(
-            k[8 + y, Z0 - 8 : Z0, :], swap(k[12 + y, Z0 - 8 : Z0, :])
-        )
-
-
-def round_four(flags, state, from_y, planes, speeds, sides, above, out, a, b, k, m):
+        at = slice(Z0 - 8, Z0 + 40)
+        msg[768 + y * 48 : 816 + y * 48, :] = mix(k[8 + y, at, :], swap(k[12 + y, at, :]))
+    for i in range(PAIRS):
+        speeds[i] = k[i, Z0 - 16 : Z0 + 48, :]
+
+
+def round_two(flags, state, from_y, planes, speeds, tile, near, far, a, b, k, m):
     clear(a, b, -8, 40)
-    load_left(flags, state, from_y, a, b, -8, 48)
+    load_left(flags, state, from_y, a, b)
+    load_left_speeds(k, speeds, from_y)
+    advance(a, b, k, m, planes, 1, -8, 40)
+    for y in range(TY):
+        rows = lower_of(a, b, y + 8, 0, 32) if y < 8 else upper_of(a, b, y - 8, 0, 32)
+        tile[y * 32 : y * 32 + 32, :] = rows
+        near[y * 16 : y * 16 + 16, :] = rows[:16]
+        far[y * 16 : y * 16 + 16, :] = rows[16:]
+
+
+def round_three(tile, from_y, edges, from_c, planes, speeds, state, msg, a, b, k, m):
+    clear(a, b, -16, 48)
+    load_right(a, b, tile, from_y, edges, from_c)
     for i in range(PAIRS):
-        k[i, Z0 - 8 : Z0, :] = left_speeds(
-            i, lambda y: from_y[768 + y * 8 : 776 + y * 8, :], lambda j: sides[j, 8:16, :]
-        )
-        k[i, Z0 : Z0 + 40, :] = left_speeds(
-            i, lambda y: above[896 + y * 56 : 936 + y * 56, :], lambda j: speeds[j, 0:40, :]
-        )
+        k[i, Z0 - 16 : Z0 + 48, :] = speeds[i]
+    advance(a, b, k, m, planes, 2, -16, 48)
+    put_out(a, b, state, msg)
+
+
+def round_four(flags, state, from_y, planes, speeds, above, out, a, b, k, m):
+    clear(a, b, -8, 40)
+    load_left(flags, state, from_y, a, b)
+    load_left_speeds(k, speeds, above)
     advance(a, b, k, m, planes, 3, -8, 40)
     for j in range(4):
         first = 4 * j + 9 if j < 2 else 4 * j - 7
@@ -393,9 +388,8 @@
 ):
     zh, yc, zl, core, gz = (lax.axis_index(a) for a in AXES)
     gy = zl * 2 + core
-    flip_z = (gz + core) % 2
+    flip_z = gz % 2
     ty = gy * 4 + jnp.where(core == 0, yc - zl, zl - yc) % 4
-    tz = gz * 4 + zh + flip_z * (3 - 2 * zh)
     place = jnp.stack([zl, core, flip_z]).astype(jnp.int32)
 
     roof = jnp.repeat(jnp.repeat(obstacle_top, 2, axis=0), 2, axis=1)[:, :, None]
@@ -406,9 +400,9 @@
 
     classes = weight_class[:, None] == jnp.arange(16, dtype=jnp.int32)[None, :]
     weights = jnp.sum(jnp.where(classes, weight_table[None, :], 0.0), axis=1)
-    own = lax.dynamic_slice_in_dim(traces, 24 - 8 * gz, 8, axis=1)[:, ::-1]
+    own = lax.dynamic_slice_in_dim(traces, 28 - 8 * gz - 4 * core, 4, axis=1)[:, ::-1]
     terms = weights[:, None] * own.astype(F32)
-    terms = terms.reshape(4, 128, 8).transpose(0, 2, 1).reshape(32, 128)
+    terms = terms.reshape(4, 128, 4).transpose(0, 2, 1).reshape(16, 128)
     cells = receiver_cell.astype(F32).reshape(4, 128)
     receivers = jnp.concatenate([terms, cells, jnp.zeros((4, 128), F32)], axis=0)
 
@@ -421,36 +415,42 @@
         return lax.ppermute(array, AXES, pairs_along(dy, dz))
 
 
-    (tile,) = call(unpack_kernel, [(768, 128)], got)
+    def around(near, far):
+        after = moved(near, 0, 1)
+        before = moved(far, 0, -1)
+        edges = jnp.concatenate([after, before], axis=0)
+        return edges, moved(edges, 1, 0)
+
+    tile, near, far = call(unpack_kernel, [(768, 128), (384, 128), (384, 128)], got)
     from_y = moved(tile, 1, 0)
-    from_z = moved(tile, 0, 1)
-    works = jnp.stack([(zh == 3 * core), ty * 16 - 8 * (gz % 2)]).astype(jnp.int32)
-    (planes,) = call(source_kernel, [(4, PAIRS, 8, 128)], got, flags=works, cost=20_000_000)
-    planes = lax.all_to_all(planes, "gz", 0, 0, tiled=True)
-    from_c = moved(from_z, 1, 0)
+    firsts = [
+        zl * 128 - 8 * (gz % 2) + 16 * ((yc - zl) % 4),
+        zl * 128 - 8 * (gz % 2) + 64 + 16 * ((zl - yc) % 4),
+    ]
+    works = jnp.stack([zh == 0] + firsts).astype(jnp.int32)
+    (planes,) = call(source_kernel, [(8, PAIRS * 4, 128)], got, flags=works, cost=20_000_000)
+    planes = lax.all_to_all(planes, ("core", "gz"), 0, 0, tiled=True)
+    edges, from_c = around(near, far)
     first_y = (ty == 0).astype(jnp.int32)[None]
-    first_z = (tz == 0).astype(jnp.int32)[None]
-
-    state, msg, speeds, sides = call(
-        round_one, [(1344, 128), (1120, 128), (PAIRS, 64, 128), (PAIRS, 16, 128)],
-        tile, from_z, from_y, from_c, planes, scratch=True,
+
+    state, msg, speeds = call(
+        round_one, [(1152, 128), (960, 128), (PAIRS, 64, 128)],
+        tile, from_y, edges, from_c, planes, scratch=True,
     )
     above = moved(msg, -1, 0)
-    sides = moved(sides, 0, -1)
-    tile, msg = call(
-        round_two, [(768, 128), (512, 128)],
+    tile, near, far = call(
+        round_two, [(512, 128), (256, 128), (256, 128)],
         state, above, planes, speeds, flags=first_y, scratch=True,
     )
     from_y = moved(tile, 1, 0)
-    from_z = moved(msg, 0, -1)
-    from_c = moved(from_z, 1, 0)
+    edges, from_c = around(near, far)
     state, msg = call(
-        round_three, [(1152, 128), (800, 128)],
-        tile, from_z, from_y, from_c, planes, speeds, sides, flags=first_z, scratch=True,
+        round_three, [(1152, 128), (768, 128)],
+        tile, from_y, edges, from_c, planes, speeds, scratch=True,
     )
     (out,) = call(
         round_four, [(16, 16, 128)],
-        state, moved(msg, -1, 0), planes, speeds, sides, above, flags=first_y, scratch=True,
+        state, moved(msg, -1, 0), planes, speeds, above, flags=first_y, scratch=True,
     )
     out = lax.all_to_all(out, ("zh", "yc"), 0, 0, tiled=True)
     (wavefield,) = call(deliver_kernel, [(4, 64, 128)], out, flags=place)

time: 251 us -> 208 us (0.83)
  the two profiles are of different devices: /device:TPU:71 before, /device:TPU:64 now
where the time goes in v2:
time: 208 us; the launch traced here: 207 us
  blocking collectives  90.5 us (44%)
  Pallas kernels  39.6 us (19%)
  starting transfers between devices  39 us (19%)
  waiting for transfers between devices  33.2 us (16%)
  local copies, waits for them, and re-layouts  3.96 us (2%)
    all_to_all x1, blocking collectives, local(): got = lax.all_to_all(packed, ('zh', 'yc'), 0, 0, tiled=True)  53.6 us
    pallas_call x8, Pallas kernels, call(): pl.pallas_call(kernel, out_shape=shapes, in_specs=specs, out_specs=[VM] *...  39.6 us
    ppermute x10, starting transfers between devices, moved(): return lax.ppermute(array, AXES, pairs_along(dy, dz))  39 us
    ppermute x10, waiting for transfers between devices, moved(): return lax.ppermute(array, AXES, pairs_along(dy, dz))  33.2 us
    all_to_all x1, blocking collectives, local(): out = lax.all_to_all(out, ('zh', 'yc'), 0, 0, tiled=True)  26 us
    all_to_all x1, blocking collectives, local(): planes = lax.all_to_all(planes, ('core', 'gz'), 0, 0, tiled=True)  11 us
  transfers between devices with their start and end apart: 10, of which 6 were waited for; matrix products, arithmetic and copies ran while one was open for 0% of the time, Pallas kernels for 3%

profile of v2, /device:TPU:64, one launch (start us, length us, event | category | flops | bytes accessed | tf_op | source)
XLA Modules:
  0.0 207.0 jit_solution(18017964721715960915)
XLA Ops:
  0.0 0.7 copy-done.4
  0.7 0.1 copy-done
  0.8 0.1 rev.3
  0.9 0.5 copy-done.6
  1.5 0.1 copy.18
  1.6 0.6 copy-done.7
  2.1 0.1 copy.16
  2.3 0.0 copy-start.3
  2.3 0.1 copy.17
  2.4 0.1 copy.19
  2.5 0.1 pad.5.clone
  2.5 0.6 copy-done.5
  3.1 0.1 select_reduce_fusion
  3.2 0.1 pad_add_fusion.flags
  3.3 0.1 maximum_maximum_fusion.receivers
  3.4 0.1 and_select_fusion.speed
  3.5 0.8 copy-done.1
  4.3 0.1 copy-done.2
  4.4 0.9 shard_map.91
  5.3 53.6 %all_to_all.15.got = f32[16,72,128]{2,1,0:T(8,128)S(1)} all-to-all(f32[16,72,128]{2,1,0:T(8,128)S(1)} %shard_map.91), channel_id=1, replica_groups=mesh['zh'=4,'yc'=4,'zl'=4,'core'=2,'gz'=4] {'zh','yc'}, dimensions={0} | all-to-all | bytes 1179648 | tf_op jit(solution)/shard_map/all_to_all | solution.py:412
  58.9 0.3 shard_map.92
  59.2 1.3 collective-permute-start.1
  60.5 8.5 %collective-permute-start.2 = (f32[384,128]{1,0:T(8,128)S(1)}, f32[384,128]{1,0:T(8,128)S(1)}, u32[]{:S(2)}, u32[]{:S(2)}) collective-permute-start(f32[384,128]{1,0:T(8,128)S(1)} %get-tuple-element.18), channel_id=1, source_target_pairs={{0,128},{128,256},{256,384},{384,385},{385,257},{257,129},{129,1},... | collective-permute-start | bytes 589832 | tf_op jit(solution)/shard_map/ppermute | solution.py:415
  68.9 2.8 %collective-permute-start = (f32[768,128]{1,0:T(8,128)S(1)}, f32[768,128]{1,0:T(8,128)S(1)}, u32[]{:S(2)}, u32[]{:S(2)}) collective-permute-start(f32[768,128]{1,0:T(8,128)S(1)} %get-tuple-element.16.tile), channel_id=1, source_target_pairs={{32,0},{160,128},{288,256},{416,384},{417,385},{289,257},{161,129}... | collective-permute-start | bytes 1179656 | tf_op jit(solution)/shard_map/ppermute | solution.py:415
  71.7 0.9 collective-permute-done.1
  72.6 3.5 %collective-permute-done.2 = f32[384,128]{1,0:T(8,128)S(1)} collective-permute-done((f32[384,128]{1,0:T(8,128)S(1)}, f32[384,128]{1,0:T(8,128)S(1)}, u32[]{:S(2)}, u32[]{:S(2)}) %collective-permute-start.2) | collective-permute-done | bytes 196640 | tf_op jit(solution)/shard_map/ppermute | solution.py:415
  76.2 7.7 %collective-permute-start.3 = (f32[768,128]{1,0:T(8,128)S(1)}, f32[768,128]{1,0:T(8,128)S(1)}, u32[]{:S(2)}, u32[]{:S(2)}) collective-permute-start(f32[768,128]{1,0:T(8,128)S(1)} %constant_dynamic-update-slice_fusion.edges), channel_id=1, source_target_pairs={{32,0},{160,128},{288,256},{416,384},{417,385},{289,257},{161,129}... | collective-permute-start | bytes 1179656 | tf_op jit(solution)/shard_map/ppermute | solution.py:415
  83.9 0.1 pad_add_fusion.1.flags
  84.0 5.4 %shard_map.93 = f32[8,64,128]{2,1,0:T(8,128)S(1)} custom-call(s32[3]{0:T(128)S(1)} %pad_add_fusion.1.flags, f32[16,72,128]{2,1,0:T(8,128)S(1)} %all_to_all.15.got), custom_call_target="tpu_custom_call" | custom-call | flops 20000000 | bytes 1000000 | tf_op jit(solution)/shard_map/pallas_call | solution.py:363
  89.4 11.0 %all_to_all.16.planes = f32[8,64,128]{2,1,0:T(8,128)S(1)} all-to-all(f32[8,64,128]{2,1,0:T(8,128)S(1)} %shard_map.93), channel_id=1, replica_groups=mesh['zh'=4,'yc'=4,'zl'=4,'core'=2,'gz'=4] {'core','gz'}, dimensions={0} | all-to-all | bytes 524288 | tf_op jit(solution)/shard_map/all_to_all | solution.py:432
  100.3 0.0 collective-permute-done.3.from_c
  100.3 9.2 %shard_map.94 = (f32[1152,128]{1,0:T(8,128)S(1)}, f32[960,128]{1,0:T(8,128)}, f32[16,64,128]{2,1,0:T(8,128)S(1)}) custom-call(f32[768,128]{1,0:T(8,128)S(1)} %get-tuple-element.16.tile, f32[768,128]{1,0:T(8,128)S(1)} %collective-permute-done.from_y, f32[768,128]{1,0:T(8,128)S(1)} %constant_dynamic-update-slice_fusion.edges, ...), custom_call_target="tpu_custom_call" | custom-call | flops 2000000 | bytes 1000000 | tf_op jit(solution)/shard_map/pallas_call | solution.py:363
  109.6 1.9 collective-permute-start.4
  111.5 10.2 %collective-permute-done.4.from_y.above = f32[960,128]{1,0:T(8,128)S(1)} collective-permute-done((f32[960,128]{1,0:T(8,128)}, f32[960,128]{1,0:T(8,128)S(1)}, u32[]{:S(2)}, u32[]{:S(2)}) %collective-permute-start.4) | collective-permute-done | bytes 491552 | tf_op jit(solution)/shard_map/ppermute | solution.py:415
  121.7 7.2 %shard_map.95 = (f32[512,128]{1,0:T(8,128)S(1)}, f32[256,128]{1,0:T(8,128)S(1)}, f32[256,128]{1,0:T(8,128)S(1)}) custom-call(s32[1]{0:T(128)} %bitcast.3.flags, f32[1152,128]{1,0:T(8,128)S(1)} %get-tuple-element.19.state, f32[960,128]{1,0:T(8,128)S(1)} %collective-permute-done.4.from_y.above, f32[8,64,128]{2,1,0:T(8,128)S(1)} %all_to_all.16.planes, ...), custom_call_target="tpu_custom_call" | custom-call | flops 2000000 | bytes 1000000 | tf_op jit(solution)/shard_map/pallas_call | solution.py:363
  128.9 1.3 collective-permute-start.6
  130.2 8.5 %collective-permute-start.7 = (f32[256,128]{1,0:T(8,128)S(1)}, f32[256,128]{1,0:T(8,128)S(1)}, u32[]{:S(2)}, u32[]{:S(2)}) collective-permute-start(f32[256,128]{1,0:T(8,128)S(1)} %get-tuple-element.24), channel_id=1, source_target_pairs={{0,128},{128,256},{256,384},{384,385},{385,257},{257,129},{129,1},... | collective-permute-start | bytes 393224 | tf_op jit(solution)/shard_map/ppermute | solution.py:415
  138.7 1.9 collective-permute-start.5
  140.6 4.6 %collective-permute-done.6 = f32[256,128]{1,0:T(8,128)S(1)} collective-permute-done((f32[256,128]{1,0:T(8,128)S(1)}, f32[256,128]{1,0:T(8,128)S(1)}, u32[]{:S(2)}, u32[]{:S(2)}) %collective-permute-start.6) | collective-permute-done | bytes 131104 | tf_op jit(solution)/shard_map/ppermute | solution.py:415
  145.3 3.2 %collective-permute-start.8 = (f32[512,128]{1,0:T(8,128)S(1)}, f32[512,128]{1,0:T(8,128)S(1)}, u32[]{:S(2)}, u32[]{:S(2)}) collective-permute-start(f32[512,128]{1,0:T(8,128)S(1)} %constant_dynamic-update-slice_fusion.2.edges), channel_id=1, source_target_pairs={{32,0},{160,128},{288,256},{416,384},{417,385},{289,257},{161,129}... | collective-permute-start | bytes 786440 | tf_op jit(solution)/shard_map/ppermute | solution.py:415
  148.5 0.0 collective-permute-done.5.from_y
  148.5 5.0 %collective-permute-done.8.from_c = f32[512,128]{1,0:T(8,128)S(1)} collective-permute-done((f32[512,128]{1,0:T(8,128)S(1)}, f32[512,128]{1,0:T(8,128)S(1)}, u32[]{:S(2)}, u32[]{:S(2)}) %collective-permute-start.8) | collective-permute-done | bytes 262176 | tf_op jit(solution)/shard_map/ppermute | solution.py:415
  153.6 8.0 %shard_map.96 = (f32[1152,128]{1,0:T(8,128)S(1)}, f32[768,128]{1,0:T(8,128)S(1)}) custom-call(f32[512,128]{1,0:T(8,128)S(1)} %get-tuple-element.22.tile, f32[512,128]{1,0:T(8,128)S(1)} %collective-permute-done.5.from_y, f32[512,128]{1,0:T(8,128)S(1)} %constant_dynamic-update-slice_fusion.2.edges, f32[512,128]{1,0:T(8,128)S(1)} %collective-permute-done.8.from_c, ...), custom_call_target="tpu_custom_call" | custom-call | flops 2000000 | bytes 1000000 | tf_op jit(solution)/shard_map/pallas_call | solution.py:363
  161.6 1.9 collective-permute-start.9
  163.5 8.9 %collective-permute-done.9.from_y = f32[768,128]{1,0:T(8,128)S(1)} collective-permute-done((f32[768,128]{1,0:T(8,128)S(1)}, f32[768,128]{1,0:T(8,128)S(1)}, u32[]{:S(2)}, u32[]{:S(2)}) %collective-permute-start.9) | collective-permute-done | bytes 393248 | tf_op jit(solution)/shard_map/ppermute | solution.py:415
  172.4 7.2 %shard_map.97 = f32[16,16,128]{2,1,0:T(8,128)S(1)} custom-call(s32[1]{0:T(128)} %bitcast.3.flags, f32[1152,128]{1,0:T(8,128)S(1)} %get-tuple-element.25.state, f32[768,128]{1,0:T(8,128)S(1)} %collective-permute-done.9.from_y, f32[8,64,128]{2,1,0:T(8,128)S(1)} %all_to_all.16.planes, f32[16,64,128]{2,1,0:T(8,128)S(1)} %get-tuple-element.21.speeds, ...), custom_call_target="tpu_custom_call" | custom-call | flops 2000000 | bytes 1000000 | tf_op jit(solution)/shard_map/pallas_call | solution.py:363
  179.7 26.0 %all_to_all.17.got = f32[16,16,128]{2,1,0:T(8,128)S(1)} all-to-all(f32[16,16,128]{2,1,0:T(8,128)S(1)} %shard_map.97), channel_id=1, replica_groups=mesh['zh'=4,'yc'=4,'zl'=4,'core'=2,'gz'=4] {'zh','yc'}, dimensions={0} | all-to-all | bytes 262144 | tf_op jit(solution)/shard_map/all_to_all | solution.py:455
  205.7 1.4 shard_map.98
  (26 shorter events, 0.1 us)
Async XLA Ops:
  0.0 0.8 copy-start
  0.0 0.7 copy-start.4
  0.8 0.7 copy-start.6
  1.5 0.7 copy-start.7
  2.3 1.1 copy-start.3
  2.5 0.7 copy-start.5
  2.5 0.7 copy-start.8
  3.4 0.9 copy-start.1
  3.4 1.0 copy-start.2
  59.2 13.4 %collective-permute-start.1 = (f32[384,128]{1,0:T(8,128)S(1)}, f32[384,128]{1,0:T(8,128)S(1)}, u32[]{:S(2)}, u32[]{:S(2)}) collective-permute-start(f32[384,128]{1,0:T(8,128)S(1)} %get-tuple-element.17), channel_id=1, source_target_pairs={{128,0},{256,128},{384,256},{385,384},{257,385},{129,257},{1,129},... | collective-permute-start | bytes 589832 | tf_op jit(solution)/shard_map/ppermute | solution.py:415
  60.5 15.7 %collective-permute-start.2 = (f32[384,128]{1,0:T(8,128)S(1)}, f32[384,128]{1,0:T(8,128)S(1)}, u32[]{:S(2)}, u32[]{:S(2)}) collective-permute-start(f32[384,128]{1,0:T(8,128)S(1)} %get-tuple-element.18), channel_id=1, source_target_pairs={{0,128},{128,256},{256,384},{384,385},{385,257},{257,129},{129,1},... | collective-permute-start | bytes 589832 | tf_op jit(solution)/shard_map/ppermute | solution.py:415
  68.9 31.4 %collective-permute-start = (f32[768,128]{1,0:T(8,128)S(1)}, f32[768,128]{1,0:T(8,128)S(1)}, u32[]{:S(2)}, u32[]{:S(2)}) collective-permute-start(f32[768,128]{1,0:T(8,128)S(1)} %get-tuple-element.16.tile), channel_id=1, source_target_pairs={{32,0},{160,128},{288,256},{416,384},{417,385},{289,257},{161,129}... | collective-permute-start | bytes 1179656 | tf_op jit(solution)/shard_map/ppermute | solution.py:415
  76.2 24.2 %collective-permute-start.3 = (f32[768,128]{1,0:T(8,128)S(1)}, f32[768,128]{1,0:T(8,128)S(1)}, u32[]{:S(2)}, u32[]{:S(2)}) collective-permute-start(f32[768,128]{1,0:T(8,128)S(1)} %constant_dynamic-update-slice_fusion.edges), channel_id=1, source_target_pairs={{32,0},{160,128},{288,256},{416,384},{417,385},{289,257},{161,129}... | collective-permute-start | bytes 1179656 | tf_op jit(solution)/shard_map/ppermute | solution.py:415
  109.6 12.1 %collective-permute-start.4 = (f32[960,128]{1,0:T(8,128)}, f32[960,128]{1,0:T(8,128)S(1)}, u32[]{:S(2)}, u32[]{:S(2)}) collective-permute-start(f32[960,128]{1,0:T(8,128)} %get-tuple-element.20), channel_id=1, source_target_pairs={{0,32},{128,160},{256,288},{384,416},{385,417},{257,289},{129,161}... | collective-permute-start | bytes 1474568 | tf_op jit(solution)/shard_map/ppermute | solution.py:415
  128.9 16.3 %collective-permute-start.6 = (f32[256,128]{1,0:T(8,128)S(1)}, f32[256,128]{1,0:T(8,128)S(1)}, u32[]{:S(2)}, u32[]{:S(2)}) collective-permute-start(f32[256,128]{1,0:T(8,128)S(1)} %get-tuple-element.23), channel_id=1, source_target_pairs={{128,0},{256,128},{384,256},{385,384},{257,385},{129,257},{1,129},... | collective-permute-start | bytes 393224 | tf_op jit(solution)/shard_map/ppermute | solution.py:415
  130.2 15.0 %collective-permute-start.7 = (f32[256,128]{1,0:T(8,128)S(1)}, f32[256,128]{1,0:T(8,128)S(1)}, u32[]{:S(2)}, u32[]{:S(2)}) collective-permute-start(f32[256,128]{1,0:T(8,128)S(1)} %get-tuple-element.24), channel_id=1, source_target_pairs={{0,128},{128,256},{256,384},{384,385},{385,257},{257,129},{129,1},... | collective-permute-start | bytes 393224 | tf_op jit(solution)/shard_map/ppermute | solution.py:415
  138.7 9.8 %collective-permute-start.5 = (f32[512,128]{1,0:T(8,128)S(1)}, f32[512,128]{1,0:T(8,128)S(1)}, u32[]{:S(2)}, u32[]{:S(2)}) collective-permute-start(f32[512,128]{1,0:T(8,128)S(1)} %get-tuple-element.22.tile), channel_id=1, source_target_pairs={{32,0},{160,128},{288,256},{416,384},{417,385},{289,257},{161,129}... | collective-permute-start | bytes 786440 | tf_op jit(solution)/shard_map/ppermute | solution.py:415
  145.3 8.3 %collective-permute-start.8 = (f32[512,128]{1,0:T(8,128)S(1)}, f32[512,128]{1,0:T(8,128)S(1)}, u32[]{:S(2)}, u32[]{:S(2)}) collective-permute-start(f32[512,128]{1,0:T(8,128)S(1)} %constant_dynamic-update-slice_fusion.2.edges), channel_id=1, source_target_pairs={{32,0},{160,128},{288,256},{416,384},{417,385},{289,257},{161,129}... | collective-permute-start | bytes 786440 | tf_op jit(solution)/shard_map/ppermute | solution.py:415
  161.6 10.9 %collective-permute-start.9 = (f32[768,128]{1,0:T(8,128)S(1)}, f32[768,128]{1,0:T(8,128)S(1)}, u32[]{:S(2)}, u32[]{:S(2)}) collective-permute-start(f32[768,128]{1,0:T(8,128)S(1)} %get-tuple-element.26), channel_id=1, source_target_pairs={{0,32},{128,160},{256,288},{384,416},{385,417},{257,289},{129,161}... | collective-permute-start | bytes 1179656 | tf_op jit(solution)/shard_map/ppermute | solution.py:415

commit v3 on v2

v3 whole, which is shorter than its diff:
```python
import jax
import jax.numpy as jnp
from jax import lax
from jax.experimental import pallas as pl
from jax.experimental.pallas import tpu as pltpu
from jax.sharding import Mesh, PartitionSpec as P


AXES = ("zh", "yc", "zl", "core", "gz")
SIZES = (4, 4, 4, 2, 4)
F32 = jnp.float32
VM = pl.BlockSpec(memory_space=pltpu.VMEM)
SM = pl.BlockSpec(memory_space=pltpu.SMEM)

TZ, KS = 32, 8
ROWS, WZ, Z0 = 16, 80, 24
FIELD_ROWS, MSG_ROWS = 48, 72


def linear(zh, yc, zl, core, gz):
    return (((zh * 4 + yc) * 4 + zl) * 2 + core) * 4 + gz


def tile_devices():
    table = {}
    for zh in range(4):
        for yc in range(4):
            for zl in range(4):
                for core in range(2):
                    for gz in range(4):
                        gy = zl * 2 + core
                        ty = gy * 4 + ((yc - zl) % 4 if core == 0 else (zl - yc) % 4)
                        tz = gz * 4 + (zh if gz % 2 == 0 else 3 - zh)
                        table[ty, tz] = linear(zh, yc, zl, core, gz)
    return table


def pairs_along(dy, dz):
    table = tile_devices()
    return [
        (table[ty + dy, tz + dz], table[ty, tz])
        for (ty, tz) in sorted(table)
        if (ty + dy, tz + dz) in table
    ]


def source_of(flags, ys, zs):
    zh = zs + flags[2] * (3 - 2 * zs)
    yc = (flags[0] + ys - 2 * flags[1] * ys) & 3
    return zh * 4 + yc


def lane_group(rows):
    return lax.broadcasted_iota(jnp.int32, (rows, 128), 1) // 32


def low_lanes(rows):
    return lax.broadcasted_iota(jnp.int32, (rows, 128), 1) < 64


def pack_kernel(flags, now, prev, speed, receivers, out):
    group = lane_group(16)
    for field, ref in enumerate((now, prev, speed)):
        for x in range(4):
            parts = [ref[x, pl.ds(q, 16, stride=4), :] for q in range(4)]
            for zs in range(4):
                piece = None
                for q in range(4):
                    turn = (32 * (q - zs)) % 128
                    moved = parts[q] if turn == 0 else pltpu.roll(parts[q], turn, 1)
                    piece = moved if piece is None else jnp.where(group == q, moved, piece)
                for ys in range(4):
                    target = source_of(flags, ys, zs)
                    first = field * 16 + x * 4
                    out[target, first : first + 4, :] = piece[4 * ys : 4 * ys + 4]
    rows = receivers[...]
    for target in range(16):
        out[target, FIELD_ROWS:MSG_ROWS, :] = rows


def unpack_kernel(got, tile, near, far):
    low = low_lanes(128)
    solids = []
    for p in range(4):
        parts = [
            [got[pl.ds(16 * field + 4 * p + g, 16, stride=MSG_ROWS), :] for g in range(4)]
            for field in range(3)
        ]
        tile[128 * p : 128 * p + 128, :] = jnp.concatenate(parts[0] + parts[1], axis=0).T
        speeds = jnp.concatenate(parts[2], axis=0)
        solids.append(jnp.concatenate([speeds, jnp.zeros_like(speeds)], axis=0).T)
    for j in range(2):
        tile[512 + 128 * j : 640 + 128 * j, :] = jnp.where(
            low, solids[j], pltpu.roll(solids[j + 2], 64, 1)
        )
    for r in range(24):
        near[r * 16 : r * 16 + 16, :] = tile[r * 32 : r * 32 + 16, :]
        far[r * 16 : r * 16 + 16, :] = tile[r * 32 + 16 : r * 32 + 32, :]


def source_kernel(flags, got, out):
    out[...] = jnp.zeros_like(out)

    @pl.when(flags[0] == 1)
    def _():
        offset = lax.broadcasted_iota(jnp.int32, (8, 512), 0) // 4
        lanes = lax.broadcasted_iota(jnp.int32, (128, 512), 0)

        def shard(src, totals):
            base = src * MSG_ROWS
            terms = got[pl.ds(pl.multiple_of(base + FIELD_ROWS, 8), 16), :]
            cell = got[pl.ds(pl.multiple_of(base + 64, 8), 8), :]
            terms = jnp.concatenate([terms[4 * j : 4 * j + 4] for j in range(4)], axis=1)
            terms = jnp.concatenate([terms, terms], axis=0)
            cell = jnp.concatenate([cell[j : j + 1] for j in range(4)], axis=1)
            cell = cell.astype(jnp.int32)
            cell_x = cell >> 9
            upper = terms.astype(jnp.bfloat16).astype(F32)
            lower = terms - upper
            results = []
            for window in range(2):
                cell_y = (cell & 511) - flags[1 + window]
                lane = jnp.where(
                    (cell_y >= 0) & (cell_y < 32), (cell_y >> 2) * 16 + (cell_x >> 2), -1
                )
                at_lane = (lanes == lane).astype(F32).astype(jnp.bfloat16)
                row = jnp.broadcast_to((cell_x & 3) * 4 + (cell_y & 3), (8, 512)) - offset
                here = [row == 2 * j for j in range(ROWS // 2)]
                total = totals[window]
                for part in (upper, lower):
                    rows = jnp.concatenate([jnp.where(h, part, 0.0) for h in here], axis=0)
                    total = total + lax.dot_general(
                        rows.astype(jnp.bfloat16),
                        at_lane,
                        (((1,), (1,)), ((), ())),
                        preferred_element_type=F32,
                    )
                results.append(total)
            return tuple(results)

        zero = jnp.zeros((ROWS * 4, 128), F32)
        totals = lax.fori_loop(0, 16, shard, (zero, zero))
        for window in range(2):
            out[4 * window] = totals[window]


def swap(rows):
    return pltpu.roll(rows, 64, 1)


def mix(lower, upper):
    return jnp.where(low_lanes(lower.shape[0]), lower, upper)


def load_pair(a, b, r, z, lower, upper):
    at = z + Z0
    a[r, at : at + lower.shape[0], :] = mix(lower, swap(upper))
    b[r, at : at + lower.shape[0], :] = mix(swap(lower), upper)


def middle_of(a, b, r, z, count):
    at = slice(z + Z0, z + Z0 + count)
    return mix(pltpu.roll(a[r, at, :], 96, 1), pltpu.roll(b[r, at, :], 32, 1))


def advance(a, b, k, m, planes, chunk, z_first, z_last, opening=False):
    top = (lax.broadcasted_iota(jnp.int32, (8, 128), 0) == 0).astype(F32)
    lane = lax.broadcasted_iota(jnp.int32, (8, 128), 1)
    first_g, first_m, last_m = lane < 16, lane % 16 == 0, lane % 16 == 15
    span = slice(z_first + Z0, z_last + Z0)
    starts = range(z_first + Z0, z_last + Z0, 8)

    def weigh(r, nothing):
        speed = k[r, span, :]
        m[r, span, :] = jnp.where(speed > 0.0, 2.0 - 6.0 * speed, 0.0)
        return nothing

    lax.fori_loop(0, ROWS, weigh, 0)

    def drain(field):
        def row(r, nothing):
            field[r, span, :] = jnp.where(k[r, span, :] > 0.0, field[r, span, :], 0.0)
            return nothing

        lax.fori_loop(0, ROWS, row, 0)

    def one(now, old, step):
        for at in starts:
            here = slice(at, at + 8)
            c = [now[r, here, :] for r in range(ROWS)]
            for i in range(4):
                before = jnp.where(first_m, 0.0, pltpu.roll(c[12 + i], 1, 1))
                after = jnp.where(last_m, 0.0, pltpu.roll(c[i], 127, 1))
                for p in range(4):
                    r = 4 * p + i
                    around = (before if p == 0 else c[r - 4]) + (after if p == 3 else c[r + 4])
                    if i == 0:
                        below = jnp.where(first_g, 0.0, pltpu.roll(c[r + 3], 16, 1))
                    else:
                        below = c[r - 1]
                    above = pltpu.roll(c[r - 3], 112, 1) if i == 3 else c[r + 1]
                    around = around + (below + above)
                    around = around + (now[r, at - 1 : at + 7, :] + now[r, at + 1 : at + 9, :])
                    new = m[r, here, :] * c[r] - old[r, here, :] + k[r, here, :] * around
                    if at == Z0:
                        row = planes[(step >> 2) * 4 + chunk, pl.ds(r * 4 + (step & 3), 1), :]
                        new = new + row * top
                    old[r, here, :] = new

    def two(pair, nothing):
        one(a, b, 2 * pair)
        if opening:
            pl.when(pair == 0)(lambda: drain(a))
        one(b, a, 2 * pair + 1)
        return nothing

    if opening:
        drain(b)
    lax.fori_loop(0, KS // 2, two, 0)


def clear(a, b, z_first, z_last):
    zero = jnp.zeros((8, 128), F32)
    for ref in (a, b):
        for r in range(ROWS):
            ref[r, z_first + Z0 - 8 : z_first + Z0, :] = zero
            ref[r, z_last + Z0 : z_last + Z0 + 8, :] = zero


def put_out(a, b, state, msg):
    at = slice(Z0 - 8, Z0 + 40)
    for r in range(ROWS):
        state[r] = a[r, at, :]
        state[ROWS + r] = b[r, at, :]
        msg[r * 48 : r * 48 + 48, :] = middle_of(a, b, r, -8, 48)


def load_right(a, b, tile, from_y, edges, from_c):
    for r in range(ROWS):
        rows = slice(r * TZ, r * TZ + TZ)
        load_pair(a, b, r, 0, tile[rows, :], from_y[rows, :])
        for z, first in ((TZ, 0), (-16, edges.shape[0] // 2)):
            rows = slice(first + r * 16, first + r * 16 + 16)
            load_pair(a, b, r, z, edges[rows, :], from_c[rows, :])


def load_left(flags, state, from_y, a, b):
    lane = lax.broadcasted_iota(jnp.int32, (48, 128), 1)
    given = lane < 64 - 32 * flags[0]
    at = slice(Z0 - 8, Z0 + 40)
    for r in range(ROWS):
        rows = from_y[r * 48 : r * 48 + 48, :]
        a[r, at, :] = jnp.where(given, rows, pltpu.roll(state[r], 32, 1))
        b[r, at, :] = jnp.where(given, swap(rows), pltpu.roll(state[ROWS + r], 32, 1))


def load_left_speeds(k, speeds, above):
    given = lax.broadcasted_iota(jnp.int32, (48, 128), 1) < 32
    for r in range(ROWS):
        j, p = r % 4, r // 4
        rows = above[768 + j * 48 : 816 + j * 48, :]
        rows = rows if p == 0 else pltpu.roll(rows, 128 - 32 * p, 1)
        k[r, Z0 - 8 : Z0 + 40, :] = jnp.where(given, rows, pltpu.roll(speeds[r, 8:56, :], 32, 1))


def round_one(tile, from_y, edges, from_c, planes, state, msg, speeds, a, b, k, m):
    clear(a, b, -16, 48)
    load_right(a, b, tile, from_y, edges, from_c)
    for lower, upper, first, z, count in (
        (tile, from_y, 512, 0, TZ), (edges, from_c, 256, TZ, 16), (edges, from_c, 640, -16, 16)
    ):
        for r in range(8):
            rows = slice(first + r * count, first + r * count + count)
            at = slice(z + Z0, z + Z0 + count)
            k[r, at, :] = mix(lower[rows, :], swap(upper[rows, :]))
            k[r + 8, at, :] = mix(swap(lower[rows, :]), upper[rows, :])
    advance(a, b, k, m, planes, 0, -16, 48, opening=True)
    put_out(a, b, state, msg)
    group = lane_group(48)
    for j in range(4):
        rows = k[4 + j, Z0 - 8 : Z0 + 40, :]
        for p in (0, 2, 3):
            moved = pltpu.roll(k[4 * p + j, Z0 - 8 : Z0 + 40, :], (32 * p - 32) % 128, 1)
            rows = jnp.where(group == p, moved, rows)
        msg[768 + j * 48 : 816 + j * 48, :] = rows
    for r in range(ROWS):
        speeds[r] = k[r, Z0 - 16 : Z0 + 48, :]


def round_two(flags, state, from_y, planes, speeds, tile, near, far, a, b, k, m):
    clear(a, b, -8, 40)
    load_left(flags, state, from_y, a, b)
    load_left_speeds(k, speeds, from_y)
    advance(a, b, k, m, planes, 1, -8, 40)
    for r in range(ROWS):
        rows = middle_of(a, b, r, 0, 32)
        tile[r * 32 : r * 32 + 32, :] = rows
        near[r * 16 : r * 16 + 16, :] = rows[:16]
        far[r * 16 : r * 16 + 16, :] = rows[16:]


def round_three(tile, from_y, edges, from_c, planes, speeds, state, msg, a, b, k, m):
    clear(a, b, -16, 48)
    load_right(a, b, tile, from_y, edges, from_c)
    for r in range(ROWS):
        k[r, Z0 - 16 : Z0 + 48, :] = speeds[r]
    advance(a, b, k, m, planes, 2, -16, 48)
    put_out(a, b, state, msg)


def round_four(flags, state, from_y, planes, speeds, above, out, a, b, k, m):
    clear(a, b, -8, 40)
    load_left(flags, state, from_y, a, b)
    load_left_speeds(k, speeds, above)
    advance(a, b, k, m, planes, 3, -8, 40)
    for p in range(4):
        turned = jnp.concatenate([a[4 * p + q, Z0 : Z0 + TZ, :] for q in range(4)], axis=0).T
        for g in range(4):
            out[pl.ds(4 * g + p, 16, stride=16), :] = turned[32 + 16 * g : 48 + 16 * g]


def deliver_kernel(flags, got, out):
    group = lane_group(16)
    for x in range(4):
        parts = []
        for zs in range(4):
            rows = [
                got[source_of(flags, ys, zs), pl.ds(x, 4, stride=4), :] for ys in range(4)
            ]
            parts.append(jnp.concatenate(rows, axis=0))
        for q in range(4):
            piece = None
            for zs in range(4):
                turn = (32 * (zs - q)) % 128
                moved = parts[zs] if turn == 0 else pltpu.roll(parts[zs], turn, 1)
                piece = moved if piece is None else jnp.where(group == zs, moved, piece)
            out[x, pl.ds(q, 16, stride=4), :] = piece


def call(kernel, outs, *args, flags=None, scratch=False, cost=2_000_000):
    shapes = [jax.ShapeDtypeStruct(s, F32) for s in outs]
    specs = [VM] * len(args)
    if flags is not None:
        args = (flags,) + args
        specs = [SM] + specs
    return pl.pallas_call(
        kernel,
        out_shape=shapes,
        in_specs=specs,
        out_specs=[VM] * len(outs),
        scratch_shapes=[pltpu.VMEM((ROWS, WZ, 128), F32)] * 4 if scratch else [],
        compiler_params=pltpu.CompilerParams(vmem_limit_bytes=48 * 1024 * 1024),
        cost_estimate=pl.CostEstimate(flops=cost, bytes_accessed=1_000_000, transcendentals=0),
    )(*args)


def local(
    traces,
    receiver_cell,
    weight_class,
    weight_table,
    obstacle_top,
    obstacle_thick,
    courant,
    p_now,
    p_prev,
):
    zh, yc, zl, core, gz = (lax.axis_index(a) for a in AXES)
    gy = zl * 2 + core
    flip_z = gz % 2
    ty = gy * 4 + jnp.where(core == 0, yc - zl, zl - yc) % 4
    place = jnp.stack([zl, core, flip_z]).astype(jnp.int32)

    roof = jnp.repeat(jnp.repeat(obstacle_top, 2, axis=0), 2, axis=1)[:, :, None]
    thickness = jnp.repeat(jnp.repeat(obstacle_thick, 2, axis=0), 2, axis=1)[:, :, None]
    depth = gz * 128 + jnp.arange(128, dtype=jnp.int32)[None, None, :]
    solid = (depth >= roof) & (depth < roof + thickness)
    speed = jnp.where(solid, 0.0, courant)

    classes = weight_class[:, None] == jnp.arange(16, dtype=jnp.int32)[None, :]
    weights = jnp.sum(jnp.where(classes, weight_table[None, :], 0.0), axis=1)
    own = lax.dynamic_slice_in_dim(traces, 28 - 8 * gz - 4 * core, 4, axis=1)[:, ::-1]
    terms = weights[:, None] * own.astype(F32)
    terms = terms.reshape(4, 128, 4).transpose(0, 2, 1).reshape(16, 128)
    cells = receiver_cell.astype(F32).reshape(4, 128)
    receivers = jnp.concatenate([terms, cells, jnp.zeros((4, 128), F32)], axis=0)

    (packed,) = call(
        pack_kernel, [(16, MSG_ROWS, 128)], p_now, p_prev, speed, receivers, flags=place
    )
    got = lax.all_to_all(packed, ("zh", "yc"), 0, 0, tiled=True).reshape(16 * MSG_ROWS, 128)

    def moved(array, dy, dz):
        return lax.ppermute(array, AXES, pairs_along(dy, dz))


    def around(near, far):
        after = moved(near, 0, 1)
        before = moved(far, 0, -1)
        edges = jnp.concatenate([after, before], axis=0)
        return edges, moved(edges, 1, 0)

    tile, near, far = call(unpack_kernel, [(768, 128), (384, 128), (384, 128)], got)
    from_y = moved(tile, 1, 0)
    firsts = [
        zl * 128 - 8 * (gz % 2) + 16 * ((yc - zl) % 4),
        zl * 128 - 8 * (gz % 2) + 64 + 16 * ((zl - yc) % 4),
    ]
    works = jnp.stack([zh == 0] + firsts).astype(jnp.int32)
    (planes,) = call(source_kernel, [(8, ROWS * 4, 128)], got, flags=works, cost=20_000_000)
    planes = lax.all_to_all(planes, ("core", "gz"), 0, 0, tiled=True)
    edges, from_c = around(near, far)
    first_y = (ty == 0).astype(jnp.int32)[None]

    state, msg, speeds = call(
        round_one, [(2 * ROWS, 48, 128), (960, 128), (ROWS, 64, 128)],
        tile, from_y, edges, from_c, planes, scratch=True,
    )
    above = moved(msg, -1, 0)
    tile, near, far = call(
        round_two, [(512, 128), (256, 128), (256, 128)],
        state, above, planes, speeds, flags=first_y, scratch=True,
    )
    from_y = moved(tile, 1, 0)
    edges, from_c = around(near, far)
    state, msg = call(
        round_three, [(2 * ROWS, 48, 128), (768, 128)],
        tile, from_y, edges, from_c, planes, speeds, scratch=True,
    )
    (out,) = call(
        round_four, [(256, 128)],
        state, moved(msg, -1, 0), planes, speeds, above, flags=first_y, scratch=True,
    )
    out = lax.all_to_all(out.reshape(16, 16, 128), ("zh", "yc"), 0, 0, tiled=True)
    (wavefield,) = call(deliver_kernel, [(4, 64, 128)], out, flags=place)
    return wavefield


def solution(mesh):
    fine = Mesh(mesh.devices.reshape(SIZES), AXES)
    gx, gy, gz = ("zh", "yc"), ("zl", "core"), "gz"
    placed = (
        P(gx, None),
        P(gx),
        P(gx),
        P(),
        P(gx, gy),
        P(gx, gy),
        P(gx, gy, gz),
        P(gx, gy, gz),
        P(gx, gy, gz),
    )

    return jax.shard_map(
        local, mesh=fine, in_specs=placed, out_specs=P(gx, gy, gz), check_vma=False
    )
```

time: 208 us -> 189 us (0.909)
  Pallas kernels: 39.6 us -> 20.9 us
    pallas_call x8, Pallas kernels: 39.6 us -> 20.9 us  [call(): pl.pallas_call(kernel, out_shape=shapes, in_specs=specs, out_specs=[VM] *...]
  transfers between devices with their start and end apart: 10 -> 10, of which waited for: 6 -> 7; matrix products, arithmetic and copies ran while one was open for 0% -> 0% of each run, Pallas kernels for 3% -> 3%
where the time goes in v3:
time: 189 us; the launch traced here: 188 us
  blocking collectives  90.4 us (48%)
  starting transfers between devices  39 us (21%)
  waiting for transfers between devices  33.1 us (18%)
  Pallas kernels  20.9 us (11%)
  local copies, waits for them, and re-layouts  3.96 us (2%)
    all_to_all x1, blocking collectives, local(): lax.all_to_all(packed, ('zh', 'yc'), 0, 0, tiled=True)  53.6 us
    ppermute x10, starting transfers between devices, moved(): return lax.ppermute(array, AXES, pairs_along(dy, dz))  39 us
    ppermute x10, waiting for transfers between devices, moved(): return lax.ppermute(array, AXES, pairs_along(dy, dz))  33.1 us
    all_to_all x1, blocking collectives, local(): lax.all_to_all(out.reshape(16, 16, 128), ('zh', 'yc'), 0, 0, tiled=True)  25.9 us
    pallas_call x8, Pallas kernels, call(): pl.pallas_call(kernel, out_shape=shapes, in_specs=specs, out_specs=[VM] *...  20.9 us
    all_to_all x1, blocking collectives, local(): planes = lax.all_to_all(planes, ('core', 'gz'), 0, 0, tiled=True)  11 us
  transfers between devices with their start and end apart: 10, of which 7 were waited for; matrix products, arithmetic and copies ran while one was open for 0% of the time, Pallas kernels for 3%

profile of v3, /device:TPU:64, one launch (start us, length us, event | category | flops | bytes accessed | tf_op | source)
XLA Modules:
  0.0 188.1 jit_solution(11054999046230956844)
XLA Ops:
  0.0 0.7 copy-done.4
  0.7 0.1 copy-done
  0.8 0.1 rev.3
  0.9 0.5 copy-done.6
  1.5 0.1 copy.18
  1.6 0.6 copy-done.7
  2.1 0.1 copy.16
  2.3 0.0 copy-start.3
  2.3 0.1 copy.17
  2.4 0.1 copy.19
  2.5 0.1 pad.5.clone
  2.5 0.6 copy-done.5
  3.1 0.1 select_reduce_fusion
  3.2 0.1 pad_add_fusion.flags
  3.3 0.1 maximum_maximum_fusion.receivers
  3.4 0.1 and_select_fusion.speed
  3.5 0.8 copy-done.1
  4.3 0.1 copy-done.2
  4.4 0.9 shard_map.91
  5.3 53.6 %all_to_all.15 = f32[16,72,128]{2,1,0:T(8,128)S(1)} all-to-all(f32[16,72,128]{2,1,0:T(8,128)S(1)} %shard_map.91), channel_id=1, replica_groups=mesh['zh'=4,'yc'=4,'zl'=4,'core'=2,'gz'=4] {'zh','yc'}, dimensions={0} | all-to-all | bytes 1179648 | tf_op jit(solution)/shard_map/all_to_all | solution.py:391
  58.9 0.3 shard_map.92
  59.2 1.3 collective-permute-start.1
  60.5 8.5 %collective-permute-start.2 = (f32[384,128]{1,0:T(8,128)S(1)}, f32[384,128]{1,0:T(8,128)S(1)}, u32[]{:S(2)}, u32[]{:S(2)}) collective-permute-start(f32[384,128]{1,0:T(8,128)S(1)} %get-tuple-element.18), channel_id=1, source_target_pairs={{0,128},{128,256},{256,384},{384,385},{385,257},{257,129},{129,1},... | collective-permute-start | bytes 589832 | tf_op jit(solution)/shard_map/ppermute | solution.py:394
  68.9 2.8 %collective-permute-start = (f32[768,128]{1,0:T(8,128)S(1)}, f32[768,128]{1,0:T(8,128)S(1)}, u32[]{:S(2)}, u32[]{:S(2)}) collective-permute-start(f32[768,128]{1,0:T(8,128)S(1)} %get-tuple-element.16.tile), channel_id=1, source_target_pairs={{32,0},{160,128},{288,256},{416,384},{417,385},{289,257},{161,129}... | collective-permute-start | bytes 1179656 | tf_op jit(solution)/shard_map/ppermute | solution.py:394
  71.7 0.9 collective-permute-done.1
  72.6 3.5 %collective-permute-done.2 = f32[384,128]{1,0:T(8,128)S(1)} collective-permute-done((f32[384,128]{1,0:T(8,128)S(1)}, f32[384,128]{1,0:T(8,128)S(1)}, u32[]{:S(2)}, u32[]{:S(2)}) %collective-permute-start.2) | collective-permute-done | bytes 196640 | tf_op jit(solution)/shard_map/ppermute | solution.py:394
  76.2 7.7 %collective-permute-start.3 = (f32[768,128]{1,0:T(8,128)S(1)}, f32[768,128]{1,0:T(8,128)S(1)}, u32[]{:S(2)}, u32[]{:S(2)}) collective-permute-start(f32[768,128]{1,0:T(8,128)S(1)} %constant_dynamic-update-slice_fusion.edges), channel_id=1, source_target_pairs={{32,0},{160,128},{288,256},{416,384},{417,385},{289,257},{161,129}... | collective-permute-start | bytes 1179656 | tf_op jit(solution)/shard_map/ppermute | solution.py:394
  83.9 0.1 pad_add_fusion.1.flags
  84.0 5.8 %shard_map.93 = f32[8,64,128]{2,1,0:T(8,128)S(1)} custom-call(s32[3]{0:T(128)S(1)} %pad_add_fusion.1.flags, f32[1152,128]{1,0:T(8,128)S(1)} %bitcast.21), custom_call_target="tpu_custom_call" | custom-call | flops 20000000 | bytes 1000000 | tf_op jit(solution)/shard_map/pallas_call | solution.py:346
  89.8 11.0 %all_to_all.16.planes = f32[8,64,128]{2,1,0:T(8,128)S(1)} all-to-all(f32[8,64,128]{2,1,0:T(8,128)S(1)} %shard_map.93), channel_id=1, replica_groups=mesh['zh'=4,'yc'=4,'zl'=4,'core'=2,'gz'=4] {'core','gz'}, dimensions={0} | all-to-all | bytes 524288 | tf_op jit(solution)/shard_map/all_to_all | solution.py:411
  100.8 0.0 collective-permute-done.from_y
  100.8 4.4 %shard_map.94 = (f32[32,48,128]{2,1,0:T(8,128)S(1)}, f32[960,128]{1,0:T(8,128)}, f32[16,64,128]{2,1,0:T(8,128)S(1)}) custom-call(f32[768,128]{1,0:T(8,128)S(1)} %get-tuple-element.16.tile, f32[768,128]{1,0:T(8,128)S(1)} %collective-permute-done.from_y, f32[768,128]{1,0:T(8,128)S(1)} %constant_dynamic-update-slice_fusion.edges, ...), custom_call_target="tpu_custom_call" | custom-call | flops 2000000 | bytes 1000000 | tf_op jit(solution)/shard_map/pallas_call | solution.py:346
  105.2 1.9 %collective-permute-start.4 = (f32[960,128]{1,0:T(8,128)}, f32[960,128]{1,0:T(8,128)S(1)}, u32[]{:S(2)}, u32[]{:S(2)}) collective-permute-start(f32[960,128]{1,0:T(8,128)} %get-tuple-element.20), channel_id=1, source_target_pairs={{0,32},{128,160},{256,288},{384,416},{385,417},{257,289},{129,161}... | collective-permute-start | bytes 1474568 | tf_op jit(solution)/shard_map/ppermute | solution.py:394
  107.2 10.2 %collective-permute-done.4.from_y.above = f32[960,128]{1,0:T(8,128)S(1)} collective-permute-done((f32[960,128]{1,0:T(8,128)}, f32[960,128]{1,0:T(8,128)S(1)}, u32[]{:S(2)}, u32[]{:S(2)}) %collective-permute-start.4) | collective-permute-done | bytes 491552 | tf_op jit(solution)/shard_map/ppermute | solution.py:394
  117.3 2.6 %shard_map.95 = (f32[512,128]{1,0:T(8,128)S(1)}, f32[256,128]{1,0:T(8,128)S(1)}, f32[256,128]{1,0:T(8,128)S(1)}) custom-call(s32[1]{0:T(128)} %bitcast.3.flags, f32[32,48,128]{2,1,0:T(8,128)S(1)} %get-tuple-element.19.state, f32[960,128]{1,0:T(8,128)S(1)} %collective-permute-done.4.from_y.above, f32[8,64,128]{2,1,0:T(8,128)S(1)} %all_to_all.16.planes, ...), custom_call_target="tpu_custom_call" | custom-call | flops 2000000 | bytes 1000000 | tf_op jit(solution)/shard_map/pallas_call | solution.py:346
  119.9 1.3 collective-permute-start.6
  121.2 8.5 %collective-permute-start.7 = (f32[256,128]{1,0:T(8,128)S(1)}, f32[256,128]{1,0:T(8,128)S(1)}, u32[]{:S(2)}, u32[]{:S(2)}) collective-permute-start(f32[256,128]{1,0:T(8,128)S(1)} %get-tuple-element.24), channel_id=1, source_target_pairs={{0,128},{128,256},{256,384},{384,385},{385,257},{257,129},{129,1},... | collective-permute-start | bytes 393224 | tf_op jit(solution)/shard_map/ppermute | solution.py:394
  129.7 1.9 %collective-permute-start.5 = (f32[512,128]{1,0:T(8,128)S(1)}, f32[512,128]{1,0:T(8,128)S(1)}, u32[]{:S(2)}, u32[]{:S(2)}) collective-permute-start(f32[512,128]{1,0:T(8,128)S(1)} %get-tuple-element.22.tile), channel_id=1, source_target_pairs={{32,0},{160,128},{288,256},{416,384},{417,385},{289,257},{161,129}... | collective-permute-start | bytes 786440 | tf_op jit(solution)/shard_map/ppermute | solution.py:394
  131.6 4.3 %collective-permute-done.6 = f32[256,128]{1,0:T(8,128)S(1)} collective-permute-done((f32[256,128]{1,0:T(8,128)S(1)}, f32[256,128]{1,0:T(8,128)S(1)}, u32[]{:S(2)}, u32[]{:S(2)}) %collective-permute-start.6) | collective-permute-done | bytes 131104 | tf_op jit(solution)/shard_map/ppermute | solution.py:394
  135.9 0.2 collective-permute-done.7
  136.2 3.2 %collective-permute-start.8 = (f32[512,128]{1,0:T(8,128)S(1)}, f32[512,128]{1,0:T(8,128)S(1)}, u32[]{:S(2)}, u32[]{:S(2)}) collective-permute-start(f32[512,128]{1,0:T(8,128)S(1)} %constant_dynamic-update-slice_fusion.2.edges), channel_id=1, source_target_pairs={{32,0},{160,128},{288,256},{416,384},{417,385},{289,257},{161,129}... | collective-permute-start | bytes 786440 | tf_op jit(solution)/shard_map/ppermute | solution.py:394
  139.4 5.0 %collective-permute-done.8.from_c = f32[512,128]{1,0:T(8,128)S(1)} collective-permute-done((f32[512,128]{1,0:T(8,128)S(1)}, f32[512,128]{1,0:T(8,128)S(1)}, u32[]{:S(2)}, u32[]{:S(2)}) %collective-permute-start.8) | collective-permute-done | bytes 262176 | tf_op jit(solution)/shard_map/ppermute | solution.py:394
  144.4 3.0 %shard_map.96 = (f32[32,48,128]{2,1,0:T(8,128)S(1)}, f32[768,128]{1,0:T(8,128)S(1)}) custom-call(f32[512,128]{1,0:T(8,128)S(1)} %get-tuple-element.22.tile, f32[512,128]{1,0:T(8,128)S(1)} %collective-permute-done.5.from_y, f32[512,128]{1,0:T(8,128)S(1)} %constant_dynamic-update-slice_fusion.2.edges, f32[512,128]{1,0:T(8,128)S(1)} %collective-permute-done.8.from_c, ...), custom_call_target="tpu_custom_call" | custom-call | flops 2000000 | bytes 1000000 | tf_op jit(solution)/shard_map/pallas_call | solution.py:346
  147.4 1.9 %collective-permute-start.9 = (f32[768,128]{1,0:T(8,128)S(1)}, f32[768,128]{1,0:T(8,128)S(1)}, u32[]{:S(2)}, u32[]{:S(2)}) collective-permute-start(f32[768,128]{1,0:T(8,128)S(1)} %get-tuple-element.26), channel_id=1, source_target_pairs={{0,32},{128,160},{256,288},{384,416},{385,417},{257,289},{129,161}... | collective-permute-start | bytes 1179656 | tf_op jit(solution)/shard_map/ppermute | solution.py:394
  149.4 9.0 %collective-permute-done.9.from_y = f32[768,128]{1,0:T(8,128)S(1)} collective-permute-done((f32[768,128]{1,0:T(8,128)S(1)}, f32[768,128]{1,0:T(8,128)S(1)}, u32[]{:S(2)}, u32[]{:S(2)}) %collective-permute-start.9) | collective-permute-done | bytes 393248 | tf_op jit(solution)/shard_map/ppermute | solution.py:394
  158.3 2.5 %shard_map.97 = f32[256,128]{1,0:T(8,128)S(1)} custom-call(s32[1]{0:T(128)} %bitcast.3.flags, f32[32,48,128]{2,1,0:T(8,128)S(1)} %get-tuple-element.25.state, f32[768,128]{1,0:T(8,128)S(1)} %collective-permute-done.9.from_y, f32[8,64,128]{2,1,0:T(8,128)S(1)} %all_to_all.16.planes, f32[16,64,128]{2,1,0:T(8,128)S(1)} %get-tuple-element.21.speeds, ...), custom_call_target="tpu_custom_call" | custom-call | flops 2000000 | bytes 1000000 | tf_op jit(solution)/shard_map/pallas_call | solution.py:346
  160.8 25.9 %all_to_all.17.got = f32[16,16,128]{2,1,0:T(8,128)S(1)} all-to-all(f32[16,16,128]{2,1,0:T(8,128)S(1)} %bitcast.22), channel_id=1, replica_groups=mesh['zh'=4,'yc'=4,'zl'=4,'core'=2,'gz'=4] {'zh','yc'}, dimensions={0} | all-to-all | bytes 262144 | tf_op jit(solution)/shard_map/all_to_all | solution.py:434
  186.7 1.4 shard_map.98
  (26 shorter events, 0.1 us)
Async XLA Ops:
  0.0 0.8 copy-start
  0.0 0.7 copy-start.4
  0.8 0.7 copy-start.6
  1.5 0.7 copy-start.7
  2.3 1.1 copy-start.3
  2.5 0.7 copy-start.5
  2.5 0.7 copy-start.8
  3.4 0.9 copy-start.1
  3.4 1.0 copy-start.2
  59.2 13.4 %collective-permute-start.1 = (f32[384,128]{1,0:T(8,128)S(1)}, f32[384,128]{1,0:T(8,128)S(1)}, u32[]{:S(2)}, u32[]{:S(2)}) collective-permute-start(f32[384,128]{1,0:T(8,128)S(1)} %get-tuple-element.17), channel_id=1, source_target_pairs={{128,0},{256,128},{384,256},{385,384},{257,385},{129,257},{1,129},... | collective-permute-start | bytes 589832 | tf_op jit(solution)/shard_map/ppermute | solution.py:394
  60.5 15.7 %collective-permute-start.2 = (f32[384,128]{1,0:T(8,128)S(1)}, f32[384,128]{1,0:T(8,128)S(1)}, u32[]{:S(2)}, u32[]{:S(2)}) collective-permute-start(f32[384,128]{1,0:T(8,128)S(1)} %get-tuple-element.18), channel_id=1, source_target_pairs={{0,128},{128,256},{256,384},{384,385},{385,257},{257,129},{129,1},... | collective-permute-start | bytes 589832 | tf_op jit(solution)/shard_map/ppermute | solution.py:394
  68.9 31.8 %collective-permute-start = (f32[768,128]{1,0:T(8,128)S(1)}, f32[768,128]{1,0:T(8,128)S(1)}, u32[]{:S(2)}, u32[]{:S(2)}) collective-permute-start(f32[768,128]{1,0:T(8,128)S(1)} %get-tuple-element.16.tile), channel_id=1, source_target_pairs={{32,0},{160,128},{288,256},{416,384},{417,385},{289,257},{161,129}... | collective-permute-start | bytes 1179656 | tf_op jit(solution)/shard_map/ppermute | solution.py:394
  76.2 24.6 %collective-permute-start.3 = (f32[768,128]{1,0:T(8,128)S(1)}, f32[768,128]{1,0:T(8,128)S(1)}, u32[]{:S(2)}, u32[]{:S(2)}) collective-permute-start(f32[768,128]{1,0:T(8,128)S(1)} %constant_dynamic-update-slice_fusion.edges), channel_id=1, source_target_pairs={{32,0},{160,128},{288,256},{416,384},{417,385},{289,257},{161,129}... | collective-permute-start | bytes 1179656 | tf_op jit(solution)/shard_map/ppermute | solution.py:394
  105.2 12.1 %collective-permute-start.4 = (f32[960,128]{1,0:T(8,128)}, f32[960,128]{1,0:T(8,128)S(1)}, u32[]{:S(2)}, u32[]{:S(2)}) collective-permute-start(f32[960,128]{1,0:T(8,128)} %get-tuple-element.20), channel_id=1, source_target_pairs={{0,32},{128,160},{256,288},{384,416},{385,417},{257,289},{129,161}... | collective-permute-start | bytes 1474568 | tf_op jit(solution)/shard_map/ppermute | solution.py:394
  119.9 16.0 %collective-permute-start.6 = (f32[256,128]{1,0:T(8,128)S(1)}, f32[256,128]{1,0:T(8,128)S(1)}, u32[]{:S(2)}, u32[]{:S(2)}) collective-permute-start(f32[256,128]{1,0:T(8,128)S(1)} %get-tuple-element.23), channel_id=1, source_target_pairs={{128,0},{256,128},{384,256},{385,384},{257,385},{129,257},{1,129},... | collective-permute-start | bytes 393224 | tf_op jit(solution)/shard_map/ppermute | solution.py:394
  121.2 14.9 %collective-permute-start.7 = (f32[256,128]{1,0:T(8,128)S(1)}, f32[256,128]{1,0:T(8,128)S(1)}, u32[]{:S(2)}, u32[]{:S(2)}) collective-permute-start(f32[256,128]{1,0:T(8,128)S(1)} %get-tuple-element.24), channel_id=1, source_target_pairs={{0,128},{128,256},{256,384},{384,385},{385,257},{257,129},{129,1},... | collective-permute-start | bytes 393224 | tf_op jit(solution)/shard_map/ppermute | solution.py:394
  129.7 9.7 %collective-permute-start.5 = (f32[512,128]{1,0:T(8,128)S(1)}, f32[512,128]{1,0:T(8,128)S(1)}, u32[]{:S(2)}, u32[]{:S(2)}) collective-permute-start(f32[512,128]{1,0:T(8,128)S(1)} %get-tuple-element.22.tile), channel_id=1, source_target_pairs={{32,0},{160,128},{288,256},{416,384},{417,385},{289,257},{161,129}... | collective-permute-start | bytes 786440 | tf_op jit(solution)/shard_map/ppermute | solution.py:394
  136.2 8.3 %collective-permute-start.8 = (f32[512,128]{1,0:T(8,128)S(1)}, f32[512,128]{1,0:T(8,128)S(1)}, u32[]{:S(2)}, u32[]{:S(2)}) collective-permute-start(f32[512,128]{1,0:T(8,128)S(1)} %constant_dynamic-update-slice_fusion.2.edges), channel_id=1, source_target_pairs={{32,0},{160,128},{288,256},{416,384},{417,385},{289,257},{161,129}... | collective-permute-start | bytes 786440 | tf_op jit(solution)/shard_map/ppermute | solution.py:394
  147.4 10.9 %collective-permute-start.9 = (f32[768,128]{1,0:T(8,128)S(1)}, f32[768,128]{1,0:T(8,128)S(1)}, u32[]{:S(2)}, u32[]{:S(2)}) collective-permute-start(f32[768,128]{1,0:T(8,128)S(1)} %get-tuple-element.26), channel_id=1, source_target_pairs={{0,32},{128,160},{256,288},{384,416},{385,417},{257,289},{129,161}... | collective-permute-start | bytes 1179656 | tf_op jit(solution)/shard_map/ppermute | solution.py:394

commit v4 on v3

--- a/solution.py
+++ b/solution.py
@@ -58,7 +58,39 @@
     return lax.broadcasted_iota(jnp.int32, (rows, 128), 1) < 64
 
 
-def pack_kernel(flags, now, prev, speed, receivers, out):
+def pack_kernel(
+    flags, table, now, prev, courant, tops, thicks, traces, cells, classes, out, speed, samples
+):
+    depth = (lax.broadcasted_iota(jnp.int32, (64, 128), 1) + flags[3]).astype(F32)
+    row = lax.broadcasted_iota(jnp.int32, (64, 32), 0) // 2
+    match = row == lax.broadcasted_iota(jnp.int32, (64, 32), 1)
+
+    def along_y(line):
+        values = jnp.where(match, jnp.broadcast_to(line.astype(F32), (64, 32)), 0.0)
+        return jnp.broadcast_to(jnp.sum(values, axis=1, keepdims=True), (64, 128))
+
+    for half in range(2):
+        roof = along_y(tops[half : half + 1, :])
+        floor = roof + along_y(thicks[half : half + 1, :])
+        solid = (depth >= roof) & (depth < floor)
+        for x in (2 * half, 2 * half + 1):
+            speed[x] = jnp.where(solid, 0.0, courant[x])
+
+    given = traces[...].astype(F32)
+    for first in range(8):
+        samples[first] = given[4 * first : 4 * first + 4, :]
+    own = samples[flags[4]]
+    kinds = classes[...]
+    weights = jnp.zeros((4, 128), F32)
+    for kind in range(16):
+        weights = jnp.where(kinds == kind, table[kind], weights)
+    terms = [own[:, 128 * j : 128 * j + 128] * weights[j : j + 1, :] for j in range(4)]
+    receivers = jnp.concatenate(
+        terms + [cells[...].astype(F32), jnp.zeros((4, 128), F32)], axis=0
+    )
+    for target in range(16):
+        out[target, FIELD_ROWS:MSG_ROWS, :] = receivers
+
     group = lane_group(16)
     for field, ref in enumerate((now, prev, speed)):
         for x in range(4):
@@ -73,9 +105,6 @@
                     target = source_of(flags, ys, zs)
                     first = field * 16 + x * 4
                     out[target, first : first + 4, :] = piece[4 * ys : 4 * ys + 4]
-    rows = receivers[...]
-    for target in range(16):
-        out[target, FIELD_ROWS:MSG_ROWS, :] = rows
 
 
 def unpack_kernel(got, tile, near, far):
@@ -106,7 +135,7 @@
         offset = lax.broadcasted_iota(jnp.int32, (8, 512), 0) // 4
         lanes = lax.broadcasted_iota(jnp.int32, (128, 512), 0)
 
-        def shard(src, totals):
+        def shard(src, total):
             base = src * MSG_ROWS
             terms = got[pl.ds(pl.multiple_of(base + FIELD_ROWS, 8), 16), :]
             cell = got[pl.ds(pl.multiple_of(base + 64, 8), 8), :]
@@ -117,31 +146,28 @@
             cell_x = cell >> 9
             upper = terms.astype(jnp.bfloat16).astype(F32)
             lower = terms - upper
-            results = []
+            at_lane = []
             for window in range(2):
                 cell_y = (cell & 511) - flags[1 + window]
                 lane = jnp.where(
                     (cell_y >= 0) & (cell_y < 32), (cell_y >> 2) * 16 + (cell_x >> 2), -1
                 )
-                at_lane = (lanes == lane).astype(F32).astype(jnp.bfloat16)
-                row = jnp.broadcast_to((cell_x & 3) * 4 + (cell_y & 3), (8, 512)) - offset
-                here = [row == 2 * j for j in range(ROWS // 2)]
-                total = totals[window]
-                for part in (upper, lower):
-                    rows = jnp.concatenate([jnp.where(h, part, 0.0) for h in here], axis=0)
-                    total = total + lax.dot_general(
-                        rows.astype(jnp.bfloat16),
-                        at_lane,
-                        (((1,), (1,)), ((), ())),
-                        preferred_element_type=F32,
-                    )
-                results.append(total)
-            return tuple(results)
-
-        zero = jnp.zeros((ROWS * 4, 128), F32)
-        totals = lax.fori_loop(0, 16, shard, (zero, zero))
-        for window in range(2):
-            out[4 * window] = totals[window]
+                at_lane.append((lanes == lane).astype(F32))
+            at_lane = jnp.concatenate(at_lane, axis=0).astype(jnp.bfloat16)
+            row = jnp.broadcast_to((cell_x & 3) * 4 + (cell_y & 3), (8, 512)) - offset
+            here = [row == 2 * j for j in range(ROWS // 2)]
+            rows = [jnp.where(h, part, 0.0) for part in (upper, lower) for h in here]
+            return total + lax.dot_general(
+                jnp.concatenate(rows, axis=0).astype(jnp.bfloat16),
+                at_lane,
+                (((1,), (1,)), ((), ())),
+                preferred_element_type=F32,
+            )
+
+        total = lax.fori_loop(0, 16, shard, jnp.zeros((ROWS * 8, 256), F32))
+        total = total[: ROWS * 4] + total[ROWS * 4 :]
+        out[0] = total[:, :128]
+        out[4] = total[:, 128:]
 
 
 def swap(rows):
@@ -203,7 +229,7 @@
                     around = around + (now[r, at - 1 : at + 7, :] + now[r, at + 1 : at + 9, :])
                     new = m[r, here, :] * c[r] - old[r, here, :] + k[r, here, :] * around
                     if at == Z0:
-                        row = planes[(step >> 2) * 4 + chunk, pl.ds(r * 4 + (step & 3), 1), :]
+                        row = planes[(step >> 2) * 4 + chunk, pl.ds(r * 4 + 3 - (step & 3), 1), :]
                         new = new + row * top
                     old[r, here, :] = new
 
@@ -369,24 +395,17 @@
     gy = zl * 2 + core
     flip_z = gz % 2
     ty = gy * 4 + jnp.where(core == 0, yc - zl, zl - yc) % 4
-    place = jnp.stack([zl, core, flip_z]).astype(jnp.int32)
-
-    roof = jnp.repeat(jnp.repeat(obstacle_top, 2, axis=0), 2, axis=1)[:, :, None]
-    thickness = jnp.repeat(jnp.repeat(obstacle_thick, 2, axis=0), 2, axis=1)[:, :, None]
-    depth = gz * 128 + jnp.arange(128, dtype=jnp.int32)[None, None, :]
-    solid = (depth >= roof) & (depth < roof + thickness)
-    speed = jnp.where(solid, 0.0, courant)
-
-    classes = weight_class[:, None] == jnp.arange(16, dtype=jnp.int32)[None, :]
-    weights = jnp.sum(jnp.where(classes, weight_table[None, :], 0.0), axis=1)
-    own = lax.dynamic_slice_in_dim(traces, 28 - 8 * gz - 4 * core, 4, axis=1)[:, ::-1]
-    terms = weights[:, None] * own.astype(F32)
-    terms = terms.reshape(4, 128, 4).transpose(0, 2, 1).reshape(16, 128)
-    cells = receiver_cell.astype(F32).reshape(4, 128)
-    receivers = jnp.concatenate([terms, cells, jnp.zeros((4, 128), F32)], axis=0)
-
-    (packed,) = call(
-        pack_kernel, [(16, MSG_ROWS, 128)], p_now, p_prev, speed, receivers, flags=place
+    place = jnp.stack([zl, core, flip_z, gz * 128, 7 - 2 * gz - core]).astype(jnp.int32)
+    packed = pl.pallas_call(
+        pack_kernel,
+        out_shape=jax.ShapeDtypeStruct((16, MSG_ROWS, 128), F32),
+        in_specs=[SM, SM] + [VM] * 8,
+        out_specs=VM,
+        scratch_shapes=[pltpu.VMEM((4, 64, 128), F32), pltpu.VMEM((8, 4, 512), F32)],
+        name="pack",
+    )(
+        place, weight_table, p_now, p_prev, courant, obstacle_top, obstacle_thick,
+        traces.T, receiver_cell.reshape(4, 128), weight_class.reshape(4, 128),
     )
     got = lax.all_to_all(packed, ("zh", "yc"), 0, 0, tiled=True).reshape(16 * MSG_ROWS, 128)
 

time: 189 us -> 185 us (0.979)
  the two profiles are of different devices: /device:TPU:64 before, /device:TPU:8 now
where the time goes in v4:
time: 185 us; the launch traced here: 184 us
  blocking collectives  101 us (55%)
  starting transfers between devices  36.5 us (20%)
  waiting for transfers between devices  24.3 us (13%)
  Pallas kernels  20.9 us (11%)
    all_to_all x1, blocking collectives, local(): lax.all_to_all(packed, ('zh', 'yc'), 0, 0, tiled=True)  50.8 us
    ppermute x10, starting transfers between devices, moved(): return lax.ppermute(array, AXES, pairs_along(dy, dz))  36.5 us
    all_to_all x1, blocking collectives, local(): planes = lax.all_to_all(planes, ('core', 'gz'), 0, 0, tiled=True)  25.7 us
    all_to_all x1, blocking collectives, local(): lax.all_to_all(out.reshape(16, 16, 128), ('zh', 'yc'), 0, 0, tiled=True)  24.9 us
    ppermute x10, waiting for transfers between devices, moved(): return lax.ppermute(array, AXES, pairs_along(dy, dz))  24.3 us
    pallas_call x7, Pallas kernels, call(): pl.pallas_call(kernel, out_shape=shapes, in_specs=specs, out_specs=[VM] *...  18.6 us
  transfers between devices with their start and end apart: 10, of which 5 were waited for; matrix products, arithmetic and copies ran while one was open for 0% of the time, Pallas kernels for 2%

profile of v4, /device:TPU:8, one launch (start us, length us, event | category | flops | bytes accessed | tf_op | source)
XLA Modules:
  0.0 184.2 jit_solution(17524172700698623099)
XLA Ops:
  0.0 0.6 stack.38.flags
  0.6 2.3 %pack.1 = f32[16,72,128]{2,1,0:T(8,128)} custom-call(s32[5]{0:T(128)} %stack.38.flags, f32[16]{0:T(128)} %table.1, f32[4,64,128]{2,1,0:T(8,128)} %now.1, f32[4,64,128]{2,1,0:T(8,128)} %prev.1, f32[4,64,128]{2,1,0:T(8,128)} %courant.1, s32[2,32]{1,0:T(2,128)} %tops.1, s32[2,32]{1,0:T(2,128)} %thicks.1, bf16[32,512]{1,0:T(8,128)(2,1)} %bitcast.17, ...), custom_call_target="tpu_custom_call" | custom-call | tf_op jit(solution)/shard_map/pack/pallas_call | solution.py:399
  2.9 50.8 %all_to_all.15 = f32[16,72,128]{2,1,0:T(8,128)S(1)} all-to-all(f32[16,72,128]{2,1,0:T(8,128)} %pack.1), channel_id=1, replica_groups=mesh['zh'=4,'yc'=4,'zl'=4,'core'=2,'gz'=4] {'zh','yc'}, dimensions={0} | all-to-all | bytes 1179648 | tf_op jit(solution)/shard_map/all_to_all | solution.py:410
  53.7 0.3 shard_map.91
  54.0 1.3 collective-permute-start.1
  55.3 8.5 %collective-permute-start.2 = (f32[384,128]{1,0:T(8,128)S(1)}, f32[384,128]{1,0:T(8,128)S(1)}, u32[]{:S(2)}, u32[]{:S(2)}) collective-permute-start(f32[384,128]{1,0:T(8,128)S(1)} %get-tuple-element.18), channel_id=1, source_target_pairs={{0,128},{128,256},{256,384},{384,385},{385,257},{257,129},{129,1},... | collective-permute-start | bytes 589832 | tf_op jit(solution)/shard_map/ppermute | solution.py:413
  63.8 1.9 %collective-permute-start = (f32[768,128]{1,0:T(8,128)S(1)}, f32[768,128]{1,0:T(8,128)S(1)}, u32[]{:S(2)}, u32[]{:S(2)}) collective-permute-start(f32[768,128]{1,0:T(8,128)S(1)} %get-tuple-element.16.tile), channel_id=1, source_target_pairs={{32,0},{160,128},{288,256},{416,384},{417,385},{289,257},{161,129}... | collective-permute-start | bytes 1179656 | tf_op jit(solution)/shard_map/ppermute | solution.py:413
  65.7 0.0 collective-permute-done.1
  65.7 1.2 collective-permute-done.2
  67.0 1.9 %collective-permute-start.3 = (f32[768,128]{1,0:T(8,128)S(1)}, f32[768,128]{1,0:T(8,128)S(1)}, u32[]{:S(2)}, u32[]{:S(2)}) collective-permute-start(f32[768,128]{1,0:T(8,128)S(1)} %constant_dynamic-update-slice_fusion.edges), channel_id=1, source_target_pairs={{32,0},{160,128},{288,256},{416,384},{417,385},{289,257},{161,129}... | collective-permute-start | bytes 1179656 | tf_op jit(solution)/shard_map/ppermute | solution.py:413
  69.0 0.1 pad_add_fusion.flags
  69.1 4.4 %shard_map.92 = f32[8,64,128]{2,1,0:T(8,128)S(1)} custom-call(s32[3]{0:T(128)S(1)} %pad_add_fusion.flags, f32[1152,128]{1,0:T(8,128)S(1)} %bitcast.15), custom_call_target="tpu_custom_call" | custom-call | flops 20000000 | bytes 1000000 | tf_op jit(solution)/shard_map/pallas_call | solution.py:372
  73.5 25.7 %all_to_all.16.planes = f32[8,64,128]{2,1,0:T(8,128)S(1)} all-to-all(f32[8,64,128]{2,1,0:T(8,128)S(1)} %shard_map.92), channel_id=1, replica_groups=mesh['zh'=4,'yc'=4,'zl'=4,'core'=2,'gz'=4] {'core','gz'}, dimensions={0} | all-to-all | bytes 524288 | tf_op jit(solution)/shard_map/all_to_all | solution.py:430
  99.2 0.0 collective-permute-done.from_y
  99.2 0.0 collective-permute-done.3.from_c
  99.2 4.5 %shard_map.93 = (f32[32,48,128]{2,1,0:T(8,128)S(1)}, f32[960,128]{1,0:T(8,128)}, f32[16,64,128]{2,1,0:T(8,128)S(1)}) custom-call(f32[768,128]{1,0:T(8,128)S(1)} %get-tuple-element.16.tile, f32[768,128]{1,0:T(8,128)S(1)} %collective-permute-done.from_y, f32[768,128]{1,0:T(8,128)S(1)} %constant_dynamic-update-slice_fusion.edges, ...), custom_call_target="tpu_custom_call" | custom-call | flops 2000000 | bytes 1000000 | tf_op jit(solution)/shard_map/pallas_call | solution.py:372
  103.7 3.2 %collective-permute-start.4 = (f32[960,128]{1,0:T(8,128)}, f32[960,128]{1,0:T(8,128)S(1)}, u32[]{:S(2)}, u32[]{:S(2)}) collective-permute-start(f32[960,128]{1,0:T(8,128)} %get-tuple-element.20), channel_id=1, source_target_pairs={{0,32},{128,160},{256,288},{384,416},{385,417},{257,289},{129,161}... | collective-permute-start | bytes 1474568 | tf_op jit(solution)/shard_map/ppermute | solution.py:413
  106.9 7.7 %collective-permute-done.4.from_y.above = f32[960,128]{1,0:T(8,128)S(1)} collective-permute-done((f32[960,128]{1,0:T(8,128)}, f32[960,128]{1,0:T(8,128)S(1)}, u32[]{:S(2)}, u32[]{:S(2)}) %collective-permute-start.4) | collective-permute-done | bytes 491552 | tf_op jit(solution)/shard_map/ppermute | solution.py:413
  114.6 2.6 %shard_map.94 = (f32[512,128]{1,0:T(8,128)S(1)}, f32[256,128]{1,0:T(8,128)S(1)}, f32[256,128]{1,0:T(8,128)S(1)}) custom-call(s32[1]{0:T(128)} %bitcast.5.flags, f32[32,48,128]{2,1,0:T(8,128)S(1)} %get-tuple-element.19.state, f32[960,128]{1,0:T(8,128)S(1)} %collective-permute-done.4.from_y.above, f32[8,64,128]{2,1,0:T(8,128)S(1)} %all_to_all.16.planes, ...), custom_call_target="tpu_custom_call" | custom-call | flops 2000000 | bytes 1000000 | tf_op jit(solution)/shard_map/pallas_call | solution.py:372
  117.2 1.3 collective-permute-start.6
  118.5 8.5 %collective-permute-start.7 = (f32[256,128]{1,0:T(8,128)S(1)}, f32[256,128]{1,0:T(8,128)S(1)}, u32[]{:S(2)}, u32[]{:S(2)}) collective-permute-start(f32[256,128]{1,0:T(8,128)S(1)} %get-tuple-element.24), channel_id=1, source_target_pairs={{0,128},{128,256},{256,384},{384,385},{385,257},{257,129},{129,1},... | collective-permute-start | bytes 393224 | tf_op jit(solution)/shard_map/ppermute | solution.py:413
  126.9 1.9 %collective-permute-start.5 = (f32[512,128]{1,0:T(8,128)S(1)}, f32[512,128]{1,0:T(8,128)S(1)}, u32[]{:S(2)}, u32[]{:S(2)}) collective-permute-start(f32[512,128]{1,0:T(8,128)S(1)} %get-tuple-element.22.tile), channel_id=1, source_target_pairs={{32,0},{160,128},{288,256},{416,384},{417,385},{289,257},{161,129}... | collective-permute-start | bytes 786440 | tf_op jit(solution)/shard_map/ppermute | solution.py:413
  128.9 5.5 %collective-permute-done.6 = f32[256,128]{1,0:T(8,128)S(1)} collective-permute-done((f32[256,128]{1,0:T(8,128)S(1)}, f32[256,128]{1,0:T(8,128)S(1)}, u32[]{:S(2)}, u32[]{:S(2)}) %collective-permute-start.6) | collective-permute-done | bytes 131104 | tf_op jit(solution)/shard_map/ppermute | solution.py:413
  134.4 0.0 collective-permute-done.7
  134.4 4.1 %collective-permute-start.8 = (f32[512,128]{1,0:T(8,128)S(1)}, f32[512,128]{1,0:T(8,128)S(1)}, u32[]{:S(2)}, u32[]{:S(2)}) collective-permute-start(f32[512,128]{1,0:T(8,128)S(1)} %constant_dynamic-update-slice_fusion.2.edges), channel_id=1, source_target_pairs={{32,0},{160,128},{288,256},{416,384},{417,385},{289,257},{161,129}... | collective-permute-start | bytes 786440 | tf_op jit(solution)/shard_map/ppermute | solution.py:413
  138.5 0.0 collective-permute-done.5.from_y
  138.5 4.1 %collective-permute-done.8.from_c = f32[512,128]{1,0:T(8,128)S(1)} collective-permute-done((f32[512,128]{1,0:T(8,128)S(1)}, f32[512,128]{1,0:T(8,128)S(1)}, u32[]{:S(2)}, u32[]{:S(2)}) %collective-permute-start.8) | collective-permute-done | bytes 262176 | tf_op jit(solution)/shard_map/ppermute | solution.py:413
  142.7 3.0 %shard_map.95 = (f32[32,48,128]{2,1,0:T(8,128)S(1)}, f32[768,128]{1,0:T(8,128)S(1)}) custom-call(f32[512,128]{1,0:T(8,128)S(1)} %get-tuple-element.22.tile, f32[512,128]{1,0:T(8,128)S(1)} %collective-permute-done.5.from_y, f32[512,128]{1,0:T(8,128)S(1)} %constant_dynamic-update-slice_fusion.2.edges, f32[512,128]{1,0:T(8,128)S(1)} %collective-permute-done.8.from_c, ...), custom_call_target="tpu_custom_call" | custom-call | flops 2000000 | bytes 1000000 | tf_op jit(solution)/shard_map/pallas_call | solution.py:372
  145.7 3.9 %collective-permute-start.9 = (f32[768,128]{1,0:T(8,128)S(1)}, f32[768,128]{1,0:T(8,128)S(1)}, u32[]{:S(2)}, u32[]{:S(2)}) collective-permute-start(f32[768,128]{1,0:T(8,128)S(1)} %get-tuple-element.26), channel_id=1, source_target_pairs={{0,32},{128,160},{256,288},{384,416},{385,417},{257,289},{129,161}... | collective-permute-start | bytes 1179656 | tf_op jit(solution)/shard_map/ppermute | solution.py:413
  149.6 5.7 %collective-permute-done.9.from_y = f32[768,128]{1,0:T(8,128)S(1)} collective-permute-done((f32[768,128]{1,0:T(8,128)S(1)}, f32[768,128]{1,0:T(8,128)S(1)}, u32[]{:S(2)}, u32[]{:S(2)}) %collective-permute-start.9) | collective-permute-done | bytes 393248 | tf_op jit(solution)/shard_map/ppermute | solution.py:413
  155.3 2.5 %shard_map.96 = f32[256,128]{1,0:T(8,128)S(1)} custom-call(s32[1]{0:T(128)} %bitcast.5.flags, f32[32,48,128]{2,1,0:T(8,128)S(1)} %get-tuple-element.25.state, f32[768,128]{1,0:T(8,128)S(1)} %collective-permute-done.9.from_y, f32[8,64,128]{2,1,0:T(8,128)S(1)} %all_to_all.16.planes, f32[16,64,128]{2,1,0:T(8,128)S(1)} %get-tuple-element.21.speeds, ...), custom_call_target="tpu_custom_call" | custom-call | flops 2000000 | bytes 1000000 | tf_op jit(solution)/shard_map/pallas_call | solution.py:372
  157.8 0.0 copy-start
  157.9 24.9 %all_to_all.17.got = f32[16,16,128]{2,1,0:T(8,128)S(1)} all-to-all(f32[16,16,128]{2,1,0:T(8,128)S(1)} %bitcast.16), channel_id=1, replica_groups=mesh['zh'=4,'yc'=4,'zl'=4,'core'=2,'gz'=4] {'zh','yc'}, dimensions={0} | all-to-all | bytes 262144 | tf_op jit(solution)/shard_map/all_to_all | solution.py:453
  182.8 0.0 copy-done
  182.8 1.4 shard_map.97
  (4 shorter events, 0.1 us)
Async XLA Ops:
  54.0 11.7 %collective-permute-start.1 = (f32[384,128]{1,0:T(8,128)S(1)}, f32[384,128]{1,0:T(8,128)S(1)}, u32[]{:S(2)}, u32[]{:S(2)}) collective-permute-start(f32[384,128]{1,0:T(8,128)S(1)} %get-tuple-element.17), channel_id=1, source_target_pairs={{128,0},{256,128},{384,256},{385,384},{257,385},{129,257},{1,129},... | collective-permute-start | bytes 589832 | tf_op jit(solution)/shard_map/ppermute | solution.py:413
  55.3 11.7 %collective-permute-start.2 = (f32[384,128]{1,0:T(8,128)S(1)}, f32[384,128]{1,0:T(8,128)S(1)}, u32[]{:S(2)}, u32[]{:S(2)}) collective-permute-start(f32[384,128]{1,0:T(8,128)S(1)} %get-tuple-element.18), channel_id=1, source_target_pairs={{0,128},{128,256},{256,384},{384,385},{385,257},{257,129},{129,1},... | collective-permute-start | bytes 589832 | tf_op jit(solution)/shard_map/ppermute | solution.py:413
  63.8 35.4 %collective-permute-start = (f32[768,128]{1,0:T(8,128)S(1)}, f32[768,128]{1,0:T(8,128)S(1)}, u32[]{:S(2)}, u32[]{:S(2)}) collective-permute-start(f32[768,128]{1,0:T(8,128)S(1)} %get-tuple-element.16.tile), channel_id=1, source_target_pairs={{32,0},{160,128},{288,256},{416,384},{417,385},{289,257},{161,129}... | collective-permute-start | bytes 1179656 | tf_op jit(solution)/shard_map/ppermute | solution.py:413
  67.0 32.2 %collective-permute-start.3 = (f32[768,128]{1,0:T(8,128)S(1)}, f32[768,128]{1,0:T(8,128)S(1)}, u32[]{:S(2)}, u32[]{:S(2)}) collective-permute-start(f32[768,128]{1,0:T(8,128)S(1)} %constant_dynamic-update-slice_fusion.edges), channel_id=1, source_target_pairs={{32,0},{160,128},{288,256},{416,384},{417,385},{289,257},{161,129}... | collective-permute-start | bytes 1179656 | tf_op jit(solution)/shard_map/ppermute | solution.py:413
  103.7 10.9 %collective-permute-start.4 = (f32[960,128]{1,0:T(8,128)}, f32[960,128]{1,0:T(8,128)S(1)}, u32[]{:S(2)}, u32[]{:S(2)}) collective-permute-start(f32[960,128]{1,0:T(8,128)} %get-tuple-element.20), channel_id=1, source_target_pairs={{0,32},{128,160},{256,288},{384,416},{385,417},{257,289},{129,161}... | collective-permute-start | bytes 1474568 | tf_op jit(solution)/shard_map/ppermute | solution.py:413
  117.2 17.2 %collective-permute-start.6 = (f32[256,128]{1,0:T(8,128)S(1)}, f32[256,128]{1,0:T(8,128)S(1)}, u32[]{:S(2)}, u32[]{:S(2)}) collective-permute-start(f32[256,128]{1,0:T(8,128)S(1)} %get-tuple-element.23), channel_id=1, source_target_pairs={{128,0},{256,128},{384,256},{385,384},{257,385},{129,257},{1,129},... | collective-permute-start | bytes 393224 | tf_op jit(solution)/shard_map/ppermute | solution.py:413
  118.5 15.9 %collective-permute-start.7 = (f32[256,128]{1,0:T(8,128)S(1)}, f32[256,128]{1,0:T(8,128)S(1)}, u32[]{:S(2)}, u32[]{:S(2)}) collective-permute-start(f32[256,128]{1,0:T(8,128)S(1)} %get-tuple-element.24), channel_id=1, source_target_pairs={{0,128},{128,256},{256,384},{384,385},{385,257},{257,129},{129,1},... | collective-permute-start | bytes 393224 | tf_op jit(solution)/shard_map/ppermute | solution.py:413
  126.9 11.6 %collective-permute-start.5 = (f32[512,128]{1,0:T(8,128)S(1)}, f32[512,128]{1,0:T(8,128)S(1)}, u32[]{:S(2)}, u32[]{:S(2)}) collective-permute-start(f32[512,128]{1,0:T(8,128)S(1)} %get-tuple-element.22.tile), channel_id=1, source_target_pairs={{32,0},{160,128},{288,256},{416,384},{417,385},{289,257},{161,129}... | collective-permute-start | bytes 786440 | tf_op jit(solution)/shard_map/ppermute | solution.py:413
  134.4 8.3 %collective-permute-start.8 = (f32[512,128]{1,0:T(8,128)S(1)}, f32[512,128]{1,0:T(8,128)S(1)}, u32[]{:S(2)}, u32[]{:S(2)}) collective-permute-start(f32[512,128]{1,0:T(8,128)S(1)} %constant_dynamic-update-slice_fusion.2.edges), channel_id=1, source_target_pairs={{32,0},{160,128},{288,256},{416,384},{417,385},{289,257},{161,129}... | collective-permute-start | bytes 786440 | tf_op jit(solution)/shard_map/ppermute | solution.py:413
  145.7 9.7 %collective-permute-start.9 = (f32[768,128]{1,0:T(8,128)S(1)}, f32[768,128]{1,0:T(8,128)S(1)}, u32[]{:S(2)}, u32[]{:S(2)}) collective-permute-start(f32[768,128]{1,0:T(8,128)S(1)} %get-tuple-element.26), channel_id=1, source_target_pairs={{0,32},{128,160},{256,288},{384,416},{385,417},{257,289},{129,161}... | collective-permute-start | bytes 1179656 | tf_op jit(solution)/shard_map/ppermute | solution.py:413
  157.8 25.0 %copy-start = (s32[5]{0:T(128)S(1)}, s32[5]{0:T(128)}, u32[]{:S(2)}) copy-start(s32[5]{0:T(128)} %stack.38.flags) | copy-start | bytes 64

commit v5 on v4

--- a/solution.py
+++ b/solution.py
@@ -261,13 +261,13 @@
         msg[r * 48 : r * 48 + 48, :] = middle_of(a, b, r, -8, 48)
 
 
-def load_right(a, b, tile, from_y, edges, from_c):
+def load_right(a, b, tile, from_y, edges, corners):
     for r in range(ROWS):
         rows = slice(r * TZ, r * TZ + TZ)
         load_pair(a, b, r, 0, tile[rows, :], from_y[rows, :])
-        for z, first in ((TZ, 0), (-16, edges.shape[0] // 2)):
-            rows = slice(first + r * 16, first + r * 16 + 16)
-            load_pair(a, b, r, z, edges[rows, :], from_c[rows, :])
+        for z, lower, upper in zip((TZ, -16), edges, corners):
+            rows = slice(r * 16, r * 16 + 16)
+            load_pair(a, b, r, z, lower[rows, :], upper[rows, :])
 
 
 def load_left(flags, state, from_y, a, b):
@@ -289,11 +289,11 @@
         k[r, Z0 - 8 : Z0 + 40, :] = jnp.where(given, rows, pltpu.roll(speeds[r, 8:56, :], 32, 1))
 
 
-def round_one(tile, from_y, edges, from_c, planes, state, msg, speeds, a, b, k, m):
+def round_one(tile, from_y, after, before, corner, other, planes, state, msg, speeds, a, b, k, m):
     clear(a, b, -16, 48)
-    load_right(a, b, tile, from_y, edges, from_c)
+    load_right(a, b, tile, from_y, (after, before), (corner, other))
     for lower, upper, first, z, count in (
-        (tile, from_y, 512, 0, TZ), (edges, from_c, 256, TZ, 16), (edges, from_c, 640, -16, 16)
+        (tile, from_y, 512, 0, TZ), (after, corner, 256, TZ, 16), (before, other, 256, -16, 16)
     ):
         for r in range(8):
             rows = slice(first + r * count, first + r * count + count)
@@ -325,9 +325,9 @@
         far[r * 16 : r * 16 + 16, :] = rows[16:]
 
 
-def round_three(tile, from_y, edges, from_c, planes, speeds, state, msg, a, b, k, m):
+def round_three(tile, from_y, after, before, corner, other, planes, speeds, state, msg, a, b, k, m):
     clear(a, b, -16, 48)
-    load_right(a, b, tile, from_y, edges, from_c)
+    load_right(a, b, tile, from_y, (after, before), (corner, other))
     for r in range(ROWS):
         k[r, Z0 - 16 : Z0 + 48, :] = speeds[r]
     advance(a, b, k, m, planes, 2, -16, 48)
@@ -416,8 +416,9 @@
     def around(near, far):
         after = moved(near, 0, 1)
         before = moved(far, 0, -1)
-        edges = jnp.concatenate([after, before], axis=0)
-        return edges, moved(edges, 1, 0)
+        corner = moved(after, 1, 0)
+        other = moved(before, 1, 0)
+        return after, before, corner, other
 
     tile, near, far = call(unpack_kernel, [(768, 128), (384, 128), (384, 128)], got)
     from_y = moved(tile, 1, 0)
@@ -428,12 +429,12 @@
     works = jnp.stack([zh == 0] + firsts).astype(jnp.int32)
     (planes,) = call(source_kernel, [(8, ROWS * 4, 128)], got, flags=works, cost=20_000_000)
     planes = lax.all_to_all(planes, ("core", "gz"), 0, 0, tiled=True)
-    edges, from_c = around(near, far)
+    edges = around(near, far)
     first_y = (ty == 0).astype(jnp.int32)[None]
 
     state, msg, speeds = call(
         round_one, [(2 * ROWS, 48, 128), (960, 128), (ROWS, 64, 128)],
-        tile, from_y, edges, from_c, planes, scratch=True,
+        tile, from_y, *edges, planes, scratch=True,
     )
     above = moved(msg, -1, 0)
     tile, near, far = call(
@@ -441,10 +442,10 @@
         state, above, planes, speeds, flags=first_y, scratch=True,
     )
     from_y = moved(tile, 1, 0)
-    edges, from_c = around(near, far)
+    edges = around(near, far)
     state, msg = call(
         round_three, [(2 * ROWS, 48, 128), (768, 128)],
-        tile, from_y, edges, from_c, planes, speeds, scratch=True,
+        tile, from_y, *edges, planes, speeds, scratch=True,
     )
     (out,) = call(
         round_four, [(256, 128)],

time: 185 us -> 179 us (0.968)
  the two profiles are of different devices: /device:TPU:8 before, /device:TPU:4 now
where the time goes in v5:
time: 179 us
  blocking collectives  83.8 us (47%)
  starting transfers between devices  43.2 us (24%)
  waiting for transfers between devices  29.2 us (16%)
  Pallas kernels  21.7 us (12%)
    all_to_all x1, blocking collectives, local(): lax.all_to_all(packed, ('zh', 'yc'), 0, 0, tiled=True)  50.2 us
    ppermute x12, starting transfers between devices, moved(): return lax.ppermute(array, AXES, pairs_along(dy, dz))  35.1 us
    all_to_all x1, blocking collectives, local(): lax.all_to_all(out.reshape(16, 16, 128), ('zh', 'yc'), 0, 0, tiled=True)  33.6 us
    ppermute x12, waiting for transfers between devices, moved(): return lax.ppermute(array, AXES, pairs_along(dy, dz))  27.4 us
    pallas_call x7, Pallas kernels, call(): pl.pallas_call(kernel, out_shape=shapes, in_specs=specs, out_specs=[VM] *...  19.3 us
    all_to_all x1, starting transfers between devices, local(): planes = lax.all_to_all(planes, ('core', 'gz'), 0, 0, tiled=True)  8.19 us
  transfers between devices with their start and end apart: 13, of which 8 were waited for; matrix products, arithmetic and copies ran while one was open for 0% of the time, Pallas kernels for 3%

profile of v5, /device:TPU:4, one launch (start us, length us, event | category | flops | bytes accessed | tf_op | source)
XLA Modules:
  0.0 178.8 jit_solution(9401886482380485703)
XLA Ops:
  0.0 0.6 stack.38.flags
  0.6 2.3 %pack.1 = f32[16,72,128]{2,1,0:T(8,128)} custom-call(s32[5]{0:T(128)} %stack.38.flags, f32[16]{0:T(128)} %table.1, f32[4,64,128]{2,1,0:T(8,128)} %now.1, f32[4,64,128]{2,1,0:T(8,128)} %prev.1, f32[4,64,128]{2,1,0:T(8,128)} %courant.1, s32[2,32]{1,0:T(2,128)} %tops.1, s32[2,32]{1,0:T(2,128)} %thicks.1, bf16[32,512]{1,0:T(8,128)(2,1)} %bitcast.17, ...), custom_call_target="tpu_custom_call" | custom-call | tf_op jit(solution)/shard_map/pack/pallas_call | solution.py:399
  3.0 50.2 %all_to_all.15 = f32[16,72,128]{2,1,0:T(8,128)S(1)} all-to-all(f32[16,72,128]{2,1,0:T(8,128)} %pack.1), channel_id=1, replica_groups=mesh['zh'=4,'yc'=4,'zl'=4,'core'=2,'gz'=4] {'zh','yc'}, dimensions={0} | all-to-all | bytes 1179648 | tf_op jit(solution)/shard_map/all_to_all | solution.py:410
  53.1 0.3 shard_map.91
  53.4 2.4 %collective-permute-start.1 = (f32[384,128]{1,0:T(8,128)S(1)}, f32[384,128]{1,0:T(8,128)S(1)}, u32[]{:S(2)}, u32[]{:S(2)}) collective-permute-start(f32[384,128]{1,0:T(8,128)S(1)} %get-tuple-element.17), channel_id=1, source_target_pairs={{128,0},{256,128},{384,256},{385,384},{257,385},{129,257},{1,129},... | collective-permute-start | bytes 589832 | tf_op jit(solution)/shard_map/ppermute | solution.py:413
  55.9 1.3 collective-permute-start
  57.2 7.4 %collective-permute-start.2 = (f32[384,128]{1,0:T(8,128)S(1)}, f32[384,128]{1,0:T(8,128)S(1)}, u32[]{:S(2)}, u32[]{:S(2)}) collective-permute-start(f32[384,128]{1,0:T(8,128)S(1)} %get-tuple-element.18), channel_id=1, source_target_pairs={{0,128},{128,256},{256,384},{384,385},{385,257},{257,129},{129,1},... | collective-permute-start | bytes 589832 | tf_op jit(solution)/shard_map/ppermute | solution.py:413
  64.6 0.1 pad_add_fusion.flags
  64.7 5.1 %shard_map.92 = f32[8,64,128]{2,1,0:T(8,128)} custom-call(s32[3]{0:T(128)S(1)} %pad_add_fusion.flags, f32[1152,128]{1,0:T(8,128)S(1)} %bitcast.15), custom_call_target="tpu_custom_call" | custom-call | flops 20000000 | bytes 1000000 | tf_op jit(solution)/shard_map/pallas_call | solution.py:372
  69.9 8.2 %all-to-all-start.1 = ((f32[8,64,128]{2,1,0:T(8,128)}), f32[8,64,128]{2,1,0:T(8,128)S(1)}, u32[]{:S(2)}, u32[]{:S(2)}) async-start(f32[8,64,128]{2,1,0:T(8,128)} %shard_map.92), calls=%async_computation.1 | async-start | bytes 524288 | tf_op jit(solution)/shard_map/all_to_all | solution.py:431
  78.0 0.0 collective-permute-done.1.after
  78.1 1.3 collective-permute-start.3
  79.3 0.0 collective-permute-done.2.before
  79.4 1.3 collective-permute-start.4
  80.7 1.8 all-to-all-done.1.planes
  82.4 0.0 collective-permute-done.from_y
  82.4 3.2 %collective-permute-done.3.corner = f32[384,128]{1,0:T(8,128)S(1)} collective-permute-done((f32[384,128]{1,0:T(8,128)S(1)}, f32[384,128]{1,0:T(8,128)S(1)}, u32[]{:S(2)}, u32[]{:S(2)}) %collective-permute-start.3) | collective-permute-done | bytes 196640 | tf_op jit(solution)/shard_map/ppermute | solution.py:413
  85.6 2.1 %collective-permute-done.4.other = f32[384,128]{1,0:T(8,128)S(1)} collective-permute-done((f32[384,128]{1,0:T(8,128)S(1)}, f32[384,128]{1,0:T(8,128)S(1)}, u32[]{:S(2)}, u32[]{:S(2)}) %collective-permute-start.4) | collective-permute-done | bytes 196640 | tf_op jit(solution)/shard_map/ppermute | solution.py:413
  87.7 4.5 %shard_map.93 = (f32[32,48,128]{2,1,0:T(8,128)S(1)}, f32[960,128]{1,0:T(8,128)}, f32[16,64,128]{2,1,0:T(8,128)S(1)}) custom-call(f32[768,128]{1,0:T(8,128)S(1)} %get-tuple-element.16.tile, f32[768,128]{1,0:T(8,128)S(1)} %collective-permute-done.from_y, f32[384,128]{1,0:T(8,128)S(1)} %collective-permute-done.1.after, ...), custom_call_target="tpu_custom_call" | custom-call | flops 2000000 | bytes 1000000 | tf_op jit(solution)/shard_map/pallas_call | solution.py:372
  92.2 3.8 %collective-permute-start.5 = (f32[960,128]{1,0:T(8,128)}, f32[960,128]{1,0:T(8,128)S(1)}, u32[]{:S(2)}, u32[]{:S(2)}) collective-permute-start(f32[960,128]{1,0:T(8,128)} %get-tuple-element.20), channel_id=1, source_target_pairs={{0,32},{128,160},{256,288},{384,416},{385,417},{257,289},{129,161}... | collective-permute-start | bytes 1474568 | tf_op jit(solution)/shard_map/ppermute | solution.py:413
  96.0 6.6 %collective-permute-done.5.from_y.above = f32[960,128]{1,0:T(8,128)S(1)} collective-permute-done((f32[960,128]{1,0:T(8,128)}, f32[960,128]{1,0:T(8,128)S(1)}, u32[]{:S(2)}, u32[]{:S(2)}) %collective-permute-start.5) | collective-permute-done | bytes 491552 | tf_op jit(solution)/shard_map/ppermute | solution.py:413
  102.6 2.6 %shard_map.94 = (f32[512,128]{1,0:T(8,128)S(1)}, f32[256,128]{1,0:T(8,128)S(1)}, f32[256,128]{1,0:T(8,128)S(1)}) custom-call(s32[1]{0:T(128)} %bitcast.5.flags, f32[32,48,128]{2,1,0:T(8,128)S(1)} %get-tuple-element.19.state, f32[960,128]{1,0:T(8,128)S(1)} %collective-permute-done.5.from_y.above, f32[8,64,128]{2,1,0:T(8,128)S(1)} %all-to-all-done.1.planes, ...), custom_call_target="tpu_custom_call" | custom-call | flops 2000000 | bytes 1000000 | tf_op jit(solution)/shard_map/pallas_call | solution.py:372
  105.1 4.6 %collective-permute-start.7 = (f32[256,128]{1,0:T(8,128)S(1)}, f32[256,128]{1,0:T(8,128)S(1)}, u32[]{:S(2)}, u32[]{:S(2)}) collective-permute-start(f32[256,128]{1,0:T(8,128)S(1)} %get-tuple-element.23), channel_id=1, source_target_pairs={{128,0},{256,128},{384,256},{385,384},{257,385},{129,257},{1,129},... | collective-permute-start | bytes 393224 | tf_op jit(solution)/shard_map/ppermute | solution.py:413
  109.8 5.2 %collective-permute-start.8 = (f32[256,128]{1,0:T(8,128)S(1)}, f32[256,128]{1,0:T(8,128)S(1)}, u32[]{:S(2)}, u32[]{:S(2)}) collective-permute-start(f32[256,128]{1,0:T(8,128)S(1)} %get-tuple-element.24), channel_id=1, source_target_pairs={{0,128},{128,256},{256,384},{384,385},{385,257},{257,129},{129,1},... | collective-permute-start | bytes 393224 | tf_op jit(solution)/shard_map/ppermute | solution.py:413
  114.9 1.3 collective-permute-start.6
  116.2 3.6 %collective-permute-done.7.after = f32[256,128]{1,0:T(8,128)S(1)} collective-permute-done((f32[256,128]{1,0:T(8,128)S(1)}, f32[256,128]{1,0:T(8,128)S(1)}, u32[]{:S(2)}, u32[]{:S(2)}) %collective-permute-start.7) | collective-permute-done | bytes 131104 | tf_op jit(solution)/shard_map/ppermute | solution.py:413
  119.9 1.3 collective-permute-start.9
  121.1 0.0 collective-permute-done.8.before
  121.1 1.3 collective-permute-start.10
  122.4 4.7 %collective-permute-done.9.corner = f32[256,128]{1,0:T(8,128)S(1)} collective-permute-done((f32[256,128]{1,0:T(8,128)S(1)}, f32[256,128]{1,0:T(8,128)S(1)}, u32[]{:S(2)}, u32[]{:S(2)}) %collective-permute-start.9) | collective-permute-done | bytes 131104 | tf_op jit(solution)/shard_map/ppermute | solution.py:413
  127.2 1.9 %collective-permute-done.10.other = f32[256,128]{1,0:T(8,128)S(1)} collective-permute-done((f32[256,128]{1,0:T(8,128)S(1)}, f32[256,128]{1,0:T(8,128)S(1)}, u32[]{:S(2)}, u32[]{:S(2)}) %collective-permute-start.10) | collective-permute-done | bytes 131104 | tf_op jit(solution)/shard_map/ppermute | solution.py:413
  129.1 0.0 collective-permute-done.6.from_y
  129.1 3.0 %shard_map.95 = (f32[32,48,128]{2,1,0:T(8,128)S(1)}, f32[768,128]{1,0:T(8,128)S(1)}) custom-call(f32[512,128]{1,0:T(8,128)S(1)} %get-tuple-element.22.tile, f32[512,128]{1,0:T(8,128)S(1)} %collective-permute-done.6.from_y, f32[256,128]{1,0:T(8,128)S(1)} %collective-permute-done.7.after, f32[256,128]{1,0:T(8,128)S(1)} %collective-permute-done.8.before, ...), custom_call_target="tpu_custom_call" | custom-call | flops 2000000 | bytes 1000000 | tf_op jit(solution)/shard_map/pallas_call | solution.py:372
  132.1 3.9 %collective-permute-start.11 = (f32[768,128]{1,0:T(8,128)S(1)}, f32[768,128]{1,0:T(8,128)S(1)}, u32[]{:S(2)}, u32[]{:S(2)}) collective-permute-start(f32[768,128]{1,0:T(8,128)S(1)} %get-tuple-element.26), channel_id=1, source_target_pairs={{0,32},{128,160},{256,288},{384,416},{385,417},{257,289},{129,161}... | collective-permute-start | bytes 1179656 | tf_op jit(solution)/shard_map/ppermute | solution.py:413
  136.1 5.3 %collective-permute-done.11.from_y = f32[768,128]{1,0:T(8,128)S(1)} collective-permute-done((f32[768,128]{1,0:T(8,128)S(1)}, f32[768,128]{1,0:T(8,128)S(1)}, u32[]{:S(2)}, u32[]{:S(2)}) %collective-permute-start.11) | collective-permute-done | bytes 393248 | tf_op jit(solution)/shard_map/ppermute | solution.py:413
  141.3 2.5 %shard_map.96 = f32[256,128]{1,0:T(8,128)S(1)} custom-call(s32[1]{0:T(128)} %bitcast.5.flags, f32[32,48,128]{2,1,0:T(8,128)S(1)} %get-tuple-element.25.state, f32[768,128]{1,0:T(8,128)S(1)} %collective-permute-done.11.from_y, f32[8,64,128]{2,1,0:T(8,128)S(1)} %all-to-all-done.1.planes, f32[16,64,128]{2,1,0:T(8,128)S(1)} %get-tuple-element.21.speeds, ...), custom_call_target="tpu_custom_call" | custom-call | flops 2000000 | bytes 1000000 | tf_op jit(solution)/shard_map/pallas_call | solution.py:372
  143.8 0.0 copy-start
  143.8 33.6 %all_to_all.16.got = f32[16,16,128]{2,1,0:T(8,128)S(1)} all-to-all(f32[16,16,128]{2,1,0:T(8,128)S(1)} %bitcast.16), channel_id=1, replica_groups=mesh['zh'=4,'yc'=4,'zl'=4,'core'=2,'gz'=4] {'zh','yc'}, dimensions={0} | all-to-all | bytes 262144 | tf_op jit(solution)/shard_map/all_to_all | solution.py:454
  177.4 0.0 copy-done
  177.4 1.4 shard_map.97
Async XLA Ops:
  53.4 24.6 %collective-permute-start.1 = (f32[384,128]{1,0:T(8,128)S(1)}, f32[384,128]{1,0:T(8,128)S(1)}, u32[]{:S(2)}, u32[]{:S(2)}) collective-permute-start(f32[384,128]{1,0:T(8,128)S(1)} %get-tuple-element.17), channel_id=1, source_target_pairs={{128,0},{256,128},{384,256},{385,384},{257,385},{129,257},{1,129},... | collective-permute-start | bytes 589832 | tf_op jit(solution)/shard_map/ppermute | solution.py:413
  55.9 26.6 %collective-permute-start = (f32[768,128]{1,0:T(8,128)S(1)}, f32[768,128]{1,0:T(8,128)S(1)}, u32[]{:S(2)}, u32[]{:S(2)}) collective-permute-start(f32[768,128]{1,0:T(8,128)S(1)} %get-tuple-element.16.tile), channel_id=1, source_target_pairs={{32,0},{160,128},{288,256},{416,384},{417,385},{289,257},{161,129}... | collective-permute-start | bytes 1179656 | tf_op jit(solution)/shard_map/ppermute | solution.py:413
  57.2 22.2 %collective-permute-start.2 = (f32[384,128]{1,0:T(8,128)S(1)}, f32[384,128]{1,0:T(8,128)S(1)}, u32[]{:S(2)}, u32[]{:S(2)}) collective-permute-start(f32[384,128]{1,0:T(8,128)S(1)} %get-tuple-element.18), channel_id=1, source_target_pairs={{0,128},{128,256},{256,384},{384,385},{385,257},{257,129},{129,1},... | collective-permute-start | bytes 589832 | tf_op jit(solution)/shard_map/ppermute | solution.py:413
  69.9 12.6 %all-to-all-start.1 = ((f32[8,64,128]{2,1,0:T(8,128)}), f32[8,64,128]{2,1,0:T(8,128)S(1)}, u32[]{:S(2)}, u32[]{:S(2)}) async-start(f32[8,64,128]{2,1,0:T(8,128)} %shard_map.92), calls=%async_computation.1 | async-start | bytes 524288 | tf_op jit(solution)/shard_map/all_to_all | solution.py:431
  78.1 7.6 %collective-permute-start.3 = (f32[384,128]{1,0:T(8,128)S(1)}, f32[384,128]{1,0:T(8,128)S(1)}, u32[]{:S(2)}, u32[]{:S(2)}) collective-permute-start(f32[384,128]{1,0:T(8,128)S(1)} %collective-permute-done.1.after), channel_id=1, source_target_pairs={{32,0},{160,128},{288,256},{416,384},{417,385},{289,257},{161,129}... | collective-permute-start | bytes 589832 | tf_op jit(solution)/shard_map/ppermute | solution.py:413
  79.4 8.4 %collective-permute-start.4 = (f32[384,128]{1,0:T(8,128)S(1)}, f32[384,128]{1,0:T(8,128)S(1)}, u32[]{:S(2)}, u32[]{:S(2)}) collective-permute-start(f32[384,128]{1,0:T(8,128)S(1)} %collective-permute-done.2.before), channel_id=1, source_target_pairs={{32,0},{160,128},{288,256},{416,384},{417,385},{289,257},{161,129}... | collective-permute-start | bytes 589832 | tf_op jit(solution)/shard_map/ppermute | solution.py:413
  92.2 10.4 %collective-permute-start.5 = (f32[960,128]{1,0:T(8,128)}, f32[960,128]{1,0:T(8,128)S(1)}, u32[]{:S(2)}, u32[]{:S(2)}) collective-permute-start(f32[960,128]{1,0:T(8,128)} %get-tuple-element.20), channel_id=1, source_target_pairs={{0,32},{128,160},{256,288},{384,416},{385,417},{257,289},{129,161}... | collective-permute-start | bytes 1474568 | tf_op jit(solution)/shard_map/ppermute | solution.py:413
  105.1 14.7 %collective-permute-start.7 = (f32[256,128]{1,0:T(8,128)S(1)}, f32[256,128]{1,0:T(8,128)S(1)}, u32[]{:S(2)}, u32[]{:S(2)}) collective-permute-start(f32[256,128]{1,0:T(8,128)S(1)} %get-tuple-element.23), channel_id=1, source_target_pairs={{128,0},{256,128},{384,256},{385,384},{257,385},{129,257},{1,129},... | collective-permute-start | bytes 393224 | tf_op jit(solution)/shard_map/ppermute | solution.py:413
  109.8 11.4 %collective-permute-start.8 = (f32[256,128]{1,0:T(8,128)S(1)}, f32[256,128]{1,0:T(8,128)S(1)}, u32[]{:S(2)}, u32[]{:S(2)}) collective-permute-start(f32[256,128]{1,0:T(8,128)S(1)} %get-tuple-element.24), channel_id=1, source_target_pairs={{0,128},{128,256},{256,384},{384,385},{385,257},{257,129},{129,1},... | collective-permute-start | bytes 393224 | tf_op jit(solution)/shard_map/ppermute | solution.py:413
  114.9 14.2 %collective-permute-start.6 = (f32[512,128]{1,0:T(8,128)S(1)}, f32[512,128]{1,0:T(8,128)S(1)}, u32[]{:S(2)}, u32[]{:S(2)}) collective-permute-start(f32[512,128]{1,0:T(8,128)S(1)} %get-tuple-element.22.tile), channel_id=1, source_target_pairs={{32,0},{160,128},{288,256},{416,384},{417,385},{289,257},{161,129}... | collective-permute-start | bytes 786440 | tf_op jit(solution)/shard_map/ppermute | solution.py:413
  119.9 7.3 %collective-permute-start.9 = (f32[256,128]{1,0:T(8,128)S(1)}, f32[256,128]{1,0:T(8,128)S(1)}, u32[]{:S(2)}, u32[]{:S(2)}) collective-permute-start(f32[256,128]{1,0:T(8,128)S(1)} %collective-permute-done.7.after), channel_id=1, source_target_pairs={{32,0},{160,128},{288,256},{416,384},{417,385},{289,257},{161,129}... | collective-permute-start | bytes 393224 | tf_op jit(solution)/shard_map/ppermute | solution.py:413
  121.1 8.0 %collective-permute-start.10 = (f32[256,128]{1,0:T(8,128)S(1)}, f32[256,128]{1,0:T(8,128)S(1)}, u32[]{:S(2)}, u32[]{:S(2)}) collective-permute-start(f32[256,128]{1,0:T(8,128)S(1)} %collective-permute-done.8.before), channel_id=1, source_target_pairs={{32,0},{160,128},{288,256},{416,384},{417,385},{289,257},{161,129}... | collective-permute-start | bytes 393224 | tf_op jit(solution)/shard_map/ppermute | solution.py:413
  132.1 9.2 %collective-permute-start.11 = (f32[768,128]{1,0:T(8,128)S(1)}, f32[768,128]{1,0:T(8,128)S(1)}, u32[]{:S(2)}, u32[]{:S(2)}) collective-permute-start(f32[768,128]{1,0:T(8,128)S(1)} %get-tuple-element.26), channel_id=1, source_target_pairs={{0,32},{128,160},{256,288},{384,416},{385,417},{257,289},{129,161}... | collective-permute-start | bytes 1179656 | tf_op jit(solution)/shard_map/ppermute | solution.py:413
  143.8 33.6 %copy-start = (s32[5]{0:T(128)S(1)}, s32[5]{0:T(128)}, u32[]{:S(2)}) copy-start(s32[5]{0:T(128)} %stack.38.flags) | copy-start | bytes 64

commit v6 on v5

--- a/solution.py
+++ b/solution.py
@@ -127,8 +127,9 @@
         far[r * 16 : r * 16 + 16, :] = tile[r * 32 + 16 : r * 32 + 32, :]
 
 
-def source_kernel(flags, got, out):
-    out[...] = jnp.zeros_like(out)
+def source_kernel(flags, got, out, mine, other):
+    for ref in (out, mine, other):
+        ref[...] = jnp.zeros_like(ref)
 
     @pl.when(flags[0] == 1)
     def _():
@@ -166,8 +167,10 @@
 
         total = lax.fori_loop(0, 16, shard, jnp.zeros((ROWS * 8, 256), F32))
         total = total[: ROWS * 4] + total[ROWS * 4 :]
-        out[0] = total[:, :128]
-        out[4] = total[:, 128:]
+        out[4 * flags[3]] = total[:, :128]
+        out[4 - 4 * flags[3]] = total[:, 128:]
+        mine[...] = total[:, :128]
+        other[...] = total[:, 128:]
 
 
 def swap(rows):
@@ -289,7 +292,12 @@
         k[r, Z0 - 8 : Z0 + 40, :] = jnp.where(given, rows, pltpu.roll(speeds[r, 8:56, :], 32, 1))
 
 
-def round_one(tile, from_y, after, before, corner, other, planes, state, msg, speeds, a, b, k, m):
+def round_one(
+    flags, tile, from_y, after, before, corner, other, mine, others, state, msg, speeds, a, b, k, m, planes
+):
+    shown = flags[1].astype(F32)
+    planes[4 * flags[0]] = mine[...] * shown
+    planes[4 - 4 * flags[0]] = others[...] * shown
     clear(a, b, -16, 48)
     load_right(a, b, tile, from_y, (after, before), (corner, other))
     for lower, upper, first, z, count in (
@@ -374,7 +382,10 @@
         out_shape=shapes,
         in_specs=specs,
         out_specs=[VM] * len(outs),
-        scratch_shapes=[pltpu.VMEM((ROWS, WZ, 128), F32)] * 4 if scratch else [],
+        scratch_shapes=(
+            [pltpu.VMEM((ROWS, WZ, 128), F32)] * 4 * scratch
+            + [pltpu.VMEM((8, ROWS * 4, 128), F32)] * (kernel is round_one)
+        ),
         compiler_params=pltpu.CompilerParams(vmem_limit_bytes=48 * 1024 * 1024),
         cost_estimate=pl.CostEstimate(flops=cost, bytes_accessed=1_000_000, transcendentals=0),
     )(*args)
@@ -426,15 +437,21 @@
         zl * 128 - 8 * (gz % 2) + 16 * ((yc - zl) % 4),
         zl * 128 - 8 * (gz % 2) + 64 + 16 * ((zl - yc) % 4),
     ]
-    works = jnp.stack([zh == 0] + firsts).astype(jnp.int32)
-    (planes,) = call(source_kernel, [(8, ROWS * 4, 128)], got, flags=works, cost=20_000_000)
+    firsts = [jnp.where(core == 0, *firsts), jnp.where(core == 0, *firsts[::-1])]
+    works = jnp.stack([zh == 0] + firsts + [core]).astype(jnp.int32)
+    planes, mine, others = call(
+        source_kernel, [(8, ROWS * 4, 128), (ROWS * 4, 128), (ROWS * 4, 128)],
+        got, flags=works, cost=20_000_000,
+    )
+    others = lax.ppermute(others, "core", [(0, 1), (1, 0)])
     planes = lax.all_to_all(planes, ("core", "gz"), 0, 0, tiled=True)
     edges = around(near, far)
+    surface = jnp.stack([core, gz == 0]).astype(jnp.int32)
     first_y = (ty == 0).astype(jnp.int32)[None]
 
     state, msg, speeds = call(
         round_one, [(2 * ROWS, 48, 128), (960, 128), (ROWS, 64, 128)],
-        tile, from_y, *edges, planes, scratch=True,
+        tile, from_y, *edges, mine, others, flags=surface, scratch=True,
     )
     above = moved(msg, -1, 0)
     tile, near, far = call(

time: 179 us -> 181 us (1.011)
  the two profiles are of different devices: /device:TPU:4 before, /device:TPU:96 now
where the time goes in v6:
time: 181 us; the launch traced here: 180 us
  blocking collectives  72.8 us (40%)
  starting transfers between devices  58.6 us (32%)
  waiting for transfers between devices  26.3 us (15%)
  Pallas kernels  21.4 us (12%)
    ppermute x12, starting transfers between devices, moved(): return lax.ppermute(array, AXES, pairs_along(dy, dz))  52.4 us
    all_to_all x1, blocking collectives, local(): lax.all_to_all(packed, ('zh', 'yc'), 0, 0, tiled=True)  49.1 us
    all_to_all x1, blocking collectives, local(): lax.all_to_all(out.reshape(16, 16, 128), ('zh', 'yc'), 0, 0, tiled=True)  23.7 us
    pallas_call x7, Pallas kernels, call(): pl.pallas_call(kernel, out_shape=shapes, in_specs=specs, out_specs=[VM] *...  19.1 us
    ppermute x12, waiting for transfers between devices, moved(): return lax.ppermute(array, AXES, pairs_along(dy, dz))  18.3 us
    all_to_all x1, waiting for transfers between devices, local(): planes = lax.all_to_all(planes, ('core', 'gz'), 0, 0, tiled=True)  6.86 us
    all_to_all x1, starting transfers between devices, local(): planes = lax.all_to_all(planes, ('core', 'gz'), 0, 0, tiled=True)  4.31 us
  transfers between devices with their start and end apart: 14, of which 6 were waited for; matrix products, arithmetic and copies ran while one was open for 0% of the time, Pallas kernels for 3%

profile of v6, /device:TPU:96, one launch (start us, length us, event | category | flops | bytes accessed | tf_op | source)
XLA Modules:
  0.0 180.2 jit_solution(11736048141635399594)
XLA Ops:
  0.0 0.7 stack.49.flags
  0.7 2.3 %pack.1 = f32[16,72,128]{2,1,0:T(8,128)} custom-call(s32[5]{0:T(128)} %stack.49.flags, f32[16]{0:T(128)} %table.1, f32[4,64,128]{2,1,0:T(8,128)} %now.1, f32[4,64,128]{2,1,0:T(8,128)} %prev.1, f32[4,64,128]{2,1,0:T(8,128)} %courant.1, s32[2,32]{1,0:T(2,128)} %tops.1, s32[2,32]{1,0:T(2,128)} %thicks.1, bf16[32,512]{1,0:T(8,128)(2,1)} %bitcast.18, ...), custom_call_target="tpu_custom_call" | custom-call | tf_op jit(solution)/shard_map/pack/pallas_call | solution.py:410
  3.0 49.1 %all_to_all.15 = f32[16,72,128]{2,1,0:T(8,128)S(1)} all-to-all(f32[16,72,128]{2,1,0:T(8,128)} %pack.1), channel_id=1, replica_groups=mesh['zh'=4,'yc'=4,'zl'=4,'core'=2,'gz'=4] {'zh','yc'}, dimensions={0} | all-to-all | bytes 1179648 | tf_op jit(solution)/shard_map/all_to_all | solution.py:421
  52.1 0.3 shard_map.91
  52.4 1.3 collective-permute-start.1
  53.7 8.5 %collective-permute-start.2 = (f32[384,128]{1,0:T(8,128)S(1)}, f32[384,128]{1,0:T(8,128)S(1)}, u32[]{:S(2)}, u32[]{:S(2)}) collective-permute-start(f32[384,128]{1,0:T(8,128)S(1)} %get-tuple-element.21), channel_id=1, source_target_pairs={{0,128},{128,256},{256,384},{384,385},{385,257},{257,129},{129,1},... | collective-permute-start | bytes 589832 | tf_op jit(solution)/shard_map/ppermute | solution.py:424
  62.2 5.6 %collective-permute-start = (f32[768,128]{1,0:T(8,128)S(1)}, f32[768,128]{1,0:T(8,128)S(1)}, u32[]{:S(2)}, u32[]{:S(2)}) collective-permute-start(f32[768,128]{1,0:T(8,128)S(1)} %get-tuple-element.19.tile), channel_id=1, source_target_pairs={{32,0},{160,128},{288,256},{416,384},{417,385},{289,257},{161,129}... | collective-permute-start | bytes 1179656 | tf_op jit(solution)/shard_map/ppermute | solution.py:424
  67.9 0.0 collective-permute-done.1.after
  67.9 2.1 %collective-permute-start.3 = (f32[384,128]{1,0:T(8,128)S(1)}, f32[384,128]{1,0:T(8,128)S(1)}, u32[]{:S(2)}, u32[]{:S(2)}) collective-permute-start(f32[384,128]{1,0:T(8,128)S(1)} %collective-permute-done.1.after), channel_id=1, source_target_pairs={{32,0},{160,128},{288,256},{416,384},{417,385},{289,257},{161,129}... | collective-permute-start | bytes 589832 | tf_op jit(solution)/shard_map/ppermute | solution.py:424
  70.0 5.7 %collective-permute-done.2.before = f32[384,128]{1,0:T(8,128)S(1)} collective-permute-done((f32[384,128]{1,0:T(8,128)S(1)}, f32[384,128]{1,0:T(8,128)S(1)}, u32[]{:S(2)}, u32[]{:S(2)}) %collective-permute-start.2) | collective-permute-done | bytes 196640 | tf_op jit(solution)/shard_map/ppermute | solution.py:424
  75.7 6.4 %collective-permute-start.4 = (f32[384,128]{1,0:T(8,128)S(1)}, f32[384,128]{1,0:T(8,128)S(1)}, u32[]{:S(2)}, u32[]{:S(2)}) collective-permute-start(f32[384,128]{1,0:T(8,128)S(1)} %collective-permute-done.2.before), channel_id=1, source_target_pairs={{32,0},{160,128},{288,256},{416,384},{417,385},{289,257},{161,129}... | collective-permute-start | bytes 589832 | tf_op jit(solution)/shard_map/ppermute | solution.py:424
  82.1 0.1 pad_add_fusion.1.flags
  82.1 5.1 %shard_map.92 = (f32[8,64,128]{2,1,0:T(8,128)}, f32[64,128]{1,0:T(8,128)S(1)}, f32[64,128]{1,0:T(8,128)S(1)}) custom-call(s32[4]{0:T(128)S(1)} %pad_add_fusion.1.flags, f32[1152,128]{1,0:T(8,128)S(1)} %bitcast.16), custom_call_target="tpu_custom_call" | custom-call | flops 20000000 | bytes 1000000 | tf_op jit(solution)/shard_map/pallas_call | solution.py:380
  87.3 1.9 %collective-permute-start.5 = (f32[64,128]{1,0:T(8,128)S(1)}, f32[64,128]{1,0:T(8,128)S(1)}, u32[]{:S(2)}, u32[]{:S(2)}) collective-permute-start(f32[64,128]{1,0:T(8,128)S(1)} %get-tuple-element.23), channel_id=1, source_target_pairs={{0,4},{4,0},{1,5},{5,1},{2,6},{6,2},{3,7},{7,3},{8,12},{12,8},{9,1... | collective-permute-start | bytes 98312 | tf_op jit(solution)/shard_map/ppermute | solution.py:446
  89.2 0.1 pad_add_fusion.flags
  89.3 1.1 collective-permute-done.5.others
  90.4 0.0 collective-permute-done.from_y
  90.4 0.0 collective-permute-done.3.corner
  90.4 0.0 collective-permute-done.4.other
  90.4 4.2 %shard_map.93 = (f32[32,48,128]{2,1,0:T(8,128)S(1)}, f32[960,128]{1,0:T(8,128)S(1)}, f32[16,64,128]{2,1,0:T(8,128)S(1)}) custom-call(s32[2]{0:T(128)S(1)} %pad_add_fusion.flags, f32[768,128]{1,0:T(8,128)S(1)} %get-tuple-element.19.tile, f32[768,128]{1,0:T(8,128)S(1)} %collective-permute-done.from_y, f32[384,128]{1,0:T(8,128)S(1)} %collective-permute-done.1.after, ...), custom_call_target="tpu_custom_call" | custom-call | flops 2000000 | bytes 1000000 | tf_op jit(solution)/shard_map/pallas_call | solution.py:380
  94.6 1.9 %collective-permute-start.6 = (f32[960,128]{1,0:T(8,128)S(1)}, f32[960,128]{1,0:T(8,128)S(1)}, u32[]{:S(2)}, u32[]{:S(2)}) collective-permute-start(f32[960,128]{1,0:T(8,128)S(1)} %get-tuple-element.25), channel_id=1, source_target_pairs={{0,32},{128,160},{256,288},{384,416},{385,417},{257,289},{129,161}... | collective-permute-start | bytes 1474568 | tf_op jit(solution)/shard_map/ppermute | solution.py:424
  96.5 4.3 %all-to-all-start.1 = ((f32[8,64,128]{2,1,0:T(8,128)}), f32[8,64,128]{2,1,0:T(8,128)S(1)}, u32[]{:S(2)}, u32[]{:S(2)}) async-start(f32[8,64,128]{2,1,0:T(8,128)} %get-tuple-element.26), calls=%async_computation.1 | async-start | bytes 524288 | tf_op jit(solution)/shard_map/all_to_all | solution.py:447
  100.8 6.9 %all-to-all-done.1.planes = f32[8,64,128]{2,1,0:T(8,128)S(1)} async-done(((f32[8,64,128]{2,1,0:T(8,128)}), f32[8,64,128]{2,1,0:T(8,128)S(1)}, u32[]{:S(2)}, u32[]{:S(2)}) %all-to-all-start.1) | async-done | bytes 262176 | tf_op jit(solution)/shard_map/all_to_all | solution.py:447
  107.7 0.0 collective-permute-done.6.from_y.above
  107.7 2.6 %shard_map.94 = (f32[512,128]{1,0:T(8,128)S(1)}, f32[256,128]{1,0:T(8,128)S(1)}, f32[256,128]{1,0:T(8,128)S(1)}) custom-call(s32[1]{0:T(128)} %bitcast.5.flags, f32[32,48,128]{2,1,0:T(8,128)S(1)} %get-tuple-element.24.state, f32[960,128]{1,0:T(8,128)S(1)} %collective-permute-done.6.from_y.above, f32[8,64,128]{2,1,0:T(8,128)S(1)} %all-to-all-done.1.planes, ...), custom_call_target="tpu_custom_call" | custom-call | flops 2000000 | bytes 1000000 | tf_op jit(solution)/shard_map/pallas_call | solution.py:380
  110.3 1.3 collective-permute-start.8
  111.6 8.5 %collective-permute-start.9 = (f32[256,128]{1,0:T(8,128)S(1)}, f32[256,128]{1,0:T(8,128)S(1)}, u32[]{:S(2)}, u32[]{:S(2)}) collective-permute-start(f32[256,128]{1,0:T(8,128)S(1)} %get-tuple-element.30), channel_id=1, source_target_pairs={{0,128},{128,256},{256,384},{384,385},{385,257},{257,129},{129,1},... | collective-permute-start | bytes 393224 | tf_op jit(solution)/shard_map/ppermute | solution.py:424
  120.1 5.1 %collective-permute-start.7 = (f32[512,128]{1,0:T(8,128)S(1)}, f32[512,128]{1,0:T(8,128)S(1)}, u32[]{:S(2)}, u32[]{:S(2)}) collective-permute-start(f32[512,128]{1,0:T(8,128)S(1)} %get-tuple-element.28.tile), channel_id=1, source_target_pairs={{32,0},{160,128},{288,256},{416,384},{417,385},{289,257},{161,129}... | collective-permute-start | bytes 786440 | tf_op jit(solution)/shard_map/ppermute | solution.py:424
  125.2 0.0 collective-permute-done.8.after
  125.2 4.7 %collective-permute-start.10 = (f32[256,128]{1,0:T(8,128)S(1)}, f32[256,128]{1,0:T(8,128)S(1)}, u32[]{:S(2)}, u32[]{:S(2)}) collective-permute-start(f32[256,128]{1,0:T(8,128)S(1)} %collective-permute-done.8.after), channel_id=1, source_target_pairs={{32,0},{160,128},{288,256},{416,384},{417,385},{289,257},{161,129}... | collective-permute-start | bytes 393224 | tf_op jit(solution)/shard_map/ppermute | solution.py:424
  129.9 1.4 collective-permute-done.9.before
  131.4 4.4 %collective-permute-start.11 = (f32[256,128]{1,0:T(8,128)S(1)}, f32[256,128]{1,0:T(8,128)S(1)}, u32[]{:S(2)}, u32[]{:S(2)}) collective-permute-start(f32[256,128]{1,0:T(8,128)S(1)} %collective-permute-done.9.before), channel_id=1, source_target_pairs={{32,0},{160,128},{288,256},{416,384},{417,385},{289,257},{161,129}... | collective-permute-start | bytes 393224 | tf_op jit(solution)/shard_map/ppermute | solution.py:424
  135.8 0.0 collective-permute-done.10.corner
  135.8 2.5 %collective-permute-done.11.other = f32[256,128]{1,0:T(8,128)S(1)} collective-permute-done((f32[256,128]{1,0:T(8,128)S(1)}, f32[256,128]{1,0:T(8,128)S(1)}, u32[]{:S(2)}, u32[]{:S(2)}) %collective-permute-start.11) | collective-permute-done | bytes 131104 | tf_op jit(solution)/shard_map/ppermute | solution.py:424
  138.3 0.0 collective-permute-done.7.from_y
  138.3 3.0 %shard_map.95 = (f32[32,48,128]{2,1,0:T(8,128)S(1)}, f32[768,128]{1,0:T(8,128)S(1)}) custom-call(f32[512,128]{1,0:T(8,128)S(1)} %get-tuple-element.28.tile, f32[512,128]{1,0:T(8,128)S(1)} %collective-permute-done.7.from_y, f32[256,128]{1,0:T(8,128)S(1)} %collective-permute-done.8.after, f32[256,128]{1,0:T(8,128)S(1)} %collective-permute-done.9.before, ...), custom_call_target="tpu_custom_call" | custom-call | flops 2000000 | bytes 1000000 | tf_op jit(solution)/shard_map/pallas_call | solution.py:380
  141.3 2.6 %collective-permute-start.12 = (f32[768,128]{1,0:T(8,128)S(1)}, f32[768,128]{1,0:T(8,128)S(1)}, u32[]{:S(2)}, u32[]{:S(2)}) collective-permute-start(f32[768,128]{1,0:T(8,128)S(1)} %get-tuple-element.32), channel_id=1, source_target_pairs={{0,32},{128,160},{256,288},{384,416},{385,417},{257,289},{129,161}... | collective-permute-start | bytes 1179656 | tf_op jit(solution)/shard_map/ppermute | solution.py:424
  143.9 8.7 %collective-permute-done.12.from_y = f32[768,128]{1,0:T(8,128)S(1)} collective-permute-done((f32[768,128]{1,0:T(8,128)S(1)}, f32[768,128]{1,0:T(8,128)S(1)}, u32[]{:S(2)}, u32[]{:S(2)}) %collective-permute-start.12) | collective-permute-done | bytes 393248 | tf_op jit(solution)/shard_map/ppermute | solution.py:424
  152.6 2.5 %shard_map.96 = f32[256,128]{1,0:T(8,128)S(1)} custom-call(s32[1]{0:T(128)} %bitcast.5.flags, f32[32,48,128]{2,1,0:T(8,128)S(1)} %get-tuple-element.31.state, f32[768,128]{1,0:T(8,128)S(1)} %collective-permute-done.12.from_y, f32[8,64,128]{2,1,0:T(8,128)S(1)} %all-to-all-done.1.planes, f32[16,64,128]{2,1,0:T(8,128)S(1)} %get-tuple-element.27.speeds, ...), custom_call_target="tpu_custom_call" | custom-call | flops 2000000 | bytes 1000000 | tf_op jit(solution)/shard_map/pallas_call | solution.py:380
  155.1 0.0 copy-start
  155.1 23.7 %all_to_all.16.got = f32[16,16,128]{2,1,0:T(8,128)S(1)} all-to-all(f32[16,16,128]{2,1,0:T(8,128)S(1)} %bitcast.17), channel_id=1, replica_groups=mesh['zh'=4,'yc'=4,'zl'=4,'core'=2,'gz'=4] {'zh','yc'}, dimensions={0} | all-to-all | bytes 262144 | tf_op jit(solution)/shard_map/all_to_all | solution.py:471
  178.9 0.0 copy-done
  178.9 1.4 shard_map.97
Async XLA Ops:
  52.4 15.5 %collective-permute-start.1 = (f32[384,128]{1,0:T(8,128)S(1)}, f32[384,128]{1,0:T(8,128)S(1)}, u32[]{:S(2)}, u32[]{:S(2)}) collective-permute-start(f32[384,128]{1,0:T(8,128)S(1)} %get-tuple-element.20), channel_id=1, source_target_pairs={{128,0},{256,128},{384,256},{385,384},{257,385},{129,257},{1,129},... | collective-permute-start | bytes 589832 | tf_op jit(solution)/shard_map/ppermute | solution.py:424
  53.7 22.0 %collective-permute-start.2 = (f32[384,128]{1,0:T(8,128)S(1)}, f32[384,128]{1,0:T(8,128)S(1)}, u32[]{:S(2)}, u32[]{:S(2)}) collective-permute-start(f32[384,128]{1,0:T(8,128)S(1)} %get-tuple-element.21), channel_id=1, source_target_pairs={{0,128},{128,256},{256,384},{384,385},{385,257},{257,129},{129,1},... | collective-permute-start | bytes 589832 | tf_op jit(solution)/shard_map/ppermute | solution.py:424
  62.2 28.2 %collective-permute-start = (f32[768,128]{1,0:T(8,128)S(1)}, f32[768,128]{1,0:T(8,128)S(1)}, u32[]{:S(2)}, u32[]{:S(2)}) collective-permute-start(f32[768,128]{1,0:T(8,128)S(1)} %get-tuple-element.19.tile), channel_id=1, source_target_pairs={{32,0},{160,128},{288,256},{416,384},{417,385},{289,257},{161,129}... | collective-permute-start | bytes 1179656 | tf_op jit(solution)/shard_map/ppermute | solution.py:424
  67.9 22.5 %collective-permute-start.3 = (f32[384,128]{1,0:T(8,128)S(1)}, f32[384,128]{1,0:T(8,128)S(1)}, u32[]{:S(2)}, u32[]{:S(2)}) collective-permute-start(f32[384,128]{1,0:T(8,128)S(1)} %collective-permute-done.1.after), channel_id=1, source_target_pairs={{32,0},{160,128},{288,256},{416,384},{417,385},{289,257},{161,129}... | collective-permute-start | bytes 589832 | tf_op jit(solution)/shard_map/ppermute | solution.py:424
  75.7 14.7 %collective-permute-start.4 = (f32[384,128]{1,0:T(8,128)S(1)}, f32[384,128]{1,0:T(8,128)S(1)}, u32[]{:S(2)}, u32[]{:S(2)}) collective-permute-start(f32[384,128]{1,0:T(8,128)S(1)} %collective-permute-done.2.before), channel_id=1, source_target_pairs={{32,0},{160,128},{288,256},{416,384},{417,385},{289,257},{161,129}... | collective-permute-start | bytes 589832 | tf_op jit(solution)/shard_map/ppermute | solution.py:424
  87.3 3.1 %collective-permute-start.5 = (f32[64,128]{1,0:T(8,128)S(1)}, f32[64,128]{1,0:T(8,128)S(1)}, u32[]{:S(2)}, u32[]{:S(2)}) collective-permute-start(f32[64,128]{1,0:T(8,128)S(1)} %get-tuple-element.23), channel_id=1, source_target_pairs={{0,4},{4,0},{1,5},{5,1},{2,6},{6,2},{3,7},{7,3},{8,12},{12,8},{9,1... | collective-permute-start | bytes 98312 | tf_op jit(solution)/shard_map/ppermute | solution.py:446
  94.6 13.1 %collective-permute-start.6 = (f32[960,128]{1,0:T(8,128)S(1)}, f32[960,128]{1,0:T(8,128)S(1)}, u32[]{:S(2)}, u32[]{:S(2)}) collective-permute-start(f32[960,128]{1,0:T(8,128)S(1)} %get-tuple-element.25), channel_id=1, source_target_pairs={{0,32},{128,160},{256,288},{384,416},{385,417},{257,289},{129,161}... | collective-permute-start | bytes 1474568 | tf_op jit(solution)/shard_map/ppermute | solution.py:424
  96.5 11.2 %all-to-all-start.1 = ((f32[8,64,128]{2,1,0:T(8,128)}), f32[8,64,128]{2,1,0:T(8,128)S(1)}, u32[]{:S(2)}, u32[]{:S(2)}) async-start(f32[8,64,128]{2,1,0:T(8,128)} %get-tuple-element.26), calls=%async_computation.1 | async-start | bytes 524288 | tf_op jit(solution)/shard_map/all_to_all | solution.py:447
  110.3 14.9 %collective-permute-start.8 = (f32[256,128]{1,0:T(8,128)S(1)}, f32[256,128]{1,0:T(8,128)S(1)}, u32[]{:S(2)}, u32[]{:S(2)}) collective-permute-start(f32[256,128]{1,0:T(8,128)S(1)} %get-tuple-element.29), channel_id=1, source_target_pairs={{128,0},{256,128},{384,256},{385,384},{257,385},{129,257},{1,129},... | collective-permute-start | bytes 393224 | tf_op jit(solution)/shard_map/ppermute | solution.py:424
  111.6 19.8 %collective-permute-start.9 = (f32[256,128]{1,0:T(8,128)S(1)}, f32[256,128]{1,0:T(8,128)S(1)}, u32[]{:S(2)}, u32[]{:S(2)}) collective-permute-start(f32[256,128]{1,0:T(8,128)S(1)} %get-tuple-element.30), channel_id=1, source_target_pairs={{0,128},{128,256},{256,384},{384,385},{385,257},{257,129},{129,1},... | collective-permute-start | bytes 393224 | tf_op jit(solution)/shard_map/ppermute | solution.py:424
  120.1 18.2 %collective-permute-start.7 = (f32[512,128]{1,0:T(8,128)S(1)}, f32[512,128]{1,0:T(8,128)S(1)}, u32[]{:S(2)}, u32[]{:S(2)}) collective-permute-start(f32[512,128]{1,0:T(8,128)S(1)} %get-tuple-element.28.tile), channel_id=1, source_target_pairs={{32,0},{160,128},{288,256},{416,384},{417,385},{289,257},{161,129}... | collective-permute-start | bytes 786440 | tf_op jit(solution)/shard_map/ppermute | solution.py:424
  125.2 10.6 %collective-permute-start.10 = (f32[256,128]{1,0:T(8,128)S(1)}, f32[256,128]{1,0:T(8,128)S(1)}, u32[]{:S(2)}, u32[]{:S(2)}) collective-permute-start(f32[256,128]{1,0:T(8,128)S(1)} %collective-permute-done.8.after), channel_id=1, source_target_pairs={{32,0},{160,128},{288,256},{416,384},{417,385},{289,257},{161,129}... | collective-permute-start | bytes 393224 | tf_op jit(solution)/shard_map/ppermute | solution.py:424
  131.4 6.9 %collective-permute-start.11 = (f32[256,128]{1,0:T(8,128)S(1)}, f32[256,128]{1,0:T(8,128)S(1)}, u32[]{:S(2)}, u32[]{:S(2)}) collective-permute-start(f32[256,128]{1,0:T(8,128)S(1)} %collective-permute-done.9.before), channel_id=1, source_target_pairs={{32,0},{160,128},{288,256},{416,384},{417,385},{289,257},{161,129}... | collective-permute-start | bytes 393224 | tf_op jit(solution)/shard_map/ppermute | solution.py:424
  141.3 11.3 %collective-permute-start.12 = (f32[768,128]{1,0:T(8,128)S(1)}, f32[768,128]{1,0:T(8,128)S(1)}, u32[]{:S(2)}, u32[]{:S(2)}) collective-permute-start(f32[768,128]{1,0:T(8,128)S(1)} %get-tuple-element.32), channel_id=1, source_target_pairs={{0,32},{128,160},{256,288},{384,416},{385,417},{257,289},{129,161}... | collective-permute-start | bytes 1179656 | tf_op jit(solution)/shard_map/ppermute | solution.py:424
  155.1 23.7 %copy-start = (s32[5]{0:T(128)S(1)}, s32[5]{0:T(128)}, u32[]{:S(2)}) copy-start(s32[5]{0:T(128)} %stack.49.flags) | copy-start | bytes 64
